TPU v7x, 256 devices: a whole 4x4x8 slice. The times are simulated.
256 devices in a mesh: grp: 8 (over x_lo, y), slab: 32 (over x_hi, z, core).
Axes of the slice: x: 4 (x_hi: 2, x_lo: 2; x = x_hi * 2 + x_lo), y: 4, z: 8, core: 2. Of those that a mesh axis runs over, the one named last changes fastest.
Arguments:
- template: float32 [256, 64, 256], P('slab'), may hold values from -6 to 6
- images: bfloat16 [32, 256, 64, 256], P('grp', 'slab'), may hold values from -6 to 6
- velocity: float32 [32, 3, 256, 64, 256], P('grp', None, 'slab'), may hold values from -3 to 3
- labels: int32 [256, 64, 256], P('slab'), may hold values from 0 to 3
- stiffness: float32 [4], replicated, may hold values from 0.5 to 2
- cohort: int32 [32], P('grp'), may hold values from 0 to 7
- site_gain: float32 [8], replicated, may hold values from 0.5 to 2
Outputs:
- new_template: float32 [256, 64, 256], P('slab')
- new_velocity: float32 [32, 3, 256, 64, 256], P('grp', None, 'slab')
All inputs are finite; a program needn't handle non-finite values.
Results may differ from a plain program's by a relative error of at most 0.0003.
Values sent between devices are 32-bit elements; how exact they have to be, the bound alone decides.
No kernel may reach another device: no remote copies, remote signals or barrier semaphores. Data moves between devices by JAX's collectives and lax.ppermute only.
A program may use at most 64 MiB of HBM per device.

v0:
```python
import jax
import jax.numpy as jnp
from jax import lax
from jax.sharding import PartitionSpec as P

velocity_step = 0.05
template_step = 0.5


def extended(block, sides, width):
    for axis, dim in sides:
        count = lax.axis_size(axis)
        forward = [(i, i + 1) for i in range(count - 1)]
        backward = [(target, source) for source, target in forward]
        low = lax.ppermute(
            lax.slice_in_dim(block, block.shape[dim] - width, None, axis=dim), axis, forward
        )
        high = lax.ppermute(lax.slice_in_dim(block, 0, width, axis=dim), axis, backward)
        block = jnp.concatenate([low, block, high], axis=dim)
    return block


def slopes_of(padded):
    along_z = 0.5 * (padded[..., 2:, 1:-1, 1:-1] - padded[..., :-2, 1:-1, 1:-1])
    along_y = 0.5 * (padded[..., 1:-1, 2:, 1:-1] - padded[..., 1:-1, :-2, 1:-1])
    along_x = 0.5 * (padded[..., 1:-1, 1:-1, 2:] - padded[..., 1:-1, 1:-1, :-2])
    return jnp.stack([along_z, along_y, along_x], axis=-4)


def around_of(padded):
    beside_all = padded[..., 2:, 1:-1, 1:-1] + padded[..., :-2, 1:-1, 1:-1]
    beside_all = beside_all + padded[..., 1:-1, 2:, 1:-1] + padded[..., 1:-1, :-2, 1:-1]
    return beside_all + padded[..., 1:-1, 1:-1, 2:] + padded[..., 1:-1, 1:-1, :-2]


def pad_plane(field):
    return jnp.pad(field, [(0, 0)] * (field.ndim - 2) + [(1, 1), (1, 1)])


def local(template, images, velocity, labels, stiffness, cohort, site_gain):
    template_wide = extended(template, (("slab", 0),), 1)
    velocity_wide = extended(velocity, (("slab", 2),), 1)
    slopes = slopes_of(pad_plane(template_wide))
    levels = jnp.arange(stiffness.shape[0], dtype=jnp.int32)
    stiff_map = jnp.sum(
        jnp.where(labels[None] == levels[:, None, None, None], stiffness[:, None, None, None], 0.0),
        axis=0,
    )
    groups = jnp.arange(site_gain.shape[0], dtype=jnp.int32)
    subject_gain = jnp.sum(
        jnp.where(cohort[:, None] == groups[None, :], site_gain[None, :], 0.0), axis=1
    )
    warped = template[None] + jnp.sum(slopes[None] * velocity, axis=1)
    residual = warped - subject_gain[:, None, None, None] * images.astype(jnp.float32)
    elastic = stiff_map * (6.0 * velocity - around_of(pad_plane(velocity_wide)))
    new_velocity = velocity - velocity_step * (residual[:, None] * slopes[None] + elastic)
    group_partial = jnp.sum(residual, axis=0)
    subjects = images.shape[0] * lax.axis_size("grp")
    share = lax.psum_scatter(group_partial, "grp", scatter_dimension=1, tiled=True)
    share_rows = share.shape[1]
    own_rows = lax.dynamic_slice_in_dim(template, lax.axis_index("grp") * share_rows, share_rows, 1)
    new_template = lax.all_gather(
        own_rows - template_step * share / subjects, "grp", axis=1, tiled=True
    )
    return (new_template, new_velocity)


def solution(mesh):
    placed = (
        P("slab", None, None),
        P("grp", "slab", None, None),
        P("grp", None, "slab", None, None),
        P("slab", None, None),
        P(),
        P("grp"),
        P(),
    )
    return jax.shard_map(
        local,
        mesh=mesh,
        in_specs=placed,
        out_specs=(P("slab", None, None), P("grp", None, "slab", None, None)),
        check_vma=False,
    )
```

profile of v0, /device:TPU:6, one launch (start us, length us, event | category | flops | bytes accessed | tf_op | source)
XLA Modules:
  0.0 113.3 jit_solution(6247605921446230556)
XLA Ops:
  7.2 0.0 copy-start.2
  7.2 0.0 reduce-scatter.2.cloned.1.call-start
  7.2 0.9 fusion.21
  8.2 1.9 %collective-permute-start.1 = (f32[1,64,256]{2,1,0:T(8,128)S(1)}, f32[1,64,256]{2,1,0:T(8,128)S(1)}, u32[]{:S(2)}, u32[]{:S(2)}) collective-permute-start(f32[1,64,256]{2,1,0:T(8,128)S(1)} %get-tuple-element.8), channel_id=1, source_target_pairs={{0,1},{1,2},{2,3},{3,4},{4,5},{5,6},{6,7},{7,8},{8,9},{9,10},{10,1... | collective-permute-start | bytes 196616 | tf_op jit(solution)/shard_map/ppermute | solution.py:15
  10.1 8.0 %collective-permute-start = (f32[1,64,256]{2,1,0:T(8,128)S(1)}, f32[1,64,256]{2,1,0:T(8,128)S(1)}, u32[]{:S(2)}, u32[]{:S(2)}) collective-permute-start(f32[1,64,256]{2,1,0:T(8,128)S(1)} %get-tuple-element.9), channel_id=1, source_target_pairs={{1,0},{2,1},{3,2},{4,3},{5,4},{6,5},{7,6},{8,7},{9,8},{10,9},{11,1... | collective-permute-start | bytes 196616 | tf_op jit(solution)/shard_map/ppermute | solution.py:18
  18.1 2.7 %fusion.20 = (f32[4,3,1,64,256]{4,3,2,1,0:T(8,128)}, f32[4,3,1,64,256]{4,3,2,1,0:T(8,128)}) fusion(f32[4,3,8,64,256]{4,3,2,1,0:T(8,128)} %param.9), kind=kLoop, calls=%fused_computation.50 | loop fusion | bytes 3145728 | tf_op jit(solution)/shard_map/slice | solution.py:16
  20.8 1.9 %collective-permute-start.3 = (f32[4,3,1,64,256]{4,3,2,1,0:T(8,128)}, f32[4,3,1,64,256]{4,3,2,1,0:T(8,128)S(1)}, u32[]{:S(2)}, u32[]{:S(2)}) collective-permute-start(f32[4,3,1,64,256]{4,3,2,1,0:T(8,128)} %get-tuple-element.4), channel_id=1, source_target_pairs={{0,1},{1,2},{2,3},{3,4},{4,5},{5,6},{6,7},{7,8},{8,9},{9,10},{10,1... | collective-permute-start | bytes 2359304 | tf_op jit(solution)/shard_map/ppermute | solution.py:15
  22.7 7.3 %collective-permute-start.2 = (f32[4,3,1,64,256]{4,3,2,1,0:T(8,128)}, f32[4,3,1,64,256]{4,3,2,1,0:T(8,128)}, u32[]{:S(2)}, u32[]{:S(2)}) collective-permute-start(f32[4,3,1,64,256]{4,3,2,1,0:T(8,128)} %get-tuple-element.5), channel_id=1, source_target_pairs={{1,0},{2,1},{3,2},{4,3},{5,4},{6,5},{7,6},{8,7},{9,8},{10,9},{11,1... | collective-permute-start | bytes 2359304 | tf_op jit(solution)/shard_map/ppermute | solution.py:18
  30.0 0.0 copy-start
  30.0 1.5 %select_reduce_fusion = f32[8,64,256]{2,1,0:T(8,128)S(1)} fusion(f32[4]{0:T(128)} %param.11, s32[8,64,256]{2,1,0:T(8,128)} %param.10), kind=kLoop, calls=%fused_computation.22 | loop fusion | flops 1441792 | bytes 1048592 | tf_op jit(solution)/shard_map/reduce_sum | solution.py:45
  31.6 1.2 %select_reduce_fusion.1 = f32[4]{0:T(128)S(1)} fusion(f32[8]{0:T(128)} %param.13, s32[4]{0:T(128)} %param.12), kind=kLoop, calls=%fused_computation.47 | loop fusion | flops 92 | bytes 64 | tf_op jit(solution)/shard_map/reduce_sum | solution.py:50
  32.8 0.0 collective-permute-done.1
  32.8 0.0 collective-permute-done
  32.8 1.4 %select_maximum_fusion.2 = f32[10,66,258]{2,1,0:T(8,128)S(1)} fusion(f32[1,64,256]{2,1,0:T(8,128)S(1)} %collective-permute-done, f32[8,64,256]{2,1,0:T(8,128)} %param.7, f32[1,64,256]{2,1,0:T(8,128)S(1)} %collective-permute-done.1), kind=kLoop, calls=%fused_computation.30 | loop fusion | flops 2554200 | bytes 1336480 | tf_op jit(solution)/shard_map/concatenate | solution.py:19
  34.2 0.5 fusion.15
  34.7 0.0 copy-done.2
  34.8 0.0 copy-start.3
  34.8 0.1 pad_maximum_fusion.2
  34.9 0.0 copy-done
  34.9 1.1 multiply_reduce_fusion
  36.0 0.0 copy-done.3
  36.0 2.6 %fusion.19 = (f32[8,64,256]{2,1,0:T(8,128)}, f32[4,8,64,256]{3,2,1,0:T(8,128)}) fusion(bf16[4,8,64,256]{3,2,1,0:T(8,128)(2,1)S(1)} %copy-done.3, f32[4]{0:T(128)S(1)} %select_reduce_fusion.1, f32[4,8,64,256]{3,2,1,0:T(8,128)S(1)} %multiply_reduce_fusion, f32[8,64,256]{2,1,0:T(8,128)S(1)} %copy-done.2), kind=kLoop, calls=%fused_computation.49 | loop fusion | flops 2490368 | bytes 6291472 | tf_op jit(solution)/shard_map/reduce_sum | solution.py:57
  38.6 0.0 reduce-scatter.2.cloned.1.call-update
  38.7 0.0 copy-start.1
  38.7 0.0 collective-permute-done.3
  38.7 1.1 collective-permute-done.2
  39.8 7.6 %select_maximum_fusion = f32[4,3,10,66,258]{4,3,2,1,0:T(8,128)S(1)} fusion(f32[4,3,1,64,256]{4,3,2,1,0:T(8,128)} %collective-permute-done.2, f32[4,3,8,64,256]{4,3,2,1,0:T(8,128)} %param.9, f32[4,3,1,64,256]{4,3,2,1,0:T(8,128)S(1)} %collective-permute-done.3), kind=kLoop, calls=%fused_computation.4 | loop fusion | flops 30650400 | bytes 16037760 | tf_op jit(solution)/shard_map/concatenate | solution.py:19
  47.4 0.0 copy-done.1
  47.4 12.5 %fusion.7 = f32[4,3,8,64,256]{4,3,2,1,0:T(8,128)} fusion(f32[4,3,8,64,256]{4,3,2,1,0:T(8,128)} %param.9, f32[4,3,10,66,258]{4,3,2,1,0:T(8,128)S(1)} %select_maximum_fusion, f32[4,3,1,64,256]{4,3,2,1,0:T(8,128)S(1)} %collective-permute-done.3, f32[4,3,1,64,256]{4,3,2,1,0:T(8,128)} %collective-permute-done.2, f32[8,64,256]{2,1,0:T(8,128)S(1)} %select_reduce_fusion, ...), kind=kLoop, calls=%fused_computation.14 | loop fusion | flops 22020096 | bytes 43515904 | tf_op jit(solution)/shard_map/sub | solution.py:56
  59.9 15.8 %reduce-scatter.2.cloned.1.call-done = f32[8,8,256]{2,1,0:T(8,128)} async-done(((f32[8,64,256]{2,1,0:T(8,128)}), f32[8,8,256]{2,1,0:T(8,128)}) %reduce-scatter.2.cloned.1.call-update) | async-done | bytes 65552 | tf_op jit(solution)/shard_map/reduce_scatter | solution.py:59
  75.7 0.8 multiply_subtract_fusion.1
  76.6 29.1 %all_gather.3 = f32[8,64,256]{2,1,0:T(8,128)S(1)} all-gather(f32[8,8,256]{2,1,0:T(8,128)S(1)} %multiply_subtract_fusion.1), channel_id=1, replica_groups=mesh['grp'=8,'slab'=32] {'grp'}, dimensions={1}, use_global_device_ids=true | all-gather | bytes 589824 | tf_op jit(solution)/shard_map/all_gather | solution.py:62
  105.7 0.8 copy.10
  (1 shorter events, 0.0 us)
Async XLA Ops:
  7.2 27.6 %copy-start.2 = (f32[8,64,256]{2,1,0:T(8,128)S(1)}, f32[8,64,256]{2,1,0:T(8,128)}, u32[]{:S(2)}) copy-start(f32[8,64,256]{2,1,0:T(8,128)} %param.7) | copy-start | bytes 1572868
  7.2 68.5 %reduce-scatter.2.cloned.1.call-start = ((), (), s32[]{:S(2)}) async-start(), calls=%async_computation.1 | async-start | bytes 589824 | tf_op jit(solution)/shard_map/reduce_scatter | solution.py:59
  8.2 24.6 %collective-permute-start.1 = (f32[1,64,256]{2,1,0:T(8,128)S(1)}, f32[1,64,256]{2,1,0:T(8,128)S(1)}, u32[]{:S(2)}, u32[]{:S(2)}) collective-permute-start(f32[1,64,256]{2,1,0:T(8,128)S(1)} %get-tuple-element.8), channel_id=1, source_target_pairs={{0,1},{1,2},{2,3},{3,4},{4,5},{5,6},{6,7},{7,8},{8,9},{9,10},{10,1... | collective-permute-start | bytes 196616 | tf_op jit(solution)/shard_map/ppermute | solution.py:15
  10.1 22.7 %collective-permute-start = (f32[1,64,256]{2,1,0:T(8,128)S(1)}, f32[1,64,256]{2,1,0:T(8,128)S(1)}, u32[]{:S(2)}, u32[]{:S(2)}) collective-permute-start(f32[1,64,256]{2,1,0:T(8,128)S(1)} %get-tuple-element.9), channel_id=1, source_target_pairs={{1,0},{2,1},{3,2},{4,3},{5,4},{6,5},{7,6},{8,7},{9,8},{10,9},{11,1... | collective-permute-start | bytes 196616 | tf_op jit(solution)/shard_map/ppermute | solution.py:18
  20.8 17.9 %collective-permute-start.3 = (f32[4,3,1,64,256]{4,3,2,1,0:T(8,128)}, f32[4,3,1,64,256]{4,3,2,1,0:T(8,128)S(1)}, u32[]{:S(2)}, u32[]{:S(2)}) collective-permute-start(f32[4,3,1,64,256]{4,3,2,1,0:T(8,128)} %get-tuple-element.4), channel_id=1, source_target_pairs={{0,1},{1,2},{2,3},{3,4},{4,5},{5,6},{6,7},{7,8},{8,9},{9,10},{10,1... | collective-permute-start | bytes 2359304 | tf_op jit(solution)/shard_map/ppermute | solution.py:15
  22.7 17.1 %collective-permute-start.2 = (f32[4,3,1,64,256]{4,3,2,1,0:T(8,128)}, f32[4,3,1,64,256]{4,3,2,1,0:T(8,128)}, u32[]{:S(2)}, u32[]{:S(2)}) collective-permute-start(f32[4,3,1,64,256]{4,3,2,1,0:T(8,128)} %get-tuple-element.5), channel_id=1, source_target_pairs={{1,0},{2,1},{3,2},{4,3},{5,4},{6,5},{7,6},{8,7},{9,8},{10,9},{11,1... | collective-permute-start | bytes 2359304 | tf_op jit(solution)/shard_map/ppermute | solution.py:18
  30.0 4.9 %copy-start = (f32[4,3,8,64,256]{4,3,2,1,0:T(8,128)S(1)}, f32[4,3,8,64,256]{4,3,2,1,0:T(8,128)}, u32[]{:S(2)}) copy-start(f32[4,3,8,64,256]{4,3,2,1,0:T(8,128)} %param.9) | copy-start | bytes 18874372
  34.8 1.2 %copy-start.3 = (bf16[4,8,64,256]{3,2,1,0:T(8,128)(2,1)S(1)}, bf16[4,8,64,256]{3,2,1,0:T(8,128)(2,1)}, u32[]{:S(2)}) copy-start(bf16[4,8,64,256]{3,2,1,0:T(8,128)(2,1)} %param.8) | copy-start | bytes 3145732
  38.7 8.7 %copy-start.1 = (f32[4,8,64,256]{3,2,1,0:T(8,128)S(1)}, f32[4,8,64,256]{3,2,1,0:T(8,128)}, u32[]{:S(2)}) copy-start(f32[4,8,64,256]{3,2,1,0:T(8,128)} %get-tuple-element.3) | copy-start | bytes 6291460
Sparse Core Ops, SparseCore 0:
  38.8 36.8 reduce-scatter.1
where the time goes:
time: 114 us; the launch traced here: 113 us
  other arithmetic  29.5 us (26%)
  blocking collectives  29.1 us (26%)
  starting transfers between devices  19.2 us (17%)
  waiting for transfers between devices  17 us (15%)
  between operations  14.2 us (12%)
  local copies, waits for them, and re-layouts  4.45 us (4%)
    all_gather x1, blocking collectives, local(): lax.all_gather(own_rows - template_step * share / subjects, 'grp', axis=1...  29.1 us
    reduce_scatter x1, waiting for transfers between devices, local(): lax.psum_scatter(group_partial, 'grp', scatter_dimension=1, tiled=True)  15.8 us
    ppermute x2, starting transfers between devices, extended(): lax.ppermute(lax.slice_in_dim(block, 0, width, axis=dim), axis, backward)  15.3 us
    sub x1, other arithmetic, local(): velocity - velocity_step * (residual[:, None] * slopes[None] + elastic)  12.5 us
    concatenate x2, other arithmetic, extended(): block = jnp.concatenate([low, block, high], axis=dim)  8.97 us
    ppermute x2, starting transfers between devices, extended(): lax.ppermute(lax.slice_in_dim(block, block.shape[dim] - width, None, axis...  3.83 us
    slice x2, local copies, waits for them, and re-layouts, extended(): lax.slice_in_dim(block, block.shape[dim] - width, None, axis=dim)  3.62 us
    reduce_sum x1, other arithmetic, local(): group_partial = jnp.sum(residual, axis=0)  2.64 us
  transfers between devices with their start and end apart: 5, of which 2 were waited for; matrix products, arithmetic and copies ran while one was open for 28% of the time, Pallas kernels for 0%

commit v1 on v0

v1 whole, which is shorter than its diff:
```python
import functools

import jax
import jax.numpy as jnp
from jax import lax
from jax.experimental import pallas as pl
from jax.experimental.pallas import tpu as pltpu
from jax.sharding import PartitionSpec as P

velocity_step = 0.05
template_step = 0.5
ROWS = 16
MIB = 1 << 20


def beside_y(get_row, here, first, last, count, start):
    rows, width = here.shape
    at = lax.broadcasted_iota(jnp.int32, (rows, width), 0)
    zero = jnp.zeros((rows, width), jnp.float32)
    before = zero if first else jnp.broadcast_to(get_row(start - 1), (rows, width))
    after = zero if last else jnp.broadcast_to(get_row(start + rows), (rows, width))
    lower = jnp.where(at == 0, before, pltpu.roll(here, 1, 0))
    upper = jnp.where(at == rows - 1, after, pltpu.roll(here, rows - 1, 0))
    return lower, upper


def beside_x(here):
    rows, width = here.shape
    at = lax.broadcasted_iota(jnp.int32, (rows, width), 1)
    zero = jnp.zeros((rows, width), jnp.float32)
    lower = jnp.where(at == 0, zero, pltpu.roll(here, 1, 1))
    upper = jnp.where(at == width - 1, zero, pltpu.roll(here, width - 1, 1))
    return lower, upper


def plane_slopes(t_ref, z, j, below, above):
    count = t_ref.shape[1]
    start = j * ROWS
    rows = pl.ds(start, ROWS)
    here = t_ref[z, rows, :]
    y_low, y_high = beside_y(
        lambda at: t_ref[z, pl.ds(at, 1), :], here, j == 0, start + ROWS == count, count, start
    )
    x_low, x_high = beside_x(here)
    return 0.5 * (above - below), 0.5 * (y_high - y_low), 0.5 * (x_high - x_low)


def partial_kernel(cohort, gain, t_ref, im_ref, v_ref, sum_ref, edge_ref, first_ref, last_ref, s_ref):
    subject = pl.program_id(0)
    depth, count, width = t_ref.shape
    chunks = count // ROWS
    level = gain[cohort[subject]]

    @pl.when(subject == 0)
    def _():
        for j in range(chunks):
            rows = pl.ds(j * ROWS, ROWS)
            zero = jnp.zeros((ROWS, width), jnp.float32)

            def slope(z, below, above):
                for c, value in enumerate(plane_slopes(t_ref, z, j, below, above)):
                    s_ref[c, z, rows, :] = value

            slope(0, zero, t_ref[1, rows, :])
            slope(depth - 1, t_ref[depth - 2, rows, :], zero)

            @pl.loop(1, depth - 1)
            def _(z):
                slope(z, t_ref[z - 1, rows, :], t_ref[z + 1, rows, :])

    def accumulate(fresh):
        @pl.loop(0, depth)
        def _(z):
            for j in range(chunks):
                rows = pl.ds(j * ROWS, ROWS)
                value = t_ref[z, rows, :] - level * im_ref[0, z, rows, :].astype(jnp.float32)
                for c in range(3):
                    value = value + s_ref[c, z, rows, :] * v_ref[0, c, z, rows, :]
                if not fresh:
                    value = value + sum_ref[z, rows, :]
                sum_ref[z, rows, :] = value

        for side, z in enumerate((0, depth - 1)):
            if fresh:
                edge_ref[side] = v_ref[0, 0, z]
            else:
                edge_ref[side] = edge_ref[side] + v_ref[0, 0, z]

    pl.when(subject == 0)(lambda: accumulate(True))
    pl.when(subject > 0)(lambda: accumulate(False))
    for c in range(3):
        first_ref[0, c, 0] = v_ref[0, c, 0]
        last_ref[0, c, 0] = v_ref[0, c, depth - 1]


def move_kernel(
    cohort, gain, stiff, t_ref, tl_ref, th_ref, lab_ref, im_ref, v_ref, vl_ref, vh_ref, out_ref, s_ref, k_ref
):
    subject = pl.program_id(0)
    depth, count, width = t_ref.shape
    chunks = count // ROWS
    level = gain[cohort[subject]]

    @pl.when(subject == 0)
    def _():
        for j in range(chunks):
            rows = pl.ds(j * ROWS, ROWS)

            def slope(z, below, above):
                for c, value in enumerate(plane_slopes(t_ref, z, j, below, above)):
                    s_ref[c, z, rows, :] = value
                label = lab_ref[z, rows, :]
                rate = jnp.full((ROWS, width), stiff[0], jnp.float32)
                for kind in range(1, 4):
                    rate = jnp.where(label == kind, stiff[kind], rate)
                k_ref[z, rows, :] = velocity_step * rate

            slope(0, tl_ref[0, rows, :], t_ref[1, rows, :])
            slope(depth - 1, t_ref[depth - 2, rows, :], th_ref[0, rows, :])

            @pl.loop(1, depth - 1)
            def _(z):
                slope(z, t_ref[z - 1, rows, :], t_ref[z + 1, rows, :])

    def plane(z, below, above):
        for j in range(chunks):
            start = j * ROWS
            rows = pl.ds(start, ROWS)
            field = [v_ref[0, c, z, rows, :] for c in range(3)]
            slopes = [s_ref[c, z, rows, :] for c in range(3)]
            rate = k_ref[z, rows, :]
            value = t_ref[z, rows, :] - level * im_ref[0, z, rows, :].astype(jnp.float32)
            for c in range(3):
                value = value + slopes[c] * field[c]
            value = velocity_step * value
            for c in range(3):
                here = field[c]
                y_low, y_high = beside_y(
                    lambda at: v_ref[0, c, z, pl.ds(at, 1), :], here, j == 0, start + ROWS == count, count, start
                )
                x_low, x_high = beside_x(here)
                around = (below(c, rows) + above(c, rows)) + (y_low + y_high) + (x_low + x_high)
                out_ref[0, c, z, rows, :] = here + rate * (around - 6.0 * here) - value * slopes[c]

    plane(0, lambda c, rows: vl_ref[0, c, 0, rows, :], lambda c, rows: v_ref[0, c, 1, rows, :])
    plane(
        depth - 1,
        lambda c, rows: v_ref[0, c, depth - 2, rows, :],
        lambda c, rows: vh_ref[0, c, 0, rows, :],
    )

    @pl.loop(1, depth - 1)
    def _(z):
        plane(z, lambda c, rows: v_ref[0, c, z - 1, rows, :], lambda c, rows: v_ref[0, c, z + 1, rows, :])


def whole(shape):
    return pl.BlockSpec(shape, lambda *_: (0,) * len(shape))


def per_subject(shape):
    return pl.BlockSpec((1,) + shape[1:], lambda s, *_: (s,) + (0,) * (len(shape) - 1))


def partial_sums(cohort, gain, template, images, velocity):
    subjects = images.shape[0]
    depth, count, width = template.shape
    edge = (subjects, 3, 1, count, width)
    shapes = (template.shape, (2, count, width), edge, edge)
    return pl.pallas_call(
        partial_kernel,
        out_shape=[jax.ShapeDtypeStruct(shape, jnp.float32) for shape in shapes],
        grid_spec=pltpu.PrefetchScalarGridSpec(
            num_scalar_prefetch=2,
            grid=(subjects,),
            in_specs=[whole(template.shape), per_subject(images.shape), per_subject(velocity.shape)],
            out_specs=[whole(shapes[0]), whole(shapes[1]), per_subject(edge), per_subject(edge)],
            scratch_shapes=[pltpu.VMEM((3,) + template.shape, jnp.float32)],
        ),
        compiler_params=pltpu.CompilerParams(vmem_limit_bytes=60 * MIB),
        cost_estimate=pl.CostEstimate(flops=12 * velocity.size, bytes_accessed=10 * MIB, transcendentals=0),
        name="partial_sums",
    )(cohort, gain, template, images, velocity)


def moved(cohort, gain, stiffness, template, t_low, t_high, labels, images, velocity, v_low, v_high):
    subjects = images.shape[0]
    return pl.pallas_call(
        move_kernel,
        out_shape=jax.ShapeDtypeStruct(velocity.shape, jnp.float32),
        grid_spec=pltpu.PrefetchScalarGridSpec(
            num_scalar_prefetch=3,
            grid=(subjects,),
            in_specs=[
                whole(template.shape),
                whole(t_low.shape),
                whole(t_high.shape),
                whole(labels.shape),
                per_subject(images.shape),
                per_subject(velocity.shape),
                per_subject(v_low.shape),
                per_subject(v_high.shape),
            ],
            out_specs=per_subject(velocity.shape),
            scratch_shapes=[
                pltpu.VMEM((3,) + template.shape, jnp.float32),
                pltpu.VMEM(template.shape, jnp.float32),
            ],
        ),
        compiler_params=pltpu.CompilerParams(vmem_limit_bytes=60 * MIB),
        cost_estimate=pl.CostEstimate(flops=25 * velocity.size, bytes_accessed=16 * MIB, transcendentals=0),
        name="moved",
    )(cohort, gain, stiffness, template, t_low, t_high, labels, images, velocity, v_low, v_high)


def local(template, images, velocity, labels, stiffness, cohort, site_gain):
    depth = template.shape[0]
    count = lax.axis_size("slab")
    groups = lax.axis_size("grp")
    forward = [(i, i + 1) for i in range(count - 1)]
    backward = [(i + 1, i) for i in range(count - 1)]
    t_low = lax.ppermute(template[depth - 1 :], "slab", forward)
    t_high = lax.ppermute(template[:1], "slab", backward)
    part, edge, first, last = partial_sums(cohort, site_gain, template, images, velocity)
    v_low = lax.ppermute(last, "slab", forward)
    v_high = lax.ppermute(first, "slab", backward)
    part = jnp.concatenate(
        [
            part[:1] - 0.5 * t_low * edge[:1],
            part[1 : depth - 1],
            part[depth - 1 :] + 0.5 * t_high * edge[1:],
        ],
        axis=0,
    )
    shares = lax.all_to_all(part, "grp", 0, 0, tiled=True)
    own_planes = depth // groups
    summed = jnp.sum(shares.reshape((groups, own_planes) + template.shape[1:]), axis=0)
    own = lax.dynamic_slice_in_dim(template, lax.axis_index("grp") * own_planes, own_planes, 0)
    own = own - template_step * summed / (images.shape[0] * groups)
    new_template = lax.all_to_all(
        jnp.broadcast_to(own[None], (groups,) + own.shape).reshape(template.shape), "grp", 0, 0, tiled=True
    )
    new_velocity = moved(
        cohort, site_gain, stiffness, template, t_low, t_high, labels, images, velocity, v_low, v_high
    )
    return (new_template, new_velocity)


def solution(mesh):
    placed = (
        P("slab", None, None),
        P("grp", "slab", None, None),
        P("grp", None, "slab", None, None),
        P("slab", None, None),
        P(),
        P("grp"),
        P(),
    )
    return jax.shard_map(
        local,
        mesh=mesh,
        in_specs=placed,
        out_specs=(P("slab", None, None), P("grp", None, "slab", None, None)),
        check_vma=False,
    )
```

time: 114 us -> 63.3 us (0.56)
  blocking collectives: 29.1 us -> 0 us
  other arithmetic: 29.5 us -> 2.72 us
  Pallas kernels: 0 us -> 21.5 us
  waiting for transfers between devices: 17 us -> 2.39 us
  between operations: 14.2 us -> 0.74 us
  starting transfers between devices: 19.2 us -> 30.8 us
    all_gather x1 -> x0, blocking collectives: 29.1 us -> none  [local(): lax.all_gather(own_rows - template_step * share / subjects, 'grp', axis=1...]
    pallas_call x0 -> x2, Pallas kernels: none -> 21.5 us  [the longest x1 13.1 us: moved(): pl.pallas_call(move_kernel, out_shape=jax.ShapeDtypeStruct(velocity.shape...]
    reduce_scatter x1 -> x0, waiting for transfers between devices: 15.8 us -> none  [local(): lax.psum_scatter(group_partial, 'grp', scatter_dimension=1, tiled=True)]
    sub x2 -> x1, other arithmetic: 13.4 us -> 1 us  [local(): part[:1] - 0.5 * t_low * edge[:1]]
    all_to_all x0 -> x2, starting transfers between devices: none -> 11.6 us  [the longest x1 5.93 us: local(): shares = lax.all_to_all(part, 'grp', 0, 0, tiled=True)]
    concatenate x2 -> x1, other arithmetic: 8.97 us -> 0.83 us  [local(): jnp.concatenate([part[:1] - 0.5 * t_low * edge[:1], part[1:depth - 1], pa...]
    reduce_sum x4 -> x1, other arithmetic: 6.48 us -> 0.04 us  [local(): jnp.sum(shares.reshape((groups, own_planes) + template.shape[1:]), axis=0)]
    slice x2, local copies, waits for them, and re-layouts: 3.62 us -> 1.91 us  [the longest x1 1.02 us: local(): part[1:depth - 1]]
  transfers between devices with their start and end apart: 5 -> 6, of which waited for: 2 -> 2; matrix products, arithmetic and copies ran while one was open for 28% -> 4% of each run, Pallas kernels for 0% -> 34%
where the time goes in v1:
time: 63.3 us; the launch traced here: 62.6 us
  starting transfers between devices  30.8 us (49%)
  Pallas kernels  21.5 us (34%)
  local copies, waits for them, and re-layouts  4.45 us (7%)
  other arithmetic  2.72 us (4%)
  waiting for transfers between devices  2.39 us (4%)
  between operations  0.74 us (1%)
    pallas_call x1, Pallas kernels, moved(): pl.pallas_call(move_kernel, out_shape=jax.ShapeDtypeStruct(velocity.shape...  13.1 us
    pallas_call x1, Pallas kernels, partial_sums(): pl.pallas_call(partial_kernel, out_shape=[jax.ShapeDtypeStruct(shape, jnp...  8.42 us
    ppermute x1, starting transfers between devices, local(): t_high = lax.ppermute(template[:1], 'slab', backward)  8.05 us
    ppermute x1, starting transfers between devices, local(): v_high = lax.ppermute(first, 'slab', backward)  7.26 us
    all_to_all x1, starting transfers between devices, local(): shares = lax.all_to_all(part, 'grp', 0, 0, tiled=True)  5.93 us
    all_to_all x1, starting transfers between devices, local(): lax.all_to_all(jnp.broadcast_to(own[None], (groups,) + own.shape).reshape...  5.7 us
    ppermute x1, starting transfers between devices, local(): t_low = lax.ppermute(template[depth - 1:], 'slab', forward)  1.92 us
    ppermute x1, starting transfers between devices, local(): v_low = lax.ppermute(last, 'slab', forward)  1.91 us
  transfers between devices with their start and end apart: 6, of which 2 were waited for; matrix products, arithmetic and copies ran while one was open for 4% of the time, Pallas kernels for 34%

profile of v1, /device:TPU:6, one launch (start us, length us, event | category | flops | bytes accessed | tf_op | source)
XLA Modules:
  0.0 62.6 jit_solution(9159596069914355283)
XLA Ops:
  0.6 0.9 %fusion.1 = (f32[1,64,256]{2,1,0:T(8,128)S(1)}, f32[1,64,256]{2,1,0:T(8,128)S(1)}) fusion(f32[8,64,256]{2,1,0:T(8,128)} %t_ref.3), kind=kLoop, calls=%fused_computation.5 | loop fusion | bytes 262144 | tf_op jit(solution)/shard_map/slice | solution.py:222
  1.5 1.9 %collective-permute-start = (f32[1,64,256]{2,1,0:T(8,128)S(1)}, f32[1,64,256]{2,1,0:T(8,128)S(1)}, u32[]{:S(2)}, u32[]{:S(2)}) collective-permute-start(f32[1,64,256]{2,1,0:T(8,128)S(1)} %get-tuple-element.12), channel_id=1, source_target_pairs={{0,1},{1,2},{2,3},{3,4},{4,5},{5,6},{6,7},{7,8},{8,9},{9,10},{10,1... | collective-permute-start | bytes 196616 | tf_op jit(solution)/shard_map/ppermute | solution.py:222
  3.4 8.0 %collective-permute-start.1 = (f32[1,64,256]{2,1,0:T(8,128)S(1)}, f32[1,64,256]{2,1,0:T(8,128)S(1)}, u32[]{:S(2)}, u32[]{:S(2)}) collective-permute-start(f32[1,64,256]{2,1,0:T(8,128)S(1)} %get-tuple-element.13), channel_id=1, source_target_pairs={{1,0},{2,1},{3,2},{4,3},{5,4},{6,5},{7,6},{8,7},{9,8},{10,9},{11,1... | collective-permute-start | bytes 196616 | tf_op jit(solution)/shard_map/ppermute | solution.py:223
  11.5 8.4 %partial_sums.1 = (f32[8,64,256]{2,1,0:T(8,128)}, f32[2,64,256]{2,1,0:T(8,128)}, f32[4,3,1,64,256]{4,3,2,1,0:T(8,128)}, f32[4,3,1,64,256]{4,3,2,1,0:T(8,128)}) custom-call(s32[4]{0:T(128)} %cohort.3, f32[8]{0:T(128)} %gain.3, f32[8,64,256]{2,1,0:T(8,128)} %t_ref.3, bf16[4,8,64,256]{3,2,1,0:T(8,128)(2,1)} %im_ref.3, f32[4,3,8,64,256]{4,3,2,1,0:T(8,128)} %v_ref.3), custom_call_target="tpu_custom_call" | custom-call | flops 18874368 | bytes 10485760 | tf_op jit(solution)/shard_map/partial_sums/pallas_call | solution.py:170
  19.9 1.0 %slice.24 = f32[6,64,256]{2,1,0:T(8,128)S(1)} slice(f32[8,64,256]{2,1,0:T(8,128)} %get-tuple-element.6), slice={[1:7], [0:64], [0:256]} | slice | bytes 786432 | tf_op jit(solution)/shard_map/slice | solution.py:230
  20.9 0.0 collective-permute-done.tl_ref
  21.0 0.0 copy-start.2
  21.0 0.0 collective-permute-done.1.th_ref
  21.0 0.0 copy-start.3
  21.0 1.0 %multiply_subtract_fusion = (f32[1,64,256]{2,1,0:T(8,128)S(1)}, f32[1,64,256]{2,1,0:T(8,128)S(1)}) fusion(f32[2,64,256]{2,1,0:T(8,128)} %get-tuple-element.7, f32[1,64,256]{2,1,0:T(8,128)S(1)} %collective-permute-done.tl_ref, f32[8,64,256]{2,1,0:T(8,128)} %get-tuple-element.6, f32[1,64,256]{2,1,0:T(8,128)S(1)} %collective-permute-done.1.th_ref), kind=kLoop, calls=%fused_computation.4 | loop fusion | flops 98304 | bytes 524288 | tf_op jit(solution)/shard_map/sub | solution.py:229
  22.0 0.8 %pad_maximum_fusion = f32[8,64,256]{2,1,0:T(8,128)} fusion(f32[1,64,256]{2,1,0:T(8,128)S(1)} %get-tuple-element.11, f32[6,64,256]{2,1,0:T(8,128)S(1)} %slice.24, f32[1,64,256]{2,1,0:T(8,128)S(1)} %get-tuple-element.10), kind=kLoop, calls=%fused_computation | loop fusion | flops 262144 | bytes 1048576 | tf_op jit(solution)/shard_map/concatenate | solution.py:227
  22.8 5.9 %all-to-all-start = ((f32[8,64,256]{2,1,0:T(8,128)}), f32[8,64,256]{2,1,0:T(8,128)S(1)}, u32[]{:S(2)}, u32[]{:S(2)}) async-start(f32[8,64,256]{2,1,0:T(8,128)} %pad_maximum_fusion), calls=%async_computation | async-start | bytes 1048576 | tf_op jit(solution)/shard_map/all_to_all | solution.py:235
  28.7 1.9 %collective-permute-start.2 = (f32[4,3,1,64,256]{4,3,2,1,0:T(8,128)}, f32[4,3,1,64,256]{4,3,2,1,0:T(8,128)S(1)}, u32[]{:S(2)}, u32[]{:S(2)}) collective-permute-start(f32[4,3,1,64,256]{4,3,2,1,0:T(8,128)} %get-tuple-element.8), channel_id=1, source_target_pairs={{0,1},{1,2},{2,3},{3,4},{4,5},{5,6},{6,7},{7,8},{8,9},{9,10},{10,1... | collective-permute-start | bytes 2359304 | tf_op jit(solution)/shard_map/ppermute | solution.py:225
  30.7 7.3 %collective-permute-start.3 = (f32[4,3,1,64,256]{4,3,2,1,0:T(8,128)}, f32[4,3,1,64,256]{4,3,2,1,0:T(8,128)S(1)}, u32[]{:S(2)}, u32[]{:S(2)}) collective-permute-start(f32[4,3,1,64,256]{4,3,2,1,0:T(8,128)} %get-tuple-element.9), channel_id=1, source_target_pairs={{1,0},{2,1},{3,2},{4,3},{5,4},{6,5},{7,6},{8,7},{9,8},{10,9},{11,1... | collective-permute-start | bytes 2359304 | tf_op jit(solution)/shard_map/ppermute | solution.py:226
  37.9 0.0 all-to-all-done
  38.0 0.9 %fusion = f32[64,256]{1,0:T(8,128)S(1)} fusion(f32[64,256]{1,0:T(8,128)S(1)} %reduce_sum.9, f32[8,64,256]{2,1,0:T(8,128)} %t_ref.3, s32[]{:T(128)S(6)} %select_n.3), kind=kLoop, calls=%fused_computation.2 | loop fusion | flops 32768 | bytes 196612 | tf_op jit(solution)/shard_map/broadcast_in_dim | solution.py:241
  38.8 0.8 %reshape.23 = f32[8,64,256]{2,1,0:T(8,128)} broadcast(f32[64,256]{1,0:T(8,128)S(1)} %fusion), dimensions={1,2} | broadcast | bytes 589824 | tf_op jit(solution)/shard_map/reshape | solution.py:241
  39.7 5.7 %all-to-all-start.1 = ((f32[8,64,256]{2,1,0:T(8,128)}), f32[8,64,256]{2,1,0:T(8,128)S(1)}, u32[]{:S(2)}, u32[]{:S(2)}) async-start(f32[8,64,256]{2,1,0:T(8,128)} %reshape.23), calls=%async_computation.1 | async-start | bytes 1048576 | tf_op jit(solution)/shard_map/all_to_all | solution.py:240
  45.4 0.6 collective-permute-done.2.vl_ref
  46.0 0.0 copy-start
  46.0 1.8 %collective-permute-done.3.vh_ref = f32[4,3,1,64,256]{4,3,2,1,0:T(8,128)S(1)} collective-permute-done((f32[4,3,1,64,256]{4,3,2,1,0:T(8,128)}, f32[4,3,1,64,256]{4,3,2,1,0:T(8,128)S(1)}, u32[]{:S(2)}, u32[]{:S(2)}) %collective-permute-start.3) | collective-permute-done | bytes 786464 | tf_op jit(solution)/shard_map/ppermute | solution.py:226
  47.8 0.0 copy-done.2
  47.8 0.0 copy-done.3
  47.8 0.0 copy-done
  47.8 0.0 copy-start.1
  47.8 0.9 %copy-done.1 = f32[4,3,1,64,256]{4,3,2,1,0:T(8,128)} copy-done((f32[4,3,1,64,256]{4,3,2,1,0:T(8,128)}, f32[4,3,1,64,256]{4,3,2,1,0:T(8,128)S(1)}, u32[]{:S(2)}) %copy-start.1) | copy-done | bytes 786456
  48.7 13.1 %moved.1 = f32[4,3,8,64,256]{4,3,2,1,0:T(8,128)} custom-call(s32[4]{0:T(128)} %cohort.3, f32[8]{0:T(128)} %gain.3, f32[4]{0:T(128)} %stiff.1, f32[8,64,256]{2,1,0:T(8,128)} %t_ref.3, f32[1,64,256]{2,1,0:T(8,128)} %copy-done.2, f32[1,64,256]{2,1,0:T(8,128)} %copy-done.3, s32[8,64,256]{2,1,0:T(8,128)} %lab_ref.1, bf16[4,8,64,256]{3,2,1,0:T(8,128)(2,1)} %im_ref.3, ...), custom_call_target="tpu_custom_call" | custom-call | flops 39321600 | bytes 16777216 | tf_op jit(solution)/shard_map/moved/pallas_call | solution.py:188
  61.8 0.0 all-to-all-done.1
  61.8 0.8 %copy.10 = f32[8,64,256]{2,1,0:T(8,128)} copy(f32[8,64,256]{2,1,0:T(8,128)S(1)} %all-to-all-done.1) | data formatting | bytes 1048576
  (1 shorter events, 0.0 us)
Async XLA Ops:
  1.5 19.4 %collective-permute-start = (f32[1,64,256]{2,1,0:T(8,128)S(1)}, f32[1,64,256]{2,1,0:T(8,128)S(1)}, u32[]{:S(2)}, u32[]{:S(2)}) collective-permute-start(f32[1,64,256]{2,1,0:T(8,128)S(1)} %get-tuple-element.12), channel_id=1, source_target_pairs={{0,1},{1,2},{2,3},{3,4},{4,5},{5,6},{6,7},{7,8},{8,9},{9,10},{10,1... | collective-permute-start | bytes 196616 | tf_op jit(solution)/shard_map/ppermute | solution.py:222
  3.4 17.5 %collective-permute-start.1 = (f32[1,64,256]{2,1,0:T(8,128)S(1)}, f32[1,64,256]{2,1,0:T(8,128)S(1)}, u32[]{:S(2)}, u32[]{:S(2)}) collective-permute-start(f32[1,64,256]{2,1,0:T(8,128)S(1)} %get-tuple-element.13), channel_id=1, source_target_pairs={{1,0},{2,1},{3,2},{4,3},{5,4},{6,5},{7,6},{8,7},{9,8},{10,9},{11,1... | collective-permute-start | bytes 196616 | tf_op jit(solution)/shard_map/ppermute | solution.py:223
  21.0 26.8 %copy-start.2 = (f32[1,64,256]{2,1,0:T(8,128)}, f32[1,64,256]{2,1,0:T(8,128)S(1)}, u32[]{:S(2)}) copy-start(f32[1,64,256]{2,1,0:T(8,128)S(1)} %collective-permute-done.tl_ref) | copy-start | bytes 196612
  21.0 26.8 %copy-start.3 = (f32[1,64,256]{2,1,0:T(8,128)}, f32[1,64,256]{2,1,0:T(8,128)S(1)}, u32[]{:S(2)}) copy-start(f32[1,64,256]{2,1,0:T(8,128)S(1)} %collective-permute-done.1.th_ref) | copy-start | bytes 196612
  22.8 15.1 %all-to-all-start = ((f32[8,64,256]{2,1,0:T(8,128)}), f32[8,64,256]{2,1,0:T(8,128)S(1)}, u32[]{:S(2)}, u32[]{:S(2)}) async-start(f32[8,64,256]{2,1,0:T(8,128)} %pad_maximum_fusion), calls=%async_computation | async-start | bytes 1048576 | tf_op jit(solution)/shard_map/all_to_all | solution.py:235
  28.7 17.2 %collective-permute-start.2 = (f32[4,3,1,64,256]{4,3,2,1,0:T(8,128)}, f32[4,3,1,64,256]{4,3,2,1,0:T(8,128)S(1)}, u32[]{:S(2)}, u32[]{:S(2)}) collective-permute-start(f32[4,3,1,64,256]{4,3,2,1,0:T(8,128)} %get-tuple-element.8), channel_id=1, source_target_pairs={{0,1},{1,2},{2,3},{3,4},{4,5},{5,6},{6,7},{7,8},{8,9},{9,10},{10,1... | collective-permute-start | bytes 2359304 | tf_op jit(solution)/shard_map/ppermute | solution.py:225
  30.7 17.1 %collective-permute-start.3 = (f32[4,3,1,64,256]{4,3,2,1,0:T(8,128)}, f32[4,3,1,64,256]{4,3,2,1,0:T(8,128)S(1)}, u32[]{:S(2)}, u32[]{:S(2)}) collective-permute-start(f32[4,3,1,64,256]{4,3,2,1,0:T(8,128)} %get-tuple-element.9), channel_id=1, source_target_pairs={{1,0},{2,1},{3,2},{4,3},{5,4},{6,5},{7,6},{8,7},{9,8},{10,9},{11,1... | collective-permute-start | bytes 2359304 | tf_op jit(solution)/shard_map/ppermute | solution.py:226
  39.7 22.1 %all-to-all-start.1 = ((f32[8,64,256]{2,1,0:T(8,128)}), f32[8,64,256]{2,1,0:T(8,128)S(1)}, u32[]{:S(2)}, u32[]{:S(2)}) async-start(f32[8,64,256]{2,1,0:T(8,128)} %reshape.23), calls=%async_computation.1 | async-start | bytes 1048576 | tf_op jit(solution)/shard_map/all_to_all | solution.py:240
  46.0 1.8 %copy-start = (f32[4,3,1,64,256]{4,3,2,1,0:T(8,128)}, f32[4,3,1,64,256]{4,3,2,1,0:T(8,128)S(1)}, u32[]{:S(2)}) copy-start(f32[4,3,1,64,256]{4,3,2,1,0:T(8,128)S(1)} %collective-permute-done.2.vl_ref) | copy-start | bytes 2359300
  47.8 0.9 %copy-start.1 = (f32[4,3,1,64,256]{4,3,2,1,0:T(8,128)}, f32[4,3,1,64,256]{4,3,2,1,0:T(8,128)S(1)}, u32[]{:S(2)}) copy-start(f32[4,3,1,64,256]{4,3,2,1,0:T(8,128)S(1)} %collective-permute-done.3.vh_ref) | copy-start | bytes 2359300

commit v2 on v0

v2 whole, which is shorter than its diff:
```python
import jax
import jax.numpy as jnp
from jax import lax
from jax.experimental import pallas as pl
from jax.experimental.pallas import tpu as pltpu
from jax.sharding import PartitionSpec as P

velocity_step = 0.05
template_step = 0.5
ROWS = 16
MIB = 1 << 20


def beside_y(get_row, here, first, last, count, start):
    rows, width = here.shape
    at = lax.broadcasted_iota(jnp.int32, (rows, width), 0)
    zero = jnp.zeros((rows, width), jnp.float32)
    before = zero if first else jnp.broadcast_to(get_row(start - 1), (rows, width))
    after = zero if last else jnp.broadcast_to(get_row(start + rows), (rows, width))
    lower = jnp.where(at == 0, before, pltpu.roll(here, 1, 0))
    upper = jnp.where(at == rows - 1, after, pltpu.roll(here, rows - 1, 0))
    return lower, upper


def beside_x(here):
    rows, width = here.shape
    at = lax.broadcasted_iota(jnp.int32, (rows, width), 1)
    zero = jnp.zeros((rows, width), jnp.float32)
    lower = jnp.where(at == 0, zero, pltpu.roll(here, 1, 1))
    upper = jnp.where(at == width - 1, zero, pltpu.roll(here, width - 1, 1))
    return lower, upper


def fill_slopes(t_ref, s_ref, also=None):
    depth, count, width = s_ref.shape[1:]

    @pl.loop(0, depth)
    def _(z):
        for j in range(count // ROWS):
            start = j * ROWS
            rows = pl.ds(start, ROWS)
            here = t_ref[z + 1, rows, :]
            y_low, y_high = beside_y(
                lambda at: t_ref[z + 1, pl.ds(at, 1), :], here, j == 0, start + ROWS == count, count, start
            )
            x_low, x_high = beside_x(here)
            s_ref[0, z, rows, :] = 0.5 * (t_ref[z + 2, rows, :] - t_ref[z, rows, :])
            s_ref[1, z, rows, :] = 0.5 * (y_high - y_low)
            s_ref[2, z, rows, :] = 0.5 * (x_high - x_low)
            if also is not None:
                also(z, rows)


def template_copies(odd, t_hbm, ti_hbm, to_hbm, t_ref, sem):
    depth = t_hbm.shape[0]
    inner = jnp.where(odd == 1, 0, depth + 1)
    outer = depth + 1 - inner
    return [
        pltpu.make_async_copy(t_hbm, t_ref.at[pl.ds(1, depth)], sem.at[0]),
        pltpu.make_async_copy(ti_hbm, t_ref.at[pl.ds(inner, 1)], sem.at[1]),
        pltpu.make_async_copy(to_hbm, t_ref.at[pl.ds(outer, 1)], sem.at[2]),
    ]


def partial_kernel(
    odd_ref, cohort, gain, t_hbm, ti_hbm, to_hbm, im_hbm, v_hbm, sum_ref, inner_hbm, outer_hbm,
    t_ref, im_ref, v_ref, s_ref, t_sem, im_sem, v_sem, in_sem, out_sem,
):
    subjects, depth, count, width = im_ref.shape
    odd = odd_ref[0]
    template = template_copies(odd, t_hbm, ti_hbm, to_hbm, t_ref, t_sem)
    images = [pltpu.make_async_copy(im_hbm.at[s], im_ref.at[s], im_sem.at[s]) for s in range(subjects)]
    fields = [
        [pltpu.make_async_copy(v_hbm.at[s, c], v_ref.at[s, c], v_sem.at[s, c]) for c in range(3)]
        for s in range(subjects)
    ]
    facing = jnp.where(odd == 1, 0, depth - 1)
    inner = [
        pltpu.make_async_copy(v_ref.at[s, :, pl.ds(facing, 1)], inner_hbm.at[s], in_sem.at[s])
        for s in range(subjects)
    ]
    outer = [
        pltpu.make_async_copy(v_ref.at[s, :, pl.ds(depth - 1 - facing, 1)], outer_hbm.at[s], out_sem.at[s])
        for s in range(subjects)
    ]
    for copy in template:
        copy.start()
    for s in range(subjects):
        images[s].start()
        for copy in fields[s]:
            copy.start()
    for copy in template:
        copy.wait()
    fill_slopes(t_ref, s_ref)
    pair = 2 if subjects % 2 == 0 else 1
    for low in range(0, subjects, pair):
        members = range(low, low + pair)
        for s in members:
            images[s].wait()
            for copy in fields[s]:
                copy.wait()
            inner[s].start()
            outer[s].start()
        levels = [gain[cohort[s]] for s in members]

        @pl.loop(0, depth)
        def _(z):
            for j in range(count // ROWS):
                rows = pl.ds(j * ROWS, ROWS)
                value = float(pair) * t_ref[z + 1, rows, :]
                for s, level in zip(members, levels):
                    value = value - level * im_ref[s, z, rows, :].astype(jnp.float32)
                for c in range(3):
                    field = v_ref[low, c, z, rows, :]
                    for s in members[1:]:
                        field = field + v_ref[s, c, z, rows, :]
                    value = value + s_ref[c, z, rows, :] * field
                if low:
                    value = value + sum_ref[z, rows, :]
                sum_ref[z, rows, :] = value

    for copy in inner + outer:
        copy.wait()


def share_kernel(place, scale, t_hbm, parts_ref, out_ref, own_ref, sem):
    groups, count, width = parts_ref.shape
    copy = pltpu.make_async_copy(t_hbm.at[place[0]], own_ref, sem)
    copy.start()
    copy.wait()
    for j in range(count // ROWS):
        rows = pl.ds(j * ROWS, ROWS)
        total = parts_ref[0, rows, :]
        for g in range(1, groups):
            total = total + parts_ref[g, rows, :]
        value = own_ref[rows, :] - scale * total
        for g in range(groups):
            out_ref[g, rows, :] = value


def move_kernel(
    odd_ref, cohort, gain, stiff, t_hbm, ti_hbm, to_hbm, lab_hbm, im_hbm, v_hbm, vi_hbm, vo_hbm, out_hbm,
    t_ref, lab_ref, im_ref, v_ref, new_ref, s_ref, k_ref,
    t_sem, lab_sem, im_sem, v_sem, vi_sem, vo_sem, out_sem,
):
    subjects, depth, count, width = im_ref.shape
    odd = odd_ref[0]
    template = template_copies(odd, t_hbm, ti_hbm, to_hbm, t_ref, t_sem)
    template.append(pltpu.make_async_copy(lab_hbm, lab_ref, lab_sem))
    inner = jnp.where(odd == 1, 0, depth + 1)
    half = depth // 2

    def arrivals(s):
        copies = [pltpu.make_async_copy(im_hbm.at[s], im_ref.at[s], im_sem.at[s])]
        for c in range(3):
            copies.append(
                pltpu.make_async_copy(v_hbm.at[s, c], v_ref.at[s, c, pl.ds(1, depth)], v_sem.at[s, c])
            )
        copies.append(pltpu.make_async_copy(vi_hbm.at[s], v_ref.at[s, :, pl.ds(inner, 1)], vi_sem.at[s]))
        copies.append(
            pltpu.make_async_copy(vo_hbm.at[s], v_ref.at[s, :, pl.ds(depth + 1 - inner, 1)], vo_sem.at[s])
        )
        return copies

    def departure(s, part):
        planes = pl.ds(part * half, half)
        return pltpu.make_async_copy(new_ref.at[s, :, planes], out_hbm.at[s, :, planes], out_sem.at[s, part])

    for copy in template:
        copy.start()
    for s in range(subjects):
        for copy in arrivals(s):
            copy.start()
    for copy in template:
        copy.wait()

    def rate_of(z, rows):
        label = lab_ref[z, rows, :]
        rate = jnp.full(label.shape, stiff[0], jnp.float32)
        for kind in range(1, stiff.shape[0]):
            rate = jnp.where(label == kind, stiff[kind], rate)
        k_ref[z, rows, :] = velocity_step * rate

    fill_slopes(t_ref, s_ref, rate_of)

    @pl.loop(0, subjects)
    def _(s):
        for copy in arrivals(s):
            copy.wait()
        level = gain[cohort[s]]

        def plane(z):
            for j in range(count // ROWS):
                start = j * ROWS
                rows = pl.ds(start, ROWS)
                field = [v_ref[s, c, z + 1, rows, :] for c in range(3)]
                slopes = [s_ref[c, z, rows, :] for c in range(3)]
                rate = k_ref[z, rows, :]
                value = t_ref[z + 1, rows, :] - level * im_ref[s, z, rows, :].astype(jnp.float32)
                for c in range(3):
                    value = value + slopes[c] * field[c]
                value = velocity_step * value
                for c in range(3):
                    here = field[c]
                    y_low, y_high = beside_y(
                        lambda at: v_ref[s, c, z + 1, pl.ds(at, 1), :], here,
                        j == 0, start + ROWS == count, count, start,
                    )
                    x_low, x_high = beside_x(here)
                    around = (v_ref[s, c, z, rows, :] + v_ref[s, c, z + 2, rows, :]) + (y_low + y_high)
                    around = around + (x_low + x_high)
                    new_ref[s, c, z, rows, :] = here + rate * (around - 6.0 * here) - value * slopes[c]

        for part in range(2):
            pl.loop(part * half, (part + 1) * half)(plane)
            departure(s, part).start()

    @pl.loop(0, subjects)
    def _(s):
        for part in range(2):
            departure(s, part).wait()


SMALL = pl.BlockSpec(memory_space=pltpu.SMEM)
FAR = pl.BlockSpec(memory_space=pltpu.HBM)
FREE = pl.BlockSpec(memory_space=pl.ANY)
NEAR = pl.BlockSpec(memory_space=pltpu.VMEM)
COPY = pltpu.SemaphoreType.DMA


def partial_sums(odd, cohort, gain, template, t_inner, t_outer, images, velocity):
    subjects = images.shape[0]
    depth, count, width = template.shape
    edge = jax.ShapeDtypeStruct((subjects, 3, 1, count, width), jnp.float32)
    return pl.pallas_call(
        partial_kernel,
        out_shape=[jax.ShapeDtypeStruct(template.shape, jnp.float32), edge, edge],
        in_specs=[SMALL] * 3 + [FAR, FREE, FREE, FAR, FAR],
        out_specs=[NEAR, FAR, FAR],
        scratch_shapes=[
            pltpu.VMEM((depth + 2, count, width), jnp.float32),
            pltpu.VMEM(images.shape, images.dtype),
            pltpu.VMEM(velocity.shape, jnp.float32),
            pltpu.VMEM((3,) + template.shape, jnp.float32),
            COPY((3,)), COPY((subjects,)), COPY((subjects, 3)), COPY((subjects,)), COPY((subjects,)),
        ],
        compiler_params=pltpu.CompilerParams(vmem_limit_bytes=60 * MIB),
        cost_estimate=pl.CostEstimate(flops=4 * velocity.size, bytes_accessed=10 * MIB, transcendentals=0),
        name="partial_sums",
    )(odd, cohort, gain, template, t_inner, t_outer, images, velocity)


def share_update(place, scale, template, parts):
    return pl.pallas_call(
        lambda *refs: share_kernel(refs[0], scale, *refs[1:]),
        out_shape=jax.ShapeDtypeStruct(parts.shape, jnp.float32),
        in_specs=[SMALL, FAR, NEAR],
        out_specs=NEAR,
        scratch_shapes=[pltpu.VMEM(template.shape[1:], jnp.float32), COPY(())],
        compiler_params=pltpu.CompilerParams(vmem_limit_bytes=8 * MIB),
        cost_estimate=pl.CostEstimate(flops=parts.size, bytes_accessed=2 * MIB, transcendentals=0),
        name="share_update",
    )(place, template, parts)


def moved(odd, cohort, gain, stiffness, template, t_inner, t_outer, labels, images, velocity, v_inner, v_outer):
    subjects = images.shape[0]
    depth, count, width = template.shape
    return pl.pallas_call(
        move_kernel,
        out_shape=jax.ShapeDtypeStruct(velocity.shape, jnp.float32),
        in_specs=[SMALL] * 4 + [FAR, FREE, FREE, FAR, FAR, FAR, FREE, FREE],
        out_specs=FAR,
        scratch_shapes=[
            pltpu.VMEM((depth + 2, count, width), jnp.float32),
            pltpu.VMEM(labels.shape, labels.dtype),
            pltpu.VMEM(images.shape, images.dtype),
            pltpu.VMEM((subjects, 3, depth + 2, count, width), jnp.float32),
            pltpu.VMEM(velocity.shape, jnp.float32),
            pltpu.VMEM((3,) + template.shape, jnp.float32),
            pltpu.VMEM(template.shape, jnp.float32),
            COPY((3,)), COPY(()), COPY((subjects,)), COPY((subjects, 3)),
            COPY((subjects,)), COPY((subjects,)), COPY((subjects, 2)),
        ],
        compiler_params=pltpu.CompilerParams(vmem_limit_bytes=60 * MIB),
        cost_estimate=pl.CostEstimate(flops=8 * velocity.size, bytes_accessed=16 * MIB, transcendentals=0),
        name="moved",
    )(odd, cohort, gain, stiffness, template, t_inner, t_outer, labels, images, velocity, v_inner, v_outer)


def local(template, images, velocity, labels, stiffness, cohort, site_gain):
    depth = template.shape[0]
    slabs = lax.axis_size("slab")
    groups = lax.axis_size("grp")
    assert depth == groups and slabs % 2 == 0
    odd = lax.axis_index("slab") % 2
    place = lax.axis_index("grp").reshape(1)
    inside = [(i, i ^ 1) for i in range(slabs)]
    across = [(i, i + 1) for i in range(1, slabs - 1, 2)]
    across = across + [(target, source) for source, target in across]
    facing = jnp.where(odd == 1, 0, depth - 1)
    t_inner = lax.ppermute(lax.dynamic_slice_in_dim(template, facing, 1, 0), "slab", inside)
    t_outer = lax.ppermute(lax.dynamic_slice_in_dim(template, depth - 1 - facing, 1, 0), "slab", across)
    odd = odd.reshape(1)
    part, inner, outer = partial_sums(odd, cohort, site_gain, template, t_inner, t_outer, images, velocity)
    v_inner = lax.ppermute(inner, "slab", inside)
    v_outer = lax.ppermute(outer, "slab", across)
    parts = lax.all_to_all(part, "grp", 0, 0, tiled=True)
    shares = share_update(place, template_step / (images.shape[0] * groups), template, parts)
    new_template = lax.all_to_all(shares, "grp", 0, 0, tiled=True)
    new_velocity = moved(
        odd, cohort, site_gain, stiffness, template, t_inner, t_outer, labels, images, velocity, v_inner, v_outer
    )
    return (new_template, new_velocity)


def solution(mesh):
    placed = (
        P("slab", None, None),
        P("grp", "slab", None, None),
        P("grp", None, "slab", None, None),
        P("slab", None, None),
        P(),
        P("grp"),
        P(),
    )
    return jax.shard_map(
        local,
        mesh=mesh,
        in_specs=placed,
        out_specs=(P("slab", None, None), P("grp", None, "slab", None, None)),
        check_vma=False,
    )
```

time: 114 us -> 56.8 us (0.50)
  other arithmetic: 29.5 us -> 0 us
  blocking collectives: 29.1 us -> 0 us
  Pallas kernels: 0 us -> 20.2 us
  between operations: 14.2 us -> 0.73 us
  waiting for transfers between devices: 17 us -> 6.95 us
  starting transfers between devices: 19.2 us -> 25.2 us
    all_gather x1 -> x0, blocking collectives: 29.1 us -> none  [local(): lax.all_gather(own_rows - template_step * share / subjects, 'grp', axis=1...]
    pallas_call x0 -> x3, Pallas kernels: none -> 20.2 us  [the longest x1 12.5 us: moved(): pl.pallas_call(move_kernel, out_shape=jax.ShapeDtypeStruct(velocity.shape...]
    reduce_scatter x1 -> x0, waiting for transfers between devices: 15.8 us -> none  [local(): lax.psum_scatter(group_partial, 'grp', scatter_dimension=1, tiled=True)]
    sub x2 -> x0, other arithmetic: 13.4 us -> none  [the longest x1 12.5 us: local(): velocity - velocity_step * (residual[:, None] * slopes[None] + elastic)]
    all_to_all x0 -> x2, starting transfers between devices: none -> 10.4 us  [the longest x1 5.94 us: local(): parts = lax.all_to_all(part, 'grp', 0, 0, tiled=True)]
    concatenate x2 -> x0, other arithmetic: 8.97 us -> none  [extended(): block = jnp.concatenate([low, block, high], axis=dim)]
    reduce_sum x4 -> x0, other arithmetic: 6.48 us -> none  [the longest x1 2.64 us: local(): group_partial = jnp.sum(residual, axis=0)]
    ppermute x4, starting transfers between devices: 19.1 us -> 14.8 us  [the longest x1 8.05 us: local(): lax.ppermute(lax.dynamic_slice_in_dim(template, depth - 1 - facing, 1, 0)...]
  transfers between devices with their start and end apart: 5 -> 6, of which waited for: 2 -> 3; matrix products, arithmetic and copies ran while one was open for 28% -> 0% of each run, Pallas kernels for 0% -> 24%
where the time goes in v2:
time: 56.8 us; the launch traced here: 56.5 us
  starting transfers between devices  25.2 us (44%)
  Pallas kernels  20.2 us (36%)
  waiting for transfers between devices  6.95 us (12%)
  local copies, waits for them, and re-layouts  3.32 us (6%)
  between operations  0.73 us (1%)
    pallas_call x1, Pallas kernels, moved(): pl.pallas_call(move_kernel, out_shape=jax.ShapeDtypeStruct(velocity.shape...  12.5 us
    ppermute x1, starting transfers between devices, local(): lax.ppermute(lax.dynamic_slice_in_dim(template, depth - 1 - facing, 1, 0)...  8.05 us
    pallas_call x1, Pallas kernels, partial_sums(): pl.pallas_call(partial_kernel, out_shape=[jax.ShapeDtypeStruct(template.s...  6.77 us
    ppermute x1, starting transfers between devices, local(): v_outer = lax.ppermute(outer, 'slab', across)  6.68 us
    all_to_all x1, starting transfers between devices, local(): parts = lax.all_to_all(part, 'grp', 0, 0, tiled=True)  5.94 us
    all_to_all x1, starting transfers between devices, local(): new_template = lax.all_to_all(shares, 'grp', 0, 0, tiled=True)  4.48 us
    ppermute x1, waiting for transfers between devices, local(): v_outer = lax.ppermute(outer, 'slab', across)  3.47 us
    unnamed x11, local copies, waits for them, and re-layouts  2.38 us
  transfers between devices with their start and end apart: 6, of which 3 were waited for; matrix products, arithmetic and copies ran while one was open for 0% of the time, Pallas kernels for 24%

profile of v2, /device:TPU:6, one launch (start us, length us, event | category | flops | bytes accessed | tf_op | source)
XLA Modules:
  0.0 56.5 jit_solution(1043380419377997975)
XLA Ops:
  0.6 0.0 copy-start
  0.7 0.9 %constant_dynamic-slice_fusion = (f32[1,64,256]{2,1,0:T(8,128)S(1)}, f32[1,64,256]{2,1,0:T(8,128)S(1)}) fusion(f32[8,64,256]{2,1,0:T(8,128)} %t_hbm.3, s32[]{:T(128)S(6)} %select_n.17, s32[]{:T(128)S(6)} %select_n.16), kind=kLoop, calls=%fused_computation | loop fusion | bytes 262152 | tf_op jit(solution)/shard_map/dynamic_slice | solution.py:303
  1.6 8.0 %collective-permute-start.1 = (f32[1,64,256]{2,1,0:T(8,128)S(1)}, f32[1,64,256]{2,1,0:T(8,128)S(1)}, u32[]{:S(2)}, u32[]{:S(2)}) collective-permute-start(f32[1,64,256]{2,1,0:T(8,128)S(1)} %get-tuple-element.8), channel_id=1, source_target_pairs={{1,2},{3,4},{5,6},{7,8},{9,10},{11,12},{13,14},{15,16},{17,18},{19... | collective-permute-start | bytes 196616 | tf_op jit(solution)/shard_map/ppermute | solution.py:303
  9.7 0.1 collective-permute-start
  9.8 1.8 %collective-permute-done.1.to_hbm = f32[1,64,256]{2,1,0:T(8,128)S(1)} collective-permute-done((f32[1,64,256]{2,1,0:T(8,128)S(1)}, f32[1,64,256]{2,1,0:T(8,128)S(1)}, u32[]{:S(2)}, u32[]{:S(2)}) %collective-permute-start.1) | collective-permute-done | bytes 65568 | tf_op jit(solution)/shard_map/ppermute | solution.py:303
  11.6 0.0 copy-start.3
  11.6 0.0 collective-permute-done.ti_hbm
  11.6 0.0 copy-start.4
  11.6 0.6 %copy-done.3 = f32[1,64,256]{2,1,0:T(8,128)} copy-done((f32[1,64,256]{2,1,0:T(8,128)}, f32[1,64,256]{2,1,0:T(8,128)S(1)}, u32[]{:S(2)}) %copy-start.3) | copy-done | bytes 65560
  12.2 0.0 copy-done.4
  12.2 6.8 %partial_sums.1 = (f32[8,64,256]{2,1,0:T(8,128)}, f32[4,3,1,64,256]{4,3,2,1,0:T(8,128)}, f32[4,3,1,64,256]{4,3,2,1,0:T(8,128)}) custom-call(s32[1]{0:T(128)} %bitcast.1.odd_ref, s32[4]{0:T(128)} %cohort.3, f32[8]{0:T(128)} %gain.3, f32[8,64,256]{2,1,0:T(8,128)} %t_hbm.3, f32[1,64,256]{2,1,0:T(8,128)} %copy-done.4, f32[1,64,256]{2,1,0:T(8,128)} %copy-done.3, ...), custom_call_target="tpu_custom_call" | custom-call | flops 6291456 | bytes 10485760 | tf_op jit(solution)/shard_map/partial_sums/pallas_call | solution.py:235
  19.0 5.9 %all-to-all-start = ((f32[8,64,256]{2,1,0:T(8,128)}), f32[8,64,256]{2,1,0:T(8,128)S(1)}, u32[]{:S(2)}, u32[]{:S(2)}) async-start(f32[8,64,256]{2,1,0:T(8,128)} %get-tuple-element.5), calls=%async_computation | async-start | bytes 1048576 | tf_op jit(solution)/shard_map/all_to_all | solution.py:308
  25.0 0.0 collective-permute-start.2
  25.0 6.7 %collective-permute-start.3 = (f32[4,3,1,64,256]{4,3,2,1,0:T(8,128)}, f32[4,3,1,64,256]{4,3,2,1,0:T(8,128)S(1)}, u32[]{:S(2)}, u32[]{:S(2)}) collective-permute-start(f32[4,3,1,64,256]{4,3,2,1,0:T(8,128)} %get-tuple-element.7), channel_id=1, source_target_pairs={{1,2},{3,4},{5,6},{7,8},{9,10},{11,12},{13,14},{15,16},{17,18},{19... | collective-permute-start | bytes 2359304 | tf_op jit(solution)/shard_map/ppermute | solution.py:307
  31.7 1.6 %all-to-all-done.refs_2_ = f32[8,64,256]{2,1,0:T(8,128)S(1)} async-done(((f32[8,64,256]{2,1,0:T(8,128)}), f32[8,64,256]{2,1,0:T(8,128)S(1)}, u32[]{:S(2)}, u32[]{:S(2)}) %all-to-all-start) | async-done | bytes 524320 | tf_op jit(solution)/shard_map/all_to_all | solution.py:308
  33.3 0.0 copy-done
  33.3 0.9 %share_update.1 = f32[8,64,256]{2,1,0:T(8,128)} custom-call(s32[1]{0:T(128)} %bitcast.refs_0_, f32[8,64,256]{2,1,0:T(8,128)S(1)} %copy-done, f32[8,64,256]{2,1,0:T(8,128)S(1)} %all-to-all-done.refs_2_), custom_call_target="tpu_custom_call" | custom-call | flops 131072 | bytes 2097152 | tf_op jit(solution)/shard_map/share_update/pallas_call | solution.py:254
  34.2 4.5 %all-to-all-start.1 = ((f32[8,64,256]{2,1,0:T(8,128)}), f32[8,64,256]{2,1,0:T(8,128)S(1)}, u32[]{:S(2)}, u32[]{:S(2)}) async-start(f32[8,64,256]{2,1,0:T(8,128)} %share_update.1), calls=%async_computation.1 | async-start | bytes 1048576 | tf_op jit(solution)/shard_map/all_to_all | solution.py:310
  38.7 0.0 collective-permute-done.2.vi_hbm
  38.7 0.0 copy-start.1
  38.7 3.5 %collective-permute-done.3.vo_hbm = f32[4,3,1,64,256]{4,3,2,1,0:T(8,128)S(1)} collective-permute-done((f32[4,3,1,64,256]{4,3,2,1,0:T(8,128)}, f32[4,3,1,64,256]{4,3,2,1,0:T(8,128)S(1)}, u32[]{:S(2)}, u32[]{:S(2)}) %collective-permute-start.3) | collective-permute-done | bytes 786464 | tf_op jit(solution)/shard_map/ppermute | solution.py:307
  42.2 0.0 copy-done.1
  42.2 0.0 copy-start.2
  42.2 0.9 %copy-done.2 = f32[4,3,1,64,256]{4,3,2,1,0:T(8,128)} copy-done((f32[4,3,1,64,256]{4,3,2,1,0:T(8,128)}, f32[4,3,1,64,256]{4,3,2,1,0:T(8,128)S(1)}, u32[]{:S(2)}) %copy-start.2) | copy-done | bytes 786456
  43.1 12.5 %moved.1 = f32[4,3,8,64,256]{4,3,2,1,0:T(8,128)} custom-call(s32[1]{0:T(128)} %bitcast.1.odd_ref, s32[4]{0:T(128)} %cohort.3, f32[8]{0:T(128)} %gain.3, f32[4]{0:T(128)} %stiff.1, f32[8,64,256]{2,1,0:T(8,128)} %t_hbm.3, f32[1,64,256]{2,1,0:T(8,128)} %copy-done.4, f32[1,64,256]{2,1,0:T(8,128)} %copy-done.3, s32[8,64,256]{2,1,0:T(8,128)} %lab_hbm.1, ...), custom_call_target="tpu_custom_call" | custom-call | flops 12582912 | bytes 16777216 | tf_op jit(solution)/shard_map/moved/pallas_call | solution.py:269
  55.7 0.0 all-to-all-done.1
  55.7 0.8 %copy.10 = f32[8,64,256]{2,1,0:T(8,128)} copy(f32[8,64,256]{2,1,0:T(8,128)S(1)} %all-to-all-done.1) | data formatting | bytes 1048576
Async XLA Ops:
  0.6 32.7 %copy-start = (f32[8,64,256]{2,1,0:T(8,128)S(1)}, f32[8,64,256]{2,1,0:T(8,128)}, u32[]{:S(2)}) copy-start(f32[8,64,256]{2,1,0:T(8,128)} %t_hbm.3) | copy-start | bytes 1572868
  1.6 10.0 %collective-permute-start.1 = (f32[1,64,256]{2,1,0:T(8,128)S(1)}, f32[1,64,256]{2,1,0:T(8,128)S(1)}, u32[]{:S(2)}, u32[]{:S(2)}) collective-permute-start(f32[1,64,256]{2,1,0:T(8,128)S(1)} %get-tuple-element.8), channel_id=1, source_target_pairs={{1,2},{3,4},{5,6},{7,8},{9,10},{11,12},{13,14},{15,16},{17,18},{19... | collective-permute-start | bytes 196616 | tf_op jit(solution)/shard_map/ppermute | solution.py:303
  9.7 1.9 %collective-permute-start = (f32[1,64,256]{2,1,0:T(8,128)S(1)}, f32[1,64,256]{2,1,0:T(8,128)S(1)}, u32[]{:S(2)}, u32[]{:S(2)}) collective-permute-start(f32[1,64,256]{2,1,0:T(8,128)S(1)} %get-tuple-element.9), channel_id=1, source_target_pairs={{0,1},{1,0},{2,3},{3,2},{4,5},{5,4},{6,7},{7,6},{8,9},{9,8},{10,11... | collective-permute-start | bytes 196616 | tf_op jit(solution)/shard_map/ppermute | solution.py:302
  11.6 0.6 %copy-start.3 = (f32[1,64,256]{2,1,0:T(8,128)}, f32[1,64,256]{2,1,0:T(8,128)S(1)}, u32[]{:S(2)}) copy-start(f32[1,64,256]{2,1,0:T(8,128)S(1)} %collective-permute-done.1.to_hbm) | copy-start | bytes 196612
  11.6 0.6 %copy-start.4 = (f32[1,64,256]{2,1,0:T(8,128)}, f32[1,64,256]{2,1,0:T(8,128)S(1)}, u32[]{:S(2)}) copy-start(f32[1,64,256]{2,1,0:T(8,128)S(1)} %collective-permute-done.ti_hbm) | copy-start | bytes 196612
  19.0 14.3 %all-to-all-start = ((f32[8,64,256]{2,1,0:T(8,128)}), f32[8,64,256]{2,1,0:T(8,128)S(1)}, u32[]{:S(2)}, u32[]{:S(2)}) async-start(f32[8,64,256]{2,1,0:T(8,128)} %get-tuple-element.5), calls=%async_computation | async-start | bytes 1048576 | tf_op jit(solution)/shard_map/all_to_all | solution.py:308
  25.0 13.7 %collective-permute-start.2 = (f32[4,3,1,64,256]{4,3,2,1,0:T(8,128)}, f32[4,3,1,64,256]{4,3,2,1,0:T(8,128)S(1)}, u32[]{:S(2)}, u32[]{:S(2)}) collective-permute-start(f32[4,3,1,64,256]{4,3,2,1,0:T(8,128)} %get-tuple-element.6), channel_id=1, source_target_pairs={{0,1},{1,0},{2,3},{3,2},{4,5},{5,4},{6,7},{7,6},{8,9},{9,8},{10,11... | collective-permute-start | bytes 2359304 | tf_op jit(solution)/shard_map/ppermute | solution.py:306
  25.0 17.2 %collective-permute-start.3 = (f32[4,3,1,64,256]{4,3,2,1,0:T(8,128)}, f32[4,3,1,64,256]{4,3,2,1,0:T(8,128)S(1)}, u32[]{:S(2)}, u32[]{:S(2)}) collective-permute-start(f32[4,3,1,64,256]{4,3,2,1,0:T(8,128)} %get-tuple-element.7), channel_id=1, source_target_pairs={{1,2},{3,4},{5,6},{7,8},{9,10},{11,12},{13,14},{15,16},{17,18},{19... | collective-permute-start | bytes 2359304 | tf_op jit(solution)/shard_map/ppermute | solution.py:307
  34.2 21.5 %all-to-all-start.1 = ((f32[8,64,256]{2,1,0:T(8,128)}), f32[8,64,256]{2,1,0:T(8,128)S(1)}, u32[]{:S(2)}, u32[]{:S(2)}) async-start(f32[8,64,256]{2,1,0:T(8,128)} %share_update.1), calls=%async_computation.1 | async-start | bytes 1048576 | tf_op jit(solution)/shard_map/all_to_all | solution.py:310
  38.7 3.5 %copy-start.1 = (f32[4,3,1,64,256]{4,3,2,1,0:T(8,128)}, f32[4,3,1,64,256]{4,3,2,1,0:T(8,128)S(1)}, u32[]{:S(2)}) copy-start(f32[4,3,1,64,256]{4,3,2,1,0:T(8,128)S(1)} %collective-permute-done.2.vi_hbm) | copy-start | bytes 2359300
  42.2 0.9 %copy-start.2 = (f32[4,3,1,64,256]{4,3,2,1,0:T(8,128)}, f32[4,3,1,64,256]{4,3,2,1,0:T(8,128)S(1)}, u32[]{:S(2)}) copy-start(f32[4,3,1,64,256]{4,3,2,1,0:T(8,128)S(1)} %collective-permute-done.3.vo_hbm) | copy-start | bytes 2359300

commit v3 on v2

--- a/solution.py
+++ b/solution.py
@@ -62,67 +62,6 @@
     ]
 
 
-def partial_kernel(
-    odd_ref, cohort, gain, t_hbm, ti_hbm, to_hbm, im_hbm, v_hbm, sum_ref, inner_hbm, outer_hbm,
-    t_ref, im_ref, v_ref, s_ref, t_sem, im_sem, v_sem, in_sem, out_sem,
-):
-    subjects, depth, count, width = im_ref.shape
-    odd = odd_ref[0]
-    template = template_copies(odd, t_hbm, ti_hbm, to_hbm, t_ref, t_sem)
-    images = [pltpu.make_async_copy(im_hbm.at[s], im_ref.at[s], im_sem.at[s]) for s in range(subjects)]
-    fields = [
-        [pltpu.make_async_copy(v_hbm.at[s, c], v_ref.at[s, c], v_sem.at[s, c]) for c in range(3)]
-        for s in range(subjects)
-    ]
-    facing = jnp.where(odd == 1, 0, depth - 1)
-    inner = [
-        pltpu.make_async_copy(v_ref.at[s, :, pl.ds(facing, 1)], inner_hbm.at[s], in_sem.at[s])
-        for s in range(subjects)
-    ]
-    outer = [
-        pltpu.make_async_copy(v_ref.at[s, :, pl.ds(depth - 1 - facing, 1)], outer_hbm.at[s], out_sem.at[s])
-        for s in range(subjects)
-    ]
-    for copy in template:
-        copy.start()
-    for s in range(subjects):
-        images[s].start()
-        for copy in fields[s]:
-            copy.start()
-    for copy in template:
-        copy.wait()
-    fill_slopes(t_ref, s_ref)
-    pair = 2 if subjects % 2 == 0 else 1
-    for low in range(0, subjects, pair):
-        members = range(low, low + pair)
-        for s in members:
-            images[s].wait()
-            for copy in fields[s]:
-                copy.wait()
-            inner[s].start()
-            outer[s].start()
-        levels = [gain[cohort[s]] for s in members]
-
-        @pl.loop(0, depth)
-        def _(z):
-            for j in range(count // ROWS):
-                rows = pl.ds(j * ROWS, ROWS)
-                value = float(pair) * t_ref[z + 1, rows, :]
-                for s, level in zip(members, levels):
-                    value = value - level * im_ref[s, z, rows, :].astype(jnp.float32)
-                for c in range(3):
-                    field = v_ref[low, c, z, rows, :]
-                    for s in members[1:]:
-                        field = field + v_ref[s, c, z, rows, :]
-                    value = value + s_ref[c, z, rows, :] * field
-                if low:
-                    value = value + sum_ref[z, rows, :]
-                sum_ref[z, rows, :] = value
-
-    for copy in inner + outer:
-        copy.wait()
-
-
 def share_kernel(place, scale, t_hbm, parts_ref, out_ref, own_ref, sem):
     groups, count, width = parts_ref.shape
     copy = pltpu.make_async_copy(t_hbm.at[place[0]], own_ref, sem)
@@ -139,15 +78,16 @@
 
 
 def move_kernel(
-    odd_ref, cohort, gain, stiff, t_hbm, ti_hbm, to_hbm, lab_hbm, im_hbm, v_hbm, vi_hbm, vo_hbm, out_hbm,
+    odd_ref, cohort, gain, stiff, t_hbm, ti_hbm, to_hbm, lab_hbm, im_hbm, v_hbm,
+    sum_ref, inner_hbm, outer_hbm, out_hbm,
     t_ref, lab_ref, im_ref, v_ref, new_ref, s_ref, k_ref,
-    t_sem, lab_sem, im_sem, v_sem, vi_sem, vo_sem, out_sem,
+    t_sem, lab_sem, im_sem, v_sem, in_sem, far_sem, out_sem,
 ):
     subjects, depth, count, width = im_ref.shape
     odd = odd_ref[0]
     template = template_copies(odd, t_hbm, ti_hbm, to_hbm, t_ref, t_sem)
     template.append(pltpu.make_async_copy(lab_hbm, lab_ref, lab_sem))
-    inner = jnp.where(odd == 1, 0, depth + 1)
+    facing = jnp.where(odd == 1, 0, depth - 1)
     half = depth // 2
 
     def arrivals(s):
@@ -156,11 +96,13 @@
             copies.append(
                 pltpu.make_async_copy(v_hbm.at[s, c], v_ref.at[s, c, pl.ds(1, depth)], v_sem.at[s, c])
             )
-        copies.append(pltpu.make_async_copy(vi_hbm.at[s], v_ref.at[s, :, pl.ds(inner, 1)], vi_sem.at[s]))
-        copies.append(
-            pltpu.make_async_copy(vo_hbm.at[s], v_ref.at[s, :, pl.ds(depth + 1 - inner, 1)], vo_sem.at[s])
-        )
         return copies
+
+    def edges(s):
+        return [
+            pltpu.make_async_copy(v_ref.at[s, :, pl.ds(1 + facing, 1)], inner_hbm.at[s], in_sem.at[s]),
+            pltpu.make_async_copy(v_ref.at[s, :, pl.ds(depth - facing, 1)], outer_hbm.at[s], far_sem.at[s]),
+        ]
 
     def departure(s, part):
         planes = pl.ds(part * half, half)
@@ -171,15 +113,20 @@
     for s in range(subjects):
         for copy in arrivals(s):
             copy.start()
+    sum_ref[...] = jnp.zeros_like(sum_ref)
+    outside = jnp.zeros((count, width), jnp.float32)
+
+    @pl.loop(0, subjects)
+    def _(s):
+        for c in range(3):
+            v_ref[s, c, 0] = outside
+            v_ref[s, c, depth + 1] = outside
+
     for copy in template:
         copy.wait()
 
     def rate_of(z, rows):
-        label = lab_ref[z, rows, :]
-        rate = jnp.full(label.shape, stiff[0], jnp.float32)
-        for kind in range(1, stiff.shape[0]):
-            rate = jnp.where(label == kind, stiff[kind], rate)
-        k_ref[z, rows, :] = velocity_step * rate
+        k_ref[z, rows, :] = rate_at(lab_ref[z, rows, :], stiff)
 
     fill_slopes(t_ref, s_ref, rate_of)
 
@@ -187,6 +134,8 @@
     def _(s):
         for copy in arrivals(s):
             copy.wait()
+        for copy in edges(s):
+            copy.start()
         level = gain[cohort[s]]
 
         def plane(z):
@@ -199,6 +148,7 @@
                 value = t_ref[z + 1, rows, :] - level * im_ref[s, z, rows, :].astype(jnp.float32)
                 for c in range(3):
                     value = value + slopes[c] * field[c]
+                sum_ref[z, rows, :] = sum_ref[z, rows, :] + value
                 value = velocity_step * value
                 for c in range(3):
                     here = field[c]
@@ -217,8 +167,53 @@
 
     @pl.loop(0, subjects)
     def _(s):
+        for copy in edges(s):
+            copy.wait()
         for part in range(2):
             departure(s, part).wait()
+
+
+def rate_at(label, stiff):
+    rate = jnp.full(label.shape, stiff[0], jnp.float32)
+    for kind in range(1, stiff.shape[0]):
+        rate = jnp.where(label == kind, stiff[kind], rate)
+    return velocity_step * rate
+
+
+def edge_kernel(
+    odd_ref, stiff, lab_hbm, vi_ref, vo_ref, old_hbm, out_hbm, lab_ref, near_ref, far_ref,
+    lab_sem, near_sem, far_sem,
+):
+    subjects = vi_ref.shape[0]
+    depth = lab_hbm.shape[0]
+    odd = odd_ref[0]
+    facing = jnp.where(odd == 1, 0, depth - 1)
+    sides = ((facing, vi_ref, near_ref, near_sem, 0), (depth - 1 - facing, vo_ref, far_ref, far_sem, 1))
+
+    def fetch(s, z, buffer, sem):
+        return pltpu.make_async_copy(old_hbm.at[s, :, pl.ds(z, 1)], buffer.at[s], sem.at[0, s])
+
+    def store(s, z, buffer, sem):
+        return pltpu.make_async_copy(buffer.at[s], out_hbm.at[s, :, pl.ds(z, 1)], sem.at[1, s])
+
+    labels = [pltpu.make_async_copy(lab_hbm.at[z], lab_ref.at[side], lab_sem.at[side]) for z, *_, side in sides]
+    for copy in labels:
+        copy.start()
+    for s in range(subjects):
+        for z, _, buffer, sem, _ in sides:
+            fetch(s, z, buffer, sem).start()
+    for copy in labels:
+        copy.wait()
+    for s in range(subjects):
+        for z, halo, buffer, sem, side in sides:
+            fetch(s, z, buffer, sem).wait()
+            rate = rate_at(lab_ref[side], stiff)
+            for c in range(3):
+                buffer[s, c, 0] = buffer[s, c, 0] + rate * halo[s, c, 0]
+            store(s, z, buffer, sem).start()
+    for s in range(subjects):
+        for z, _, buffer, sem, _ in sides:
+            store(s, z, buffer, sem).wait()
 
 
 SMALL = pl.BlockSpec(memory_space=pltpu.SMEM)
@@ -226,28 +221,6 @@
 FREE = pl.BlockSpec(memory_space=pl.ANY)
 NEAR = pl.BlockSpec(memory_space=pltpu.VMEM)
 COPY = pltpu.SemaphoreType.DMA
-
-
-def partial_sums(odd, cohort, gain, template, t_inner, t_outer, images, velocity):
-    subjects = images.shape[0]
-    depth, count, width = template.shape
-    edge = jax.ShapeDtypeStruct((subjects, 3, 1, count, width), jnp.float32)
-    return pl.pallas_call(
-        partial_kernel,
-        out_shape=[jax.ShapeDtypeStruct(template.shape, jnp.float32), edge, edge],
-        in_specs=[SMALL] * 3 + [FAR, FREE, FREE, FAR, FAR],
-        out_specs=[NEAR, FAR, FAR],
-        scratch_shapes=[
-            pltpu.VMEM((depth + 2, count, width), jnp.float32),
-            pltpu.VMEM(images.shape, images.dtype),
-            pltpu.VMEM(velocity.shape, jnp.float32),
-            pltpu.VMEM((3,) + template.shape, jnp.float32),
-            COPY((3,)), COPY((subjects,)), COPY((subjects, 3)), COPY((subjects,)), COPY((subjects,)),
-        ],
-        compiler_params=pltpu.CompilerParams(vmem_limit_bytes=60 * MIB),
-        cost_estimate=pl.CostEstimate(flops=4 * velocity.size, bytes_accessed=10 * MIB, transcendentals=0),
-        name="partial_sums",
-    )(odd, cohort, gain, template, t_inner, t_outer, images, velocity)
 
 
 def share_update(place, scale, template, parts):
@@ -263,14 +236,16 @@
     )(place, template, parts)
 
 
-def moved(odd, cohort, gain, stiffness, template, t_inner, t_outer, labels, images, velocity, v_inner, v_outer):
+def moved(odd, cohort, gain, stiffness, template, t_inner, t_outer, labels, images, velocity):
     subjects = images.shape[0]
     depth, count, width = template.shape
+    edge = jax.ShapeDtypeStruct((subjects, 3, 1, count, width), jnp.float32)
+    whole = jax.ShapeDtypeStruct(velocity.shape, jnp.float32)
     return pl.pallas_call(
         move_kernel,
-        out_shape=jax.ShapeDtypeStruct(velocity.shape, jnp.float32),
-        in_specs=[SMALL] * 4 + [FAR, FREE, FREE, FAR, FAR, FAR, FREE, FREE],
-        out_specs=FAR,
+        out_shape=[jax.ShapeDtypeStruct(template.shape, jnp.float32), edge, edge, whole],
+        in_specs=[SMALL] * 4 + [FAR] * 6,
+        out_specs=[NEAR, FAR, FAR, FAR],
         scratch_shapes=[
             pltpu.VMEM((depth + 2, count, width), jnp.float32),
             pltpu.VMEM(labels.shape, labels.dtype),
@@ -285,7 +260,28 @@
         compiler_params=pltpu.CompilerParams(vmem_limit_bytes=60 * MIB),
         cost_estimate=pl.CostEstimate(flops=8 * velocity.size, bytes_accessed=16 * MIB, transcendentals=0),
         name="moved",
-    )(odd, cohort, gain, stiffness, template, t_inner, t_outer, labels, images, velocity, v_inner, v_outer)
+    )(odd, cohort, gain, stiffness, template, t_inner, t_outer, labels, images, velocity)
+
+
+def edges_added(odd, stiffness, labels, v_inner, v_outer, velocity):
+    subjects = velocity.shape[0]
+    count, width = labels.shape[1:]
+    return pl.pallas_call(
+        edge_kernel,
+        out_shape=jax.ShapeDtypeStruct(velocity.shape, jnp.float32),
+        in_specs=[SMALL] * 2 + [FAR, NEAR, NEAR, FAR],
+        out_specs=FAR,
+        scratch_shapes=[
+            pltpu.VMEM((2, count, width), labels.dtype),
+            pltpu.VMEM(v_inner.shape, jnp.float32),
+            pltpu.VMEM(v_outer.shape, jnp.float32),
+            COPY((2,)), COPY((2, subjects)), COPY((2, subjects)),
+        ],
+        input_output_aliases={5: 0},
+        compiler_params=pltpu.CompilerParams(vmem_limit_bytes=50 * MIB),
+        cost_estimate=pl.CostEstimate(flops=v_inner.size, bytes_accessed=6 * MIB, transcendentals=0),
+        name="edges_added",
+    )(odd, stiffness, labels, v_inner, v_outer, velocity)
 
 
 def local(template, images, velocity, labels, stiffness, cohort, site_gain):
@@ -302,15 +298,15 @@
     t_inner = lax.ppermute(lax.dynamic_slice_in_dim(template, facing, 1, 0), "slab", inside)
     t_outer = lax.ppermute(lax.dynamic_slice_in_dim(template, depth - 1 - facing, 1, 0), "slab", across)
     odd = odd.reshape(1)
-    part, inner, outer = partial_sums(odd, cohort, site_gain, template, t_inner, t_outer, images, velocity)
+    part, inner, outer, new_velocity = moved(
+        odd, cohort, site_gain, stiffness, template, t_inner, t_outer, labels, images, velocity
+    )
     v_inner = lax.ppermute(inner, "slab", inside)
     v_outer = lax.ppermute(outer, "slab", across)
     parts = lax.all_to_all(part, "grp", 0, 0, tiled=True)
     shares = share_update(place, template_step / (images.shape[0] * groups), template, parts)
     new_template = lax.all_to_all(shares, "grp", 0, 0, tiled=True)
-    new_velocity = moved(
-        odd, cohort, site_gain, stiffness, template, t_inner, t_outer, labels, images, velocity, v_inner, v_outer
-    )
+    new_velocity = edges_added(odd, stiffness, labels, v_inner, v_outer, new_velocity)
     return (new_template, new_velocity)
 
 

time: 56.8 us -> 57.2 us (level)
  the two profiles are of different devices: /device:TPU:6 before, /device:TPU:1 now
where the time goes in v3:
time: 57.2 us; the launch traced here: 56.8 us
  waiting for transfers between devices  18.6 us (33%)
  starting transfers between devices  18 us (31%)
  Pallas kernels  17 us (30%)
  local copies, waits for them, and re-layouts  2.42 us (4%)
  between operations  0.76 us (1%)
    pallas_call x1, Pallas kernels, moved(): pl.pallas_call(move_kernel, out_shape=[jax.ShapeDtypeStruct(template.shap...  13.1 us
    all_to_all x1, waiting for transfers between devices, local(): new_template = lax.all_to_all(shares, 'grp', 0, 0, tiled=True)  11.6 us
    all_to_all x1, waiting for transfers between devices, local(): parts = lax.all_to_all(part, 'grp', 0, 0, tiled=True)  5.2 us
    all_to_all x1, starting transfers between devices, local(): parts = lax.all_to_all(part, 'grp', 0, 0, tiled=True)  5.13 us
    ppermute x1, starting transfers between devices, local(): lax.ppermute(lax.dynamic_slice_in_dim(template, depth - 1 - facing, 1, 0)...  4.94 us
    all_to_all x1, starting transfers between devices, local(): new_template = lax.all_to_all(shares, 'grp', 0, 0, tiled=True)  3.94 us
    ppermute x1, starting transfers between devices, local(): v_outer = lax.ppermute(outer, 'slab', across)  3.92 us
    pallas_call x1, Pallas kernels, edges_added(): pl.pallas_call(edge_kernel, out_shape=jax.ShapeDtypeStruct(velocity.shape...  3.07 us
  transfers between devices with their start and end apart: 6, of which 3 were waited for; matrix products, arithmetic and copies ran while one was open for 0% of the time, Pallas kernels for 7%

profile of v3, /device:TPU:1, one launch (start us, length us, event | category | flops | bytes accessed | tf_op | source)
XLA Modules:
  0.0 56.8 jit_solution(2193893841391203338)
XLA Ops:
  0.6 0.0 copy-start
  0.6 0.0 copy-start.2
  0.7 0.0 copy-start.1
  0.7 1.0 %constant_dynamic-slice_fusion = (f32[1,64,256]{2,1,0:T(8,128)S(1)}, f32[1,64,256]{2,1,0:T(8,128)S(1)}) fusion(f32[8,64,256]{2,1,0:T(8,128)} %refs_1_.1, s32[]{:T(128)S(6)} %select_n.17, s32[]{:T(128)S(6)} %select_n.16), kind=kLoop, calls=%fused_computation | loop fusion | bytes 262152 | tf_op jit(solution)/shard_map/dynamic_slice | solution.py:299
  1.6 4.9 %collective-permute-start.1 = (f32[1,64,256]{2,1,0:T(8,128)S(1)}, f32[1,64,256]{2,1,0:T(8,128)S(1)}, u32[]{:S(2)}, u32[]{:S(2)}) collective-permute-start(f32[1,64,256]{2,1,0:T(8,128)S(1)} %get-tuple-element.10), channel_id=1, source_target_pairs={{1,2},{3,4},{5,6},{7,8},{9,10},{11,12},{13,14},{15,16},{17,18},{19... | collective-permute-start | bytes 196616 | tf_op jit(solution)/shard_map/ppermute | solution.py:299
  6.6 0.1 collective-permute-start
  6.7 1.8 %collective-permute-done.1.to_hbm = f32[1,64,256]{2,1,0:T(8,128)S(1)} collective-permute-done((f32[1,64,256]{2,1,0:T(8,128)S(1)}, f32[1,64,256]{2,1,0:T(8,128)S(1)}, u32[]{:S(2)}, u32[]{:S(2)}) %collective-permute-start.1) | collective-permute-done | bytes 65568 | tf_op jit(solution)/shard_map/ppermute | solution.py:299
  8.5 0.0 copy-start.3
  8.5 0.0 collective-permute-done.ti_hbm
  8.5 0.0 copy-start.4
  8.5 0.6 %copy-done.3 = f32[1,64,256]{2,1,0:T(8,128)} copy-done((f32[1,64,256]{2,1,0:T(8,128)}, f32[1,64,256]{2,1,0:T(8,128)S(1)}, u32[]{:S(2)}) %copy-start.3) | copy-done | bytes 65560
  9.2 0.0 copy-done.4
  9.2 13.1 %moved.1 = (f32[8,64,256]{2,1,0:T(8,128)}, f32[4,3,1,64,256]{4,3,2,1,0:T(8,128)}, f32[4,3,1,64,256]{4,3,2,1,0:T(8,128)}, f32[4,3,8,64,256]{4,3,2,1,0:T(8,128)}) custom-call(s32[1]{0:T(128)} %bitcast.1.odd_ref, s32[4]{0:T(128)} %cohort.1, f32[8]{0:T(128)} %gain.1, f32[4]{0:T(128)} %stiff.3, f32[8,64,256]{2,1,0:T(8,128)} %refs_1_.1, f32[1,64,256]{2,1,0:T(8,128)} %copy-done.4, ...), custom_call_target="tpu_custom_call" | custom-call | flops 12582912 | bytes 16777216 | tf_op jit(solution)/shard_map/moved/pallas_call | solution.py:244
  22.2 5.1 %all-to-all-start = ((f32[8,64,256]{2,1,0:T(8,128)}), f32[8,64,256]{2,1,0:T(8,128)S(1)}, u32[]{:S(2)}, u32[]{:S(2)}) async-start(f32[8,64,256]{2,1,0:T(8,128)} %get-tuple-element.6), calls=%async_computation | async-start | bytes 1048576 | tf_op jit(solution)/shard_map/all_to_all | solution.py:306
  27.4 0.0 collective-permute-start.2
  27.4 3.9 %collective-permute-start.3 = (f32[4,3,1,64,256]{4,3,2,1,0:T(8,128)}, f32[4,3,1,64,256]{4,3,2,1,0:T(8,128)S(1)}, u32[]{:S(2)}, u32[]{:S(2)}) collective-permute-start(f32[4,3,1,64,256]{4,3,2,1,0:T(8,128)} %get-tuple-element.8), channel_id=1, source_target_pairs={{1,2},{3,4},{5,6},{7,8},{9,10},{11,12},{13,14},{15,16},{17,18},{19... | collective-permute-start | bytes 2359304 | tf_op jit(solution)/shard_map/ppermute | solution.py:305
  31.3 5.2 %all-to-all-done.refs_2_ = f32[8,64,256]{2,1,0:T(8,128)S(1)} async-done(((f32[8,64,256]{2,1,0:T(8,128)}), f32[8,64,256]{2,1,0:T(8,128)S(1)}, u32[]{:S(2)}, u32[]{:S(2)}) %all-to-all-start) | async-done | bytes 524320 | tf_op jit(solution)/shard_map/all_to_all | solution.py:306
  36.5 0.0 copy-done
  36.5 0.9 %share_update.1 = f32[8,64,256]{2,1,0:T(8,128)} custom-call(s32[1]{0:T(128)} %bitcast.refs_0_, f32[8,64,256]{2,1,0:T(8,128)S(1)} %copy-done, f32[8,64,256]{2,1,0:T(8,128)S(1)} %all-to-all-done.refs_2_), custom_call_target="tpu_custom_call" | custom-call | flops 131072 | bytes 2097152 | tf_op jit(solution)/shard_map/share_update/pallas_call | solution.py:227
  37.4 3.9 %all-to-all-start.1 = ((f32[8,64,256]{2,1,0:T(8,128)}), f32[8,64,256]{2,1,0:T(8,128)S(1)}, u32[]{:S(2)}, u32[]{:S(2)}) async-start(f32[8,64,256]{2,1,0:T(8,128)} %share_update.1), calls=%async_computation.1 | async-start | bytes 1048576 | tf_op jit(solution)/shard_map/all_to_all | solution.py:308
  41.4 0.0 collective-permute-done.2.vi_ref
  41.4 0.0 collective-permute-done.3.vo_ref
  41.4 0.0 copy-done.2
  41.4 0.0 copy-done.1
  41.4 3.1 %edges_added.1 = f32[4,3,8,64,256]{4,3,2,1,0:T(8,128)} custom-call(s32[1]{0:T(128)} %bitcast.1.odd_ref, f32[4]{0:T(128)S(1)} %copy-done.2, s32[8,64,256]{2,1,0:T(8,128)S(1)} %copy-done.1, f32[4,3,1,64,256]{4,3,2,1,0:T(8,128)S(1)} %collective-permute-done.2.vi_ref, ...), custom_call_target="tpu_custom_call", output_to_operand_aliasing={{}: (5, {})} | custom-call | flops 196608 | bytes 6291456 | tf_op jit(solution)/shard_map/edges_added/pallas_call | solution.py:269
  44.5 11.6 %all-to-all-done.1 = f32[8,64,256]{2,1,0:T(8,128)S(1)} async-done(((f32[8,64,256]{2,1,0:T(8,128)}), f32[8,64,256]{2,1,0:T(8,128)S(1)}, u32[]{:S(2)}, u32[]{:S(2)}) %all-to-all-start.1) | async-done | bytes 524320 | tf_op jit(solution)/shard_map/all_to_all | solution.py:308
  56.0 0.8 %copy.12 = f32[8,64,256]{2,1,0:T(8,128)} copy(f32[8,64,256]{2,1,0:T(8,128)S(1)} %all-to-all-done.1) | data formatting | bytes 1048576
Async XLA Ops:
  0.6 35.9 %copy-start = (f32[8,64,256]{2,1,0:T(8,128)S(1)}, f32[8,64,256]{2,1,0:T(8,128)}, u32[]{:S(2)}) copy-start(f32[8,64,256]{2,1,0:T(8,128)} %refs_1_.1) | copy-start | bytes 1572868
  0.6 40.8 %copy-start.2 = (f32[4]{0:T(128)S(1)}, f32[4]{0:T(128)}, u32[]{:S(2)}) copy-start(f32[4]{0:T(128)} %stiff.3) | copy-start | bytes 52
  0.7 40.8 %copy-start.1 = (s32[8,64,256]{2,1,0:T(8,128)S(1)}, s32[8,64,256]{2,1,0:T(8,128)}, u32[]{:S(2)}) copy-start(s32[8,64,256]{2,1,0:T(8,128)} %lab_hbm.3) | copy-start | bytes 1572868
  1.6 6.9 %collective-permute-start.1 = (f32[1,64,256]{2,1,0:T(8,128)S(1)}, f32[1,64,256]{2,1,0:T(8,128)S(1)}, u32[]{:S(2)}, u32[]{:S(2)}) collective-permute-start(f32[1,64,256]{2,1,0:T(8,128)S(1)} %get-tuple-element.10), channel_id=1, source_target_pairs={{1,2},{3,4},{5,6},{7,8},{9,10},{11,12},{13,14},{15,16},{17,18},{19... | collective-permute-start | bytes 196616 | tf_op jit(solution)/shard_map/ppermute | solution.py:299
  6.6 1.9 %collective-permute-start = (f32[1,64,256]{2,1,0:T(8,128)S(1)}, f32[1,64,256]{2,1,0:T(8,128)S(1)}, u32[]{:S(2)}, u32[]{:S(2)}) collective-permute-start(f32[1,64,256]{2,1,0:T(8,128)S(1)} %get-tuple-element.11), channel_id=1, source_target_pairs={{0,1},{1,0},{2,3},{3,2},{4,5},{5,4},{6,7},{7,6},{8,9},{9,8},{10,11... | collective-permute-start | bytes 196616 | tf_op jit(solution)/shard_map/ppermute | solution.py:298
  8.5 0.6 %copy-start.3 = (f32[1,64,256]{2,1,0:T(8,128)}, f32[1,64,256]{2,1,0:T(8,128)S(1)}, u32[]{:S(2)}) copy-start(f32[1,64,256]{2,1,0:T(8,128)S(1)} %collective-permute-done.1.to_hbm) | copy-start | bytes 196612
  8.5 0.6 %copy-start.4 = (f32[1,64,256]{2,1,0:T(8,128)}, f32[1,64,256]{2,1,0:T(8,128)S(1)}, u32[]{:S(2)}) copy-start(f32[1,64,256]{2,1,0:T(8,128)S(1)} %collective-permute-done.ti_hbm) | copy-start | bytes 196612
  22.2 14.3 %all-to-all-start = ((f32[8,64,256]{2,1,0:T(8,128)}), f32[8,64,256]{2,1,0:T(8,128)S(1)}, u32[]{:S(2)}, u32[]{:S(2)}) async-start(f32[8,64,256]{2,1,0:T(8,128)} %get-tuple-element.6), calls=%async_computation | async-start | bytes 1048576 | tf_op jit(solution)/shard_map/all_to_all | solution.py:306
  27.4 14.0 %collective-permute-start.2 = (f32[4,3,1,64,256]{4,3,2,1,0:T(8,128)}, f32[4,3,1,64,256]{4,3,2,1,0:T(8,128)S(1)}, u32[]{:S(2)}, u32[]{:S(2)}) collective-permute-start(f32[4,3,1,64,256]{4,3,2,1,0:T(8,128)} %get-tuple-element.7), channel_id=1, source_target_pairs={{0,1},{1,0},{2,3},{3,2},{4,5},{5,4},{6,7},{7,6},{8,9},{9,8},{10,11... | collective-permute-start | bytes 2359304 | tf_op jit(solution)/shard_map/ppermute | solution.py:304
  27.4 14.0 %collective-permute-start.3 = (f32[4,3,1,64,256]{4,3,2,1,0:T(8,128)}, f32[4,3,1,64,256]{4,3,2,1,0:T(8,128)S(1)}, u32[]{:S(2)}, u32[]{:S(2)}) collective-permute-start(f32[4,3,1,64,256]{4,3,2,1,0:T(8,128)} %get-tuple-element.8), channel_id=1, source_target_pairs={{1,2},{3,4},{5,6},{7,8},{9,10},{11,12},{13,14},{15,16},{17,18},{19... | collective-permute-start | bytes 2359304 | tf_op jit(solution)/shard_map/ppermute | solution.py:305
  37.4 18.6 %all-to-all-start.1 = ((f32[8,64,256]{2,1,0:T(8,128)}), f32[8,64,256]{2,1,0:T(8,128)S(1)}, u32[]{:S(2)}, u32[]{:S(2)}) async-start(f32[8,64,256]{2,1,0:T(8,128)} %share_update.1), calls=%async_computation.1 | async-start | bytes 1048576 | tf_op jit(solution)/shard_map/all_to_all | solution.py:308

commit v4 on v2

--- a/solution.py
+++ b/solution.py
@@ -1,3 +1,5 @@
+import functools
+
 import jax
 import jax.numpy as jnp
 from jax import lax
@@ -123,7 +125,8 @@
         copy.wait()
 
 
-def share_kernel(place, scale, t_hbm, parts_ref, out_ref, own_ref, sem):
+def share_kernel(place, scale, t_hbm, parts_ref, _, out_ref, mark_ref, own_ref, sem):
+    mark_ref[...] = jnp.zeros_like(mark_ref)
     groups, count, width = parts_ref.shape
     copy = pltpu.make_async_copy(t_hbm.at[place[0]], own_ref, sem)
     copy.start()
@@ -138,56 +141,85 @@
             out_ref[g, rows, :] = value
 
 
-def move_kernel(
-    odd_ref, cohort, gain, stiff, t_hbm, ti_hbm, to_hbm, lab_hbm, im_hbm, v_hbm, vi_hbm, vo_hbm, out_hbm,
-    t_ref, lab_ref, im_ref, v_ref, new_ref, s_ref, k_ref,
-    t_sem, lab_sem, im_sem, v_sem, vi_sem, vo_sem, out_sem,
-):
+def rate_at(label, stiff):
+    rate = jnp.full(label.shape, stiff[0], jnp.float32)
+    for kind in range(1, stiff.shape[0]):
+        rate = jnp.where(label == kind, stiff[kind], rate)
+    return velocity_step * rate
+
+
+def move_kernel(first, final, odd_ref, cohort, gain, stiff, t_hbm, ti_hbm, to_hbm, lab_hbm, im_hbm, v_hbm, *refs):
+    if final:
+        vi_ref, vo_ref, old_hbm, _, out_hbm, *refs = refs
+    else:
+        _, out_hbm, mark_ref, *refs = refs
+        mark_ref[...] = jnp.zeros_like(mark_ref)
+    t_ref, lab_ref, im_ref, v_ref, new_ref, s_ref, k_ref, t_sem, lab_sem, im_sem, v_sem, out_sem, *refs = refs
     subjects, depth, count, width = im_ref.shape
     odd = odd_ref[0]
     template = template_copies(odd, t_hbm, ti_hbm, to_hbm, t_ref, t_sem)
     template.append(pltpu.make_async_copy(lab_hbm, lab_ref, lab_sem))
-    inner = jnp.where(odd == 1, 0, depth + 1)
+    facing = jnp.where(odd == 1, 0, depth - 1)
     half = depth // 2
 
     def arrivals(s):
-        copies = [pltpu.make_async_copy(im_hbm.at[s], im_ref.at[s], im_sem.at[s])]
+        copies = [pltpu.make_async_copy(im_hbm.at[first + s], im_ref.at[s], im_sem.at[s])]
         for c in range(3):
             copies.append(
-                pltpu.make_async_copy(v_hbm.at[s, c], v_ref.at[s, c, pl.ds(1, depth)], v_sem.at[s, c])
+                pltpu.make_async_copy(v_hbm.at[first + s, c], v_ref.at[s, c, pl.ds(1, depth)], v_sem.at[s, c])
             )
-        copies.append(pltpu.make_async_copy(vi_hbm.at[s], v_ref.at[s, :, pl.ds(inner, 1)], vi_sem.at[s]))
-        copies.append(
-            pltpu.make_async_copy(vo_hbm.at[s], v_ref.at[s, :, pl.ds(depth + 1 - inner, 1)], vo_sem.at[s])
-        )
         return copies
 
     def departure(s, part):
         planes = pl.ds(part * half, half)
-        return pltpu.make_async_copy(new_ref.at[s, :, planes], out_hbm.at[s, :, planes], out_sem.at[s, part])
+        return pltpu.make_async_copy(
+            new_ref.at[s, :, planes], out_hbm.at[first + s, :, planes], out_sem.at[s, part]
+        )
 
     for copy in template:
         copy.start()
     for s in range(subjects):
         for copy in arrivals(s):
             copy.start()
+    if final:
+        near_ref, far_ref, near_sem, far_sem = refs
+        sides = ((facing, vi_ref, near_ref, near_sem), (depth - 1 - facing, vo_ref, far_ref, far_sem))
+
+        def fetch(s, z, buffer, sem):
+            return pltpu.make_async_copy(old_hbm.at[s, :, pl.ds(z, 1)], buffer.at[s], sem.at[0, s])
+
+        def store(s, z, buffer, sem):
+            return pltpu.make_async_copy(buffer.at[s], out_hbm.at[s, :, pl.ds(z, 1)], sem.at[1, s])
+
+        for s in range(first):
+            for z, _, buffer, sem in sides:
+                fetch(s, z, buffer, sem).start()
+    outside = jnp.zeros((count, width), jnp.float32)
+    inner = jnp.where(odd == 1, 0, depth + 1)
+    for s in range(subjects):
+        for c in range(3):
+            v_ref[s, c, inner] = vi_ref[first + s, c, 0] if final else outside
+            v_ref[s, c, depth + 1 - inner] = vo_ref[first + s, c, 0] if final else outside
     for copy in template:
         copy.wait()
 
     def rate_of(z, rows):
-        label = lab_ref[z, rows, :]
-        rate = jnp.full(label.shape, stiff[0], jnp.float32)
-        for kind in range(1, stiff.shape[0]):
-            rate = jnp.where(label == kind, stiff[kind], rate)
-        k_ref[z, rows, :] = velocity_step * rate
+        k_ref[z, rows, :] = rate_at(lab_ref[z, rows, :], stiff)
 
     fill_slopes(t_ref, s_ref, rate_of)
+    if final:
+        for s in range(first):
+            for z, halo, buffer, sem in sides:
+                fetch(s, z, buffer, sem).wait()
+                for c in range(3):
+                    buffer[s, c, 0] = buffer[s, c, 0] + k_ref[z] * halo[s, c, 0]
+                store(s, z, buffer, sem).start()
 
     @pl.loop(0, subjects)
     def _(s):
         for copy in arrivals(s):
             copy.wait()
-        level = gain[cohort[s]]
+        level = gain[cohort[first + s]]
 
         def plane(z):
             for j in range(count // ROWS):
@@ -215,6 +247,11 @@
             pl.loop(part * half, (part + 1) * half)(plane)
             departure(s, part).start()
 
+    if final:
+        for s in range(first):
+            for z, _, buffer, sem in sides:
+                store(s, z, buffer, sem).wait()
+
     @pl.loop(0, subjects)
     def _(s):
         for part in range(2):
@@ -226,6 +263,7 @@
 FREE = pl.BlockSpec(memory_space=pl.ANY)
 NEAR = pl.BlockSpec(memory_space=pltpu.VMEM)
 COPY = pltpu.SemaphoreType.DMA
+MARK = jax.ShapeDtypeStruct((8, 128), jnp.float32)
 
 
 def partial_sums(odd, cohort, gain, template, t_inner, t_outer, images, velocity):
@@ -250,42 +288,45 @@
     )(odd, cohort, gain, template, t_inner, t_outer, images, velocity)
 
 
-def share_update(place, scale, template, parts):
+def share_update(place, scale, template, parts, after):
     return pl.pallas_call(
         lambda *refs: share_kernel(refs[0], scale, *refs[1:]),
-        out_shape=jax.ShapeDtypeStruct(parts.shape, jnp.float32),
-        in_specs=[SMALL, FAR, NEAR],
-        out_specs=NEAR,
+        out_shape=[jax.ShapeDtypeStruct(parts.shape, jnp.float32), MARK],
+        in_specs=[SMALL, FAR, NEAR, FAR],
+        out_specs=[NEAR, NEAR],
         scratch_shapes=[pltpu.VMEM(template.shape[1:], jnp.float32), COPY(())],
         compiler_params=pltpu.CompilerParams(vmem_limit_bytes=8 * MIB),
         cost_estimate=pl.CostEstimate(flops=parts.size, bytes_accessed=2 * MIB, transcendentals=0),
         name="share_update",
-    )(place, template, parts)
-
-
-def moved(odd, cohort, gain, stiffness, template, t_inner, t_outer, labels, images, velocity, v_inner, v_outer):
-    subjects = images.shape[0]
+    )(place, template, parts, after)
+
+
+def moved(first, last, odd, cohort, gain, stiffness, template, t_inner, t_outer, labels, images, velocity, after, earlier=()):
+    final = bool(earlier)
+    subjects = last - first
     depth, count, width = template.shape
+    edge = (first, 3, 1, count, width)
+    extra = [pltpu.VMEM(edge, jnp.float32)] * 2 + [COPY((2, first))] * 2 if final else []
     return pl.pallas_call(
-        move_kernel,
-        out_shape=jax.ShapeDtypeStruct(velocity.shape, jnp.float32),
-        in_specs=[SMALL] * 4 + [FAR, FREE, FREE, FAR, FAR, FAR, FREE, FREE],
-        out_specs=FAR,
+        functools.partial(move_kernel, first, final),
+        out_shape=[jax.ShapeDtypeStruct(velocity.shape, jnp.float32)] + ([] if final else [MARK]),
+        in_specs=[SMALL] * 4 + [FAR] * 6 + ([NEAR, NEAR, FAR] if final else []) + [FAR],
+        out_specs=[FAR] if final else [FAR, NEAR],
         scratch_shapes=[
             pltpu.VMEM((depth + 2, count, width), jnp.float32),
             pltpu.VMEM(labels.shape, labels.dtype),
-            pltpu.VMEM(images.shape, images.dtype),
+            pltpu.VMEM((subjects,) + images.shape[1:], images.dtype),
             pltpu.VMEM((subjects, 3, depth + 2, count, width), jnp.float32),
-            pltpu.VMEM(velocity.shape, jnp.float32),
+            pltpu.VMEM((subjects,) + velocity.shape[1:], jnp.float32),
             pltpu.VMEM((3,) + template.shape, jnp.float32),
             pltpu.VMEM(template.shape, jnp.float32),
-            COPY((3,)), COPY(()), COPY((subjects,)), COPY((subjects, 3)),
-            COPY((subjects,)), COPY((subjects,)), COPY((subjects, 2)),
-        ],
-        compiler_params=pltpu.CompilerParams(vmem_limit_bytes=60 * MIB),
-        cost_estimate=pl.CostEstimate(flops=8 * velocity.size, bytes_accessed=16 * MIB, transcendentals=0),
-        name="moved",
-    )(odd, cohort, gain, stiffness, template, t_inner, t_outer, labels, images, velocity, v_inner, v_outer)
+            COPY((3,)), COPY(()), COPY((subjects,)), COPY((subjects, 3)), COPY((subjects, 2)),
+        ] + extra,
+        input_output_aliases={12: 0} if final else {},
+        compiler_params=pltpu.CompilerParams(vmem_limit_bytes=(50 if final else 60) * MIB),
+        cost_estimate=pl.CostEstimate(flops=4 * velocity.size, bytes_accessed=8 * MIB, transcendentals=0),
+        name="moved_last" if final else "moved_first",
+    )(odd, cohort, gain, stiffness, template, t_inner, t_outer, labels, images, velocity, *earlier, after)
 
 
 def local(template, images, velocity, labels, stiffness, cohort, site_gain):
@@ -306,11 +347,13 @@
     v_inner = lax.ppermute(inner, "slab", inside)
     v_outer = lax.ppermute(outer, "slab", across)
     parts = lax.all_to_all(part, "grp", 0, 0, tiled=True)
-    shares = share_update(place, template_step / (images.shape[0] * groups), template, parts)
+    subjects = images.shape[0]
+    split = subjects // 2
+    shared = (odd, cohort, site_gain, stiffness, template, t_inner, t_outer, labels, images, velocity)
+    begun, first_done = moved(0, split, *shared, part)
+    shares, shares_done = share_update(place, template_step / (subjects * groups), template, parts, first_done)
     new_template = lax.all_to_all(shares, "grp", 0, 0, tiled=True)
-    new_velocity = moved(
-        odd, cohort, site_gain, stiffness, template, t_inner, t_outer, labels, images, velocity, v_inner, v_outer
-    )
+    (new_velocity,) = moved(split, subjects, *shared, shares_done, (v_inner, v_outer, begun))
     return (new_template, new_velocity)
 
 

time: 56.8 us -> 58.5 us (1.030)
  waiting for transfers between devices: 6.95 us -> 1.93 us
  Pallas kernels: 20.2 us -> 23 us
  starting transfers between devices: 25.2 us -> 27.3 us
  local copies, waits for them, and re-layouts: 3.32 us -> 4.87 us
    pallas_call x1 -> x2, Pallas kernels: 12.5 us -> 16.1 us  [moved(): pl.pallas_call(functools.partial(move_kernel, first, final), out_shape=[j...]
    ppermute x1, waiting for transfers between devices: 3.47 us -> 0.01 us  [local(): v_outer = lax.ppermute(outer, 'slab', across)]
    all_to_all x1, waiting for transfers between devices: 1.64 us -> 0.01 us  [local(): parts = lax.all_to_all(part, 'grp', 0, 0, tiled=True)]
    unnamed x11 -> x25, local copies, waits for them, and re-layouts: 2.38 us -> 3.99 us
    all_to_all x1, starting transfers between devices: 4.48 us -> 5.7 us  [local(): new_template = lax.all_to_all(shares, 'grp', 0, 0, tiled=True)]
    pallas_call x1, Pallas kernels: 0.91 us -> 0.11 us  [share_update(): pl.pallas_call(lambda *refs: share_kernel(refs[0], scale, *refs[1:]), out...]
    ppermute x1, starting transfers between devices: 8.05 us -> 8.7 us  [local(): lax.ppermute(lax.dynamic_slice_in_dim(template, depth - 1 - facing, 1, 0)...]
  transfers between devices with their start and end apart: 6 -> 6, of which waited for: 3 -> 1; matrix products, arithmetic and copies ran while one was open for 0% -> 0% of each run, Pallas kernels for 24% -> 28%
where the time goes in v4:
time: 58.5 us; the launch traced here: 57.9 us
  starting transfers between devices  27.3 us (47%)
  Pallas kernels  23 us (39%)
  local copies, waits for them, and re-layouts  4.87 us (8%)
  waiting for transfers between devices  1.93 us (3%)
  between operations  0.89 us (2%)
    pallas_call x2, Pallas kernels, moved(): pl.pallas_call(functools.partial(move_kernel, first, final), out_shape=[j...  16.1 us
    ppermute x1, starting transfers between devices, local(): lax.ppermute(lax.dynamic_slice_in_dim(template, depth - 1 - facing, 1, 0)...  8.7 us
    pallas_call x1, Pallas kernels, partial_sums(): pl.pallas_call(partial_kernel, out_shape=[jax.ShapeDtypeStruct(template.s...  6.76 us
    ppermute x1, starting transfers between devices, local(): v_outer = lax.ppermute(outer, 'slab', across)  6.69 us
    all_to_all x1, starting transfers between devices, local(): parts = lax.all_to_all(part, 'grp', 0, 0, tiled=True)  6.07 us
    all_to_all x1, starting transfers between devices, local(): new_template = lax.all_to_all(shares, 'grp', 0, 0, tiled=True)  5.7 us
    unnamed x25, local copies, waits for them, and re-layouts  3.99 us
    ppermute x1, waiting for transfers between devices, local(): lax.ppermute(lax.dynamic_slice_in_dim(template, depth - 1 - facing, 1, 0)...  1.91 us
  transfers between devices with their start and end apart: 6, of which 1 were waited for; matrix products, arithmetic and copies ran while one was open for 0% of the time, Pallas kernels for 28%

profile of v4, /device:TPU:6, one launch (start us, length us, event | category | flops | bytes accessed | tf_op | source)
XLA Modules:
  0.0 57.9 jit_solution(8204894949808097619)
XLA Ops:
  0.6 0.9 %constant_dynamic-slice_fusion = (f32[1,64,256]{2,1,0:T(8,128)S(1)}, f32[1,64,256]{2,1,0:T(8,128)S(1)}) fusion(f32[8,64,256]{2,1,0:T(8,128)} %t_hbm.5, s32[]{:T(128)S(6)} %select_n.17, s32[]{:T(128)S(6)} %select_n.16), kind=kLoop, calls=%fused_computation | loop fusion | bytes 262152 | tf_op jit(solution)/shard_map/dynamic_slice | solution.py:344
  1.5 0.1 collective-permute-start
  1.6 8.7 %collective-permute-start.1 = (f32[1,64,256]{2,1,0:T(8,128)S(1)}, f32[1,64,256]{2,1,0:T(8,128)S(1)}, u32[]{:S(2)}, u32[]{:S(2)}) collective-permute-start(f32[1,64,256]{2,1,0:T(8,128)S(1)} %get-tuple-element.16), channel_id=1, source_target_pairs={{1,2},{3,4},{5,6},{7,8},{9,10},{11,12},{13,14},{15,16},{17,18},{19... | collective-permute-start | bytes 196616 | tf_op jit(solution)/shard_map/ppermute | solution.py:344
  10.3 0.0 collective-permute-done.ti_hbm
  10.3 0.0 copy-start.3
  10.4 1.9 %collective-permute-done.1.to_hbm = f32[1,64,256]{2,1,0:T(8,128)S(1)} collective-permute-done((f32[1,64,256]{2,1,0:T(8,128)S(1)}, f32[1,64,256]{2,1,0:T(8,128)S(1)}, u32[]{:S(2)}, u32[]{:S(2)}) %collective-permute-start.1) | collective-permute-done | bytes 65568 | tf_op jit(solution)/shard_map/ppermute | solution.py:344
  12.3 0.0 copy-start.5
  12.3 0.0 copy-done.3
  12.3 0.6 %copy-done.5 = f32[1,64,256]{2,1,0:T(8,128)} copy-done((f32[1,64,256]{2,1,0:T(8,128)}, f32[1,64,256]{2,1,0:T(8,128)S(1)}, u32[]{:S(2)}) %copy-start.5) | copy-done | bytes 65560
  12.9 6.8 %partial_sums.1 = (f32[8,64,256]{2,1,0:T(8,128)}, f32[4,3,1,64,256]{4,3,2,1,0:T(8,128)}, f32[4,3,1,64,256]{4,3,2,1,0:T(8,128)}) custom-call(s32[1]{0:T(128)} %bitcast.1.odd_ref, s32[4]{0:T(128)} %cohort.5, f32[8]{0:T(128)} %gain.5, f32[8,64,256]{2,1,0:T(8,128)} %t_hbm.5, f32[1,64,256]{2,1,0:T(8,128)} %copy-done.3, f32[1,64,256]{2,1,0:T(8,128)} %copy-done.5, ...), custom_call_target="tpu_custom_call" | custom-call | flops 6291456 | bytes 10485760 | tf_op jit(solution)/shard_map/partial_sums/pallas_call | solution.py:273
  19.7 0.0 copy-start
  19.7 0.0 copy-start.1
  19.7 0.0 copy-start.2
  19.7 0.0 copy-start.4
  19.7 0.0 copy-start.6
  19.7 0.0 copy-start.8
  19.7 0.0 copy-start.9
  19.7 0.0 copy-start.11
  19.8 6.1 %all-to-all-start = ((f32[8,64,256]{2,1,0:T(8,128)}), f32[8,64,256]{2,1,0:T(8,128)S(1)}, u32[]{:S(2)}, u32[]{:S(2)}) async-start(f32[8,64,256]{2,1,0:T(8,128)} %get-tuple-element.9.refs_0_), calls=%async_computation | async-start | bytes 1048576 | tf_op jit(solution)/shard_map/all_to_all | solution.py:349
  25.8 0.0 collective-permute-start.2
  25.8 6.7 %collective-permute-start.3 = (f32[4,3,1,64,256]{4,3,2,1,0:T(8,128)}, f32[4,3,1,64,256]{4,3,2,1,0:T(8,128)}, u32[]{:S(2)}, u32[]{:S(2)}) collective-permute-start(f32[4,3,1,64,256]{4,3,2,1,0:T(8,128)} %get-tuple-element.13), channel_id=1, source_target_pairs={{1,2},{3,4},{5,6},{7,8},{9,10},{11,12},{13,14},{15,16},{17,18},{19... | collective-permute-start | bytes 2359304 | tf_op jit(solution)/shard_map/ppermute | solution.py:348
  32.5 8.5 %moved_first.1 = (f32[4,3,8,64,256]{4,3,2,1,0:T(8,128)}, f32[8,128]{1,0:T(8,128)}) custom-call(s32[1]{0:T(128)} %bitcast.1.odd_ref, s32[4]{0:T(128)} %cohort.5, f32[8]{0:T(128)} %gain.5, f32[4]{0:T(128)} %stiff.3, f32[8,64,256]{2,1,0:T(8,128)} %t_hbm.5, f32[1,64,256]{2,1,0:T(8,128)} %copy-done.3, f32[1,64,256]{2,1,0:T(8,128)} %copy-done.5, ...), custom_call_target="tpu_custom_call" | custom-call | flops 6291456 | bytes 8388608 | tf_op jit(solution)/shard_map/moved_first/pallas_call | solution.py:310
  41.0 0.0 all-to-all-done.refs_2_
  41.0 0.0 copy-done
  41.0 0.0 copy-start.10
  41.0 0.7 %copy-done.10 = f32[8,128]{1,0:T(8,128)S(1)} copy-done((f32[8,128]{1,0:T(8,128)S(1)}, f32[8,128]{1,0:T(8,128)}, u32[]{:S(2)}) %copy-start.10) | copy-done | bytes 4120
  41.7 0.1 share_update.1
  41.8 0.0 copy-start.7
  41.8 0.8 %copy-done.7 = f32[8,64,256]{2,1,0:T(8,128)} copy-done((f32[8,64,256]{2,1,0:T(8,128)}, f32[8,64,256]{2,1,0:T(8,128)S(1)}, u32[]{:S(2)}) %copy-start.7) | copy-done | bytes 524312
  42.6 5.7 %all-to-all-start.1 = ((f32[8,64,256]{2,1,0:T(8,128)}), f32[8,64,256]{2,1,0:T(8,128)}, u32[]{:S(2)}, u32[]{:S(2)}) async-start(f32[8,64,256]{2,1,0:T(8,128)} %copy-done.7), calls=%async_computation.1 | async-start | bytes 1048576 | tf_op jit(solution)/shard_map/all_to_all | solution.py:355
  48.3 0.0 collective-permute-done.2.refs_0_
  48.3 0.0 collective-permute-done.3.refs_1_
  48.3 0.0 copy-done.1
  48.3 0.0 copy-done.2
  48.3 0.0 copy-done.4
  48.4 0.0 copy-done.6
  48.4 0.0 copy-done.8
  48.4 0.0 copy-done.9
  48.4 0.0 copy-done.11
  48.4 7.7 %moved_last.1 = f32[4,3,8,64,256]{4,3,2,1,0:T(8,128)} custom-call(s32[1]{0:T(128)} %bitcast.1.odd_ref, s32[4]{0:T(128)S(1)} %copy-done.8, f32[8]{0:T(128)S(1)} %copy-done.9, f32[4]{0:T(128)S(1)} %copy-done.11, f32[8,64,256]{2,1,0:T(8,128)S(1)} %copy-done, f32[1,64,256]{2,1,0:T(8,128)S(1)} %copy-done.4, ...), custom_call_target="tpu_custom_call", output_to_operand_aliasing={{}: (12, {})} | custom-call | flops 6291456 | bytes 8388608 | tf_op jit(solution)/shard_map/moved_last/pallas_call | solution.py:310
  56.1 0.0 all-to-all-done.1
  56.1 1.9 %copy.12 = f32[8,64,256]{2,1,0:T(8,128)} copy(f32[8,64,256]{2,1,0:T(8,128)} %all-to-all-done.1) | data formatting | bytes 1048576
Async XLA Ops:
  1.5 8.8 %collective-permute-start = (f32[1,64,256]{2,1,0:T(8,128)S(1)}, f32[1,64,256]{2,1,0:T(8,128)S(1)}, u32[]{:S(2)}, u32[]{:S(2)}) collective-permute-start(f32[1,64,256]{2,1,0:T(8,128)S(1)} %get-tuple-element.17), channel_id=1, source_target_pairs={{0,1},{1,0},{2,3},{3,2},{4,5},{5,4},{6,7},{7,6},{8,9},{9,8},{10,11... | collective-permute-start | bytes 196616 | tf_op jit(solution)/shard_map/ppermute | solution.py:343
  1.6 10.6 %collective-permute-start.1 = (f32[1,64,256]{2,1,0:T(8,128)S(1)}, f32[1,64,256]{2,1,0:T(8,128)S(1)}, u32[]{:S(2)}, u32[]{:S(2)}) collective-permute-start(f32[1,64,256]{2,1,0:T(8,128)S(1)} %get-tuple-element.16), channel_id=1, source_target_pairs={{1,2},{3,4},{5,6},{7,8},{9,10},{11,12},{13,14},{15,16},{17,18},{19... | collective-permute-start | bytes 196616 | tf_op jit(solution)/shard_map/ppermute | solution.py:344
  10.3 1.9 %copy-start.3 = (f32[1,64,256]{2,1,0:T(8,128)}, f32[1,64,256]{2,1,0:T(8,128)S(1)}, u32[]{:S(2)}) copy-start(f32[1,64,256]{2,1,0:T(8,128)S(1)} %collective-permute-done.ti_hbm) | copy-start | bytes 196612
  12.3 0.6 %copy-start.5 = (f32[1,64,256]{2,1,0:T(8,128)}, f32[1,64,256]{2,1,0:T(8,128)S(1)}, u32[]{:S(2)}) copy-start(f32[1,64,256]{2,1,0:T(8,128)S(1)} %collective-permute-done.1.to_hbm) | copy-start | bytes 196612
  19.7 21.4 %copy-start = (f32[8,64,256]{2,1,0:T(8,128)S(1)}, f32[8,64,256]{2,1,0:T(8,128)}, u32[]{:S(2)}) copy-start(f32[8,64,256]{2,1,0:T(8,128)} %t_hbm.5) | copy-start | bytes 1572868
  19.7 28.7 %copy-start.1 = (bf16[4,8,64,256]{3,2,1,0:T(8,128)(2,1)S(1)}, bf16[4,8,64,256]{3,2,1,0:T(8,128)(2,1)}, u32[]{:S(2)}) copy-start(bf16[4,8,64,256]{3,2,1,0:T(8,128)(2,1)} %im_hbm.5) | copy-start | bytes 3145732
  19.7 28.7 %copy-start.2 = (s32[8,64,256]{2,1,0:T(8,128)S(1)}, s32[8,64,256]{2,1,0:T(8,128)}, u32[]{:S(2)}) copy-start(s32[8,64,256]{2,1,0:T(8,128)} %lab_hbm.3) | copy-start | bytes 1572868
  19.7 28.7 %copy-start.4 = (f32[1,64,256]{2,1,0:T(8,128)S(1)}, f32[1,64,256]{2,1,0:T(8,128)}, u32[]{:S(2)}) copy-start(f32[1,64,256]{2,1,0:T(8,128)} %copy-done.3) | copy-start | bytes 196612
  19.7 28.7 %copy-start.6 = (f32[1,64,256]{2,1,0:T(8,128)S(1)}, f32[1,64,256]{2,1,0:T(8,128)}, u32[]{:S(2)}) copy-start(f32[1,64,256]{2,1,0:T(8,128)} %copy-done.5) | copy-start | bytes 196612
  19.7 28.7 %copy-start.8 = (s32[4]{0:T(128)S(1)}, s32[4]{0:T(128)}, u32[]{:S(2)}) copy-start(s32[4]{0:T(128)} %cohort.5) | copy-start | bytes 52
  19.7 28.6 %copy-start.9 = (f32[8]{0:T(128)S(1)}, f32[8]{0:T(128)}, u32[]{:S(2)}) copy-start(f32[8]{0:T(128)} %gain.5) | copy-start | bytes 100
  19.7 28.6 %copy-start.11 = (f32[4]{0:T(128)S(1)}, f32[4]{0:T(128)}, u32[]{:S(2)}) copy-start(f32[4]{0:T(128)} %stiff.3) | copy-start | bytes 52
  19.8 21.2 %all-to-all-start = ((f32[8,64,256]{2,1,0:T(8,128)}), f32[8,64,256]{2,1,0:T(8,128)S(1)}, u32[]{:S(2)}, u32[]{:S(2)}) async-start(f32[8,64,256]{2,1,0:T(8,128)} %get-tuple-element.9.refs_0_), calls=%async_computation | async-start | bytes 1048576 | tf_op jit(solution)/shard_map/all_to_all | solution.py:349
  25.8 22.5 %collective-permute-start.2 = (f32[4,3,1,64,256]{4,3,2,1,0:T(8,128)}, f32[4,3,1,64,256]{4,3,2,1,0:T(8,128)S(1)}, u32[]{:S(2)}, u32[]{:S(2)}) collective-permute-start(f32[4,3,1,64,256]{4,3,2,1,0:T(8,128)} %get-tuple-element.12), channel_id=1, source_target_pairs={{0,1},{1,0},{2,3},{3,2},{4,5},{5,4},{6,7},{7,6},{8,9},{9,8},{10,11... | collective-permute-start | bytes 2359304 | tf_op jit(solution)/shard_map/ppermute | solution.py:347
  25.8 22.5 %collective-permute-start.3 = (f32[4,3,1,64,256]{4,3,2,1,0:T(8,128)}, f32[4,3,1,64,256]{4,3,2,1,0:T(8,128)}, u32[]{:S(2)}, u32[]{:S(2)}) collective-permute-start(f32[4,3,1,64,256]{4,3,2,1,0:T(8,128)} %get-tuple-element.13), channel_id=1, source_target_pairs={{1,2},{3,4},{5,6},{7,8},{9,10},{11,12},{13,14},{15,16},{17,18},{19... | collective-permute-start | bytes 2359304 | tf_op jit(solution)/shard_map/ppermute | solution.py:348
  41.0 0.7 %copy-start.10 = (f32[8,128]{1,0:T(8,128)S(1)}, f32[8,128]{1,0:T(8,128)}, u32[]{:S(2)}) copy-start(f32[8,128]{1,0:T(8,128)} %get-tuple-element.10.refs_3_) | copy-start | bytes 12292
  41.8 0.8 %copy-start.7 = (f32[8,64,256]{2,1,0:T(8,128)}, f32[8,64,256]{2,1,0:T(8,128)S(1)}, u32[]{:S(2)}) copy-start(f32[8,64,256]{2,1,0:T(8,128)S(1)} %get-tuple-element.11) | copy-start | bytes 1572868
  42.6 13.5 %all-to-all-start.1 = ((f32[8,64,256]{2,1,0:T(8,128)}), f32[8,64,256]{2,1,0:T(8,128)}, u32[]{:S(2)}, u32[]{:S(2)}) async-start(f32[8,64,256]{2,1,0:T(8,128)} %copy-done.7), calls=%async_computation.1 | async-start | bytes 1048576 | tf_op jit(solution)/shard_map/all_to_all | solution.py:355

commit v5 on v2

--- a/solution.py
+++ b/solution.py
@@ -8,6 +8,7 @@
 velocity_step = 0.05
 template_step = 0.5
 ROWS = 16
+AHEAD = 2
 MIB = 1 << 20
 
 
@@ -85,14 +86,19 @@
     ]
     for copy in template:
         copy.start()
-    for s in range(subjects):
-        images[s].start()
-        for copy in fields[s]:
-            copy.start()
+    pair = 2 if subjects % 2 == 0 else 1
+
+    def begin(members):
+        for s in members:
+            images[s].start()
+            for copy in fields[s]:
+                copy.start()
+
+    begin(range(pair))
     for copy in template:
         copy.wait()
+    begin(range(pair, subjects))
     fill_slopes(t_ref, s_ref)
-    pair = 2 if subjects % 2 == 0 else 1
     for low in range(0, subjects, pair):
         members = range(low, low + pair)
         for s in members:
@@ -168,7 +174,8 @@
 
     for copy in template:
         copy.start()
-    for s in range(subjects):
+    ahead = min(AHEAD, subjects)
+    for s in range(ahead):
         for copy in arrivals(s):
             copy.start()
     for copy in template:
@@ -187,6 +194,12 @@
     def _(s):
         for copy in arrivals(s):
             copy.wait()
+
+        @pl.when(s + ahead < subjects)
+        def _():
+            for copy in arrivals(s + ahead):
+                copy.start()
+
         level = gain[cohort[s]]
 
         def plane(z):

time: 56.8 us -> 55.5 us (0.977)
  Pallas kernels: 20.2 us -> 18.9 us
    pallas_call x1, Pallas kernels: 12.5 us -> 11.3 us  [moved(): pl.pallas_call(move_kernel, out_shape=jax.ShapeDtypeStruct(velocity.shape...]
  transfers between devices with their start and end apart: 6 -> 6, of which waited for: 3 -> 3; matrix products, arithmetic and copies ran while one was open for 0% -> 0% of each run, Pallas kernels for 24% -> 22%
where the time goes in v5:
time: 55.5 us; the launch traced here: 55.2 us
  starting transfers between devices  25.2 us (45%)
  Pallas kernels  18.9 us (34%)
  waiting for transfers between devices  6.95 us (13%)
  local copies, waits for them, and re-layouts  3.32 us (6%)
  between operations  0.73 us (1%)
    pallas_call x1, Pallas kernels, moved(): pl.pallas_call(move_kernel, out_shape=jax.ShapeDtypeStruct(velocity.shape...  11.3 us
    ppermute x1, starting transfers between devices, local(): lax.ppermute(lax.dynamic_slice_in_dim(template, depth - 1 - facing, 1, 0)...  8.05 us
    ppermute x1, starting transfers between devices, local(): v_outer = lax.ppermute(outer, 'slab', across)  6.68 us
    pallas_call x1, Pallas kernels, partial_sums(): pl.pallas_call(partial_kernel, out_shape=[jax.ShapeDtypeStruct(template.s...  6.67 us
    all_to_all x1, starting transfers between devices, local(): parts = lax.all_to_all(part, 'grp', 0, 0, tiled=True)  5.94 us
    all_to_all x1, starting transfers between devices, local(): new_template = lax.all_to_all(shares, 'grp', 0, 0, tiled=True)  4.48 us
    ppermute x1, waiting for transfers between devices, local(): v_outer = lax.ppermute(outer, 'slab', across)  3.47 us
    unnamed x11, local copies, waits for them, and re-layouts  2.38 us
  transfers between devices with their start and end apart: 6, of which 3 were waited for; matrix products, arithmetic and copies ran while one was open for 0% of the time, Pallas kernels for 22%

profile of v5, /device:TPU:6, one launch (start us, length us, event | category | flops | bytes accessed | tf_op | source)
XLA Modules:
  0.0 55.2 jit_solution(6153235138934270131)
XLA Ops:
  0.6 0.0 copy-start
  0.7 0.9 %constant_dynamic-slice_fusion = (f32[1,64,256]{2,1,0:T(8,128)S(1)}, f32[1,64,256]{2,1,0:T(8,128)S(1)}) fusion(f32[8,64,256]{2,1,0:T(8,128)} %t_hbm.3, s32[]{:T(128)S(6)} %select_n.17, s32[]{:T(128)S(6)} %select_n.16), kind=kLoop, calls=%fused_computation | loop fusion | bytes 262152 | tf_op jit(solution)/shard_map/dynamic_slice | solution.py:316
  1.6 8.0 %collective-permute-start.1 = (f32[1,64,256]{2,1,0:T(8,128)S(1)}, f32[1,64,256]{2,1,0:T(8,128)S(1)}, u32[]{:S(2)}, u32[]{:S(2)}) collective-permute-start(f32[1,64,256]{2,1,0:T(8,128)S(1)} %get-tuple-element.8), channel_id=1, source_target_pairs={{1,2},{3,4},{5,6},{7,8},{9,10},{11,12},{13,14},{15,16},{17,18},{19... | collective-permute-start | bytes 196616 | tf_op jit(solution)/shard_map/ppermute | solution.py:316
  9.7 0.1 collective-permute-start
  9.8 1.8 %collective-permute-done.1.to_hbm = f32[1,64,256]{2,1,0:T(8,128)S(1)} collective-permute-done((f32[1,64,256]{2,1,0:T(8,128)S(1)}, f32[1,64,256]{2,1,0:T(8,128)S(1)}, u32[]{:S(2)}, u32[]{:S(2)}) %collective-permute-start.1) | collective-permute-done | bytes 65568 | tf_op jit(solution)/shard_map/ppermute | solution.py:316
  11.6 0.0 copy-start.3
  11.6 0.0 collective-permute-done.ti_hbm
  11.6 0.0 copy-start.4
  11.6 0.6 %copy-done.3 = f32[1,64,256]{2,1,0:T(8,128)} copy-done((f32[1,64,256]{2,1,0:T(8,128)}, f32[1,64,256]{2,1,0:T(8,128)S(1)}, u32[]{:S(2)}) %copy-start.3) | copy-done | bytes 65560
  12.2 0.0 copy-done.4
  12.2 6.7 %partial_sums.1 = (f32[8,64,256]{2,1,0:T(8,128)}, f32[4,3,1,64,256]{4,3,2,1,0:T(8,128)}, f32[4,3,1,64,256]{4,3,2,1,0:T(8,128)}) custom-call(s32[1]{0:T(128)} %bitcast.1.odd_ref, s32[4]{0:T(128)} %cohort.3, f32[8]{0:T(128)} %gain.3, f32[8,64,256]{2,1,0:T(8,128)} %t_hbm.3, f32[1,64,256]{2,1,0:T(8,128)} %copy-done.4, f32[1,64,256]{2,1,0:T(8,128)} %copy-done.3, ...), custom_call_target="tpu_custom_call" | custom-call | flops 6291456 | bytes 10485760 | tf_op jit(solution)/shard_map/partial_sums/pallas_call | solution.py:248
  18.9 5.9 %all-to-all-start = ((f32[8,64,256]{2,1,0:T(8,128)}), f32[8,64,256]{2,1,0:T(8,128)S(1)}, u32[]{:S(2)}, u32[]{:S(2)}) async-start(f32[8,64,256]{2,1,0:T(8,128)} %get-tuple-element.5), calls=%async_computation | async-start | bytes 1048576 | tf_op jit(solution)/shard_map/all_to_all | solution.py:321
  24.9 0.0 collective-permute-start.2
  24.9 6.7 %collective-permute-start.3 = (f32[4,3,1,64,256]{4,3,2,1,0:T(8,128)}, f32[4,3,1,64,256]{4,3,2,1,0:T(8,128)S(1)}, u32[]{:S(2)}, u32[]{:S(2)}) collective-permute-start(f32[4,3,1,64,256]{4,3,2,1,0:T(8,128)} %get-tuple-element.7), channel_id=1, source_target_pairs={{1,2},{3,4},{5,6},{7,8},{9,10},{11,12},{13,14},{15,16},{17,18},{19... | collective-permute-start | bytes 2359304 | tf_op jit(solution)/shard_map/ppermute | solution.py:320
  31.6 1.6 %all-to-all-done.refs_2_ = f32[8,64,256]{2,1,0:T(8,128)S(1)} async-done(((f32[8,64,256]{2,1,0:T(8,128)}), f32[8,64,256]{2,1,0:T(8,128)S(1)}, u32[]{:S(2)}, u32[]{:S(2)}) %all-to-all-start) | async-done | bytes 524320 | tf_op jit(solution)/shard_map/all_to_all | solution.py:321
  33.2 0.0 copy-done
  33.2 0.9 %share_update.1 = f32[8,64,256]{2,1,0:T(8,128)} custom-call(s32[1]{0:T(128)} %bitcast.refs_0_, f32[8,64,256]{2,1,0:T(8,128)S(1)} %copy-done, f32[8,64,256]{2,1,0:T(8,128)S(1)} %all-to-all-done.refs_2_), custom_call_target="tpu_custom_call" | custom-call | flops 131072 | bytes 2097152 | tf_op jit(solution)/shard_map/share_update/pallas_call | solution.py:267
  34.1 4.5 %all-to-all-start.1 = ((f32[8,64,256]{2,1,0:T(8,128)}), f32[8,64,256]{2,1,0:T(8,128)S(1)}, u32[]{:S(2)}, u32[]{:S(2)}) async-start(f32[8,64,256]{2,1,0:T(8,128)} %share_update.1), calls=%async_computation.1 | async-start | bytes 1048576 | tf_op jit(solution)/shard_map/all_to_all | solution.py:323
  38.6 0.0 collective-permute-done.2.vi_hbm
  38.6 0.0 copy-start.1
  38.6 3.5 %collective-permute-done.3.vo_hbm = f32[4,3,1,64,256]{4,3,2,1,0:T(8,128)S(1)} collective-permute-done((f32[4,3,1,64,256]{4,3,2,1,0:T(8,128)}, f32[4,3,1,64,256]{4,3,2,1,0:T(8,128)S(1)}, u32[]{:S(2)}, u32[]{:S(2)}) %collective-permute-start.3) | collective-permute-done | bytes 786464 | tf_op jit(solution)/shard_map/ppermute | solution.py:320
  42.1 0.0 copy-done.1
  42.1 0.0 copy-start.2
  42.1 0.9 %copy-done.2 = f32[4,3,1,64,256]{4,3,2,1,0:T(8,128)} copy-done((f32[4,3,1,64,256]{4,3,2,1,0:T(8,128)}, f32[4,3,1,64,256]{4,3,2,1,0:T(8,128)S(1)}, u32[]{:S(2)}) %copy-start.2) | copy-done | bytes 786456
  43.0 11.3 %moved.1 = f32[4,3,8,64,256]{4,3,2,1,0:T(8,128)} custom-call(s32[1]{0:T(128)} %bitcast.1.odd_ref, s32[4]{0:T(128)} %cohort.3, f32[8]{0:T(128)} %gain.3, f32[4]{0:T(128)} %stiff.1, f32[8,64,256]{2,1,0:T(8,128)} %t_hbm.3, f32[1,64,256]{2,1,0:T(8,128)} %copy-done.4, f32[1,64,256]{2,1,0:T(8,128)} %copy-done.3, s32[8,64,256]{2,1,0:T(8,128)} %lab_hbm.1, ...), custom_call_target="tpu_custom_call" | custom-call | flops 12582912 | bytes 16777216 | tf_op jit(solution)/shard_map/moved/pallas_call | solution.py:282
  54.4 0.0 all-to-all-done.1
  54.4 0.8 %copy.10 = f32[8,64,256]{2,1,0:T(8,128)} copy(f32[8,64,256]{2,1,0:T(8,128)S(1)} %all-to-all-done.1) | data formatting | bytes 1048576
Async XLA Ops:
  0.6 32.6 %copy-start = (f32[8,64,256]{2,1,0:T(8,128)S(1)}, f32[8,64,256]{2,1,0:T(8,128)}, u32[]{:S(2)}) copy-start(f32[8,64,256]{2,1,0:T(8,128)} %t_hbm.3) | copy-start | bytes 1572868
  1.6 10.0 %collective-permute-start.1 = (f32[1,64,256]{2,1,0:T(8,128)S(1)}, f32[1,64,256]{2,1,0:T(8,128)S(1)}, u32[]{:S(2)}, u32[]{:S(2)}) collective-permute-start(f32[1,64,256]{2,1,0:T(8,128)S(1)} %get-tuple-element.8), channel_id=1, source_target_pairs={{1,2},{3,4},{5,6},{7,8},{9,10},{11,12},{13,14},{15,16},{17,18},{19... | collective-permute-start | bytes 196616 | tf_op jit(solution)/shard_map/ppermute | solution.py:316
  9.7 1.9 %collective-permute-start = (f32[1,64,256]{2,1,0:T(8,128)S(1)}, f32[1,64,256]{2,1,0:T(8,128)S(1)}, u32[]{:S(2)}, u32[]{:S(2)}) collective-permute-start(f32[1,64,256]{2,1,0:T(8,128)S(1)} %get-tuple-element.9), channel_id=1, source_target_pairs={{0,1},{1,0},{2,3},{3,2},{4,5},{5,4},{6,7},{7,6},{8,9},{9,8},{10,11... | collective-permute-start | bytes 196616 | tf_op jit(solution)/shard_map/ppermute | solution.py:315
  11.6 0.6 %copy-start.3 = (f32[1,64,256]{2,1,0:T(8,128)}, f32[1,64,256]{2,1,0:T(8,128)S(1)}, u32[]{:S(2)}) copy-start(f32[1,64,256]{2,1,0:T(8,128)S(1)} %collective-permute-done.1.to_hbm) | copy-start | bytes 196612
  11.6 0.6 %copy-start.4 = (f32[1,64,256]{2,1,0:T(8,128)}, f32[1,64,256]{2,1,0:T(8,128)S(1)}, u32[]{:S(2)}) copy-start(f32[1,64,256]{2,1,0:T(8,128)S(1)} %collective-permute-done.ti_hbm) | copy-start | bytes 196612
  18.9 14.3 %all-to-all-start = ((f32[8,64,256]{2,1,0:T(8,128)}), f32[8,64,256]{2,1,0:T(8,128)S(1)}, u32[]{:S(2)}, u32[]{:S(2)}) async-start(f32[8,64,256]{2,1,0:T(8,128)} %get-tuple-element.5), calls=%async_computation | async-start | bytes 1048576 | tf_op jit(solution)/shard_map/all_to_all | solution.py:321
  24.9 13.7 %collective-permute-start.2 = (f32[4,3,1,64,256]{4,3,2,1,0:T(8,128)}, f32[4,3,1,64,256]{4,3,2,1,0:T(8,128)S(1)}, u32[]{:S(2)}, u32[]{:S(2)}) collective-permute-start(f32[4,3,1,64,256]{4,3,2,1,0:T(8,128)} %get-tuple-element.6), channel_id=1, source_target_pairs={{0,1},{1,0},{2,3},{3,2},{4,5},{5,4},{6,7},{7,6},{8,9},{9,8},{10,11... | collective-permute-start | bytes 2359304 | tf_op jit(solution)/shard_map/ppermute | solution.py:319
  24.9 17.2 %collective-permute-start.3 = (f32[4,3,1,64,256]{4,3,2,1,0:T(8,128)}, f32[4,3,1,64,256]{4,3,2,1,0:T(8,128)S(1)}, u32[]{:S(2)}, u32[]{:S(2)}) collective-permute-start(f32[4,3,1,64,256]{4,3,2,1,0:T(8,128)} %get-tuple-element.7), channel_id=1, source_target_pairs={{1,2},{3,4},{5,6},{7,8},{9,10},{11,12},{13,14},{15,16},{17,18},{19... | collective-permute-start | bytes 2359304 | tf_op jit(solution)/shard_map/ppermute | solution.py:320
  34.1 20.2 %all-to-all-start.1 = ((f32[8,64,256]{2,1,0:T(8,128)}), f32[8,64,256]{2,1,0:T(8,128)S(1)}, u32[]{:S(2)}, u32[]{:S(2)}) async-start(f32[8,64,256]{2,1,0:T(8,128)} %share_update.1), calls=%async_computation.1 | async-start | bytes 1048576 | tf_op jit(solution)/shard_map/all_to_all | solution.py:323
  38.6 3.5 %copy-start.1 = (f32[4,3,1,64,256]{4,3,2,1,0:T(8,128)}, f32[4,3,1,64,256]{4,3,2,1,0:T(8,128)S(1)}, u32[]{:S(2)}) copy-start(f32[4,3,1,64,256]{4,3,2,1,0:T(8,128)S(1)} %collective-permute-done.2.vi_hbm) | copy-start | bytes 2359300
  42.1 0.9 %copy-start.2 = (f32[4,3,1,64,256]{4,3,2,1,0:T(8,128)}, f32[4,3,1,64,256]{4,3,2,1,0:T(8,128)S(1)}, u32[]{:S(2)}) copy-start(f32[4,3,1,64,256]{4,3,2,1,0:T(8,128)S(1)} %collective-permute-done.3.vo_hbm) | copy-start | bytes 2359300

commit v6 on v3

--- a/solution.py
+++ b/solution.py
@@ -8,6 +8,7 @@
 velocity_step = 0.05
 template_step = 0.5
 ROWS = 16
+AHEAD = 2
 MIB = 1 << 20
 
 
@@ -110,7 +111,8 @@
 
     for copy in template:
         copy.start()
-    for s in range(subjects):
+    ahead = min(AHEAD, subjects)
+    for s in range(ahead):
         for copy in arrivals(s):
             copy.start()
     sum_ref[...] = jnp.zeros_like(sum_ref)
@@ -136,6 +138,12 @@
             copy.wait()
         for copy in edges(s):
             copy.start()
+
+        @pl.when(s + ahead < subjects)
+        def _():
+            for copy in arrivals(s + ahead):
+                copy.start()
+
         level = gain[cohort[s]]
 
         def plane(z):

time: 57.2 us -> 56.2 us (0.983)
  Pallas kernels: 17 us -> 16 us
    pallas_call x1, Pallas kernels: 13.1 us -> 12 us  [moved(): pl.pallas_call(move_kernel, out_shape=[jax.ShapeDtypeStruct(template.shap...]
where the time goes in v6:
time: 56.2 us; the launch traced here: 55.8 us
  waiting for transfers between devices  18.6 us (33%)
  starting transfers between devices  18 us (32%)
  Pallas kernels  16 us (28%)
  local copies, waits for them, and re-layouts  2.42 us (4%)
  between operations  0.76 us (1%)
    pallas_call x1, Pallas kernels, moved(): pl.pallas_call(move_kernel, out_shape=[jax.ShapeDtypeStruct(template.shap...  12 us
    all_to_all x1, waiting for transfers between devices, local(): new_template = lax.all_to_all(shares, 'grp', 0, 0, tiled=True)  11.6 us
    all_to_all x1, waiting for transfers between devices, local(): parts = lax.all_to_all(part, 'grp', 0, 0, tiled=True)  5.2 us
    all_to_all x1, starting transfers between devices, local(): parts = lax.all_to_all(part, 'grp', 0, 0, tiled=True)  5.13 us
    ppermute x1, starting transfers between devices, local(): lax.ppermute(lax.dynamic_slice_in_dim(template, depth - 1 - facing, 1, 0)...  4.94 us
    all_to_all x1, starting transfers between devices, local(): new_template = lax.all_to_all(shares, 'grp', 0, 0, tiled=True)  3.94 us
    ppermute x1, starting transfers between devices, local(): v_outer = lax.ppermute(outer, 'slab', across)  3.92 us
    pallas_call x1, Pallas kernels, edges_added(): pl.pallas_call(edge_kernel, out_shape=jax.ShapeDtypeStruct(velocity.shape...  3.07 us
  transfers between devices with their start and end apart: 6, of which 3 were waited for; matrix products, arithmetic and copies ran while one was open for 0% of the time, Pallas kernels for 7%

profile of v6, /device:TPU:1, one launch (start us, length us, event | category | flops | bytes accessed | tf_op | source)
XLA Modules:
  0.0 55.8 jit_solution(15909111502881539329)
XLA Ops:
  0.6 0.0 copy-start
  0.6 0.0 copy-start.2
  0.7 0.0 copy-start.1
  0.7 1.0 %constant_dynamic-slice_fusion = (f32[1,64,256]{2,1,0:T(8,128)S(1)}, f32[1,64,256]{2,1,0:T(8,128)S(1)}) fusion(f32[8,64,256]{2,1,0:T(8,128)} %refs_1_.1, s32[]{:T(128)S(6)} %select_n.17, s32[]{:T(128)S(6)} %select_n.16), kind=kLoop, calls=%fused_computation | loop fusion | bytes 262152 | tf_op jit(solution)/shard_map/dynamic_slice | solution.py:307
  1.6 4.9 %collective-permute-start.1 = (f32[1,64,256]{2,1,0:T(8,128)S(1)}, f32[1,64,256]{2,1,0:T(8,128)S(1)}, u32[]{:S(2)}, u32[]{:S(2)}) collective-permute-start(f32[1,64,256]{2,1,0:T(8,128)S(1)} %get-tuple-element.10), channel_id=1, source_target_pairs={{1,2},{3,4},{5,6},{7,8},{9,10},{11,12},{13,14},{15,16},{17,18},{19... | collective-permute-start | bytes 196616 | tf_op jit(solution)/shard_map/ppermute | solution.py:307
  6.6 0.1 collective-permute-start
  6.7 1.8 %collective-permute-done.1.to_hbm = f32[1,64,256]{2,1,0:T(8,128)S(1)} collective-permute-done((f32[1,64,256]{2,1,0:T(8,128)S(1)}, f32[1,64,256]{2,1,0:T(8,128)S(1)}, u32[]{:S(2)}, u32[]{:S(2)}) %collective-permute-start.1) | collective-permute-done | bytes 65568 | tf_op jit(solution)/shard_map/ppermute | solution.py:307
  8.5 0.0 copy-start.3
  8.5 0.0 collective-permute-done.ti_hbm
  8.5 0.0 copy-start.4
  8.5 0.6 %copy-done.3 = f32[1,64,256]{2,1,0:T(8,128)} copy-done((f32[1,64,256]{2,1,0:T(8,128)}, f32[1,64,256]{2,1,0:T(8,128)S(1)}, u32[]{:S(2)}) %copy-start.3) | copy-done | bytes 65560
  9.2 0.0 copy-done.4
  9.2 12.0 %moved.1 = (f32[8,64,256]{2,1,0:T(8,128)}, f32[4,3,1,64,256]{4,3,2,1,0:T(8,128)}, f32[4,3,1,64,256]{4,3,2,1,0:T(8,128)}, f32[4,3,8,64,256]{4,3,2,1,0:T(8,128)}) custom-call(s32[1]{0:T(128)} %bitcast.1.odd_ref, s32[4]{0:T(128)} %cohort.1, f32[8]{0:T(128)} %gain.1, f32[4]{0:T(128)} %stiff.3, f32[8,64,256]{2,1,0:T(8,128)} %refs_1_.1, f32[1,64,256]{2,1,0:T(8,128)} %copy-done.4, ...), custom_call_target="tpu_custom_call" | custom-call | flops 12582912 | bytes 16777216 | tf_op jit(solution)/shard_map/moved/pallas_call | solution.py:252
  21.2 5.1 %all-to-all-start = ((f32[8,64,256]{2,1,0:T(8,128)}), f32[8,64,256]{2,1,0:T(8,128)S(1)}, u32[]{:S(2)}, u32[]{:S(2)}) async-start(f32[8,64,256]{2,1,0:T(8,128)} %get-tuple-element.6), calls=%async_computation | async-start | bytes 1048576 | tf_op jit(solution)/shard_map/all_to_all | solution.py:314
  26.3 0.0 collective-permute-start.2
  26.3 3.9 %collective-permute-start.3 = (f32[4,3,1,64,256]{4,3,2,1,0:T(8,128)}, f32[4,3,1,64,256]{4,3,2,1,0:T(8,128)S(1)}, u32[]{:S(2)}, u32[]{:S(2)}) collective-permute-start(f32[4,3,1,64,256]{4,3,2,1,0:T(8,128)} %get-tuple-element.8), channel_id=1, source_target_pairs={{1,2},{3,4},{5,6},{7,8},{9,10},{11,12},{13,14},{15,16},{17,18},{19... | collective-permute-start | bytes 2359304 | tf_op jit(solution)/shard_map/ppermute | solution.py:313
  30.3 5.2 %all-to-all-done.refs_2_ = f32[8,64,256]{2,1,0:T(8,128)S(1)} async-done(((f32[8,64,256]{2,1,0:T(8,128)}), f32[8,64,256]{2,1,0:T(8,128)S(1)}, u32[]{:S(2)}, u32[]{:S(2)}) %all-to-all-start) | async-done | bytes 524320 | tf_op jit(solution)/shard_map/all_to_all | solution.py:314
  35.5 0.0 copy-done
  35.5 0.9 %share_update.1 = f32[8,64,256]{2,1,0:T(8,128)} custom-call(s32[1]{0:T(128)} %bitcast.refs_0_, f32[8,64,256]{2,1,0:T(8,128)S(1)} %copy-done, f32[8,64,256]{2,1,0:T(8,128)S(1)} %all-to-all-done.refs_2_), custom_call_target="tpu_custom_call" | custom-call | flops 131072 | bytes 2097152 | tf_op jit(solution)/shard_map/share_update/pallas_call | solution.py:235
  36.4 3.9 %all-to-all-start.1 = ((f32[8,64,256]{2,1,0:T(8,128)}), f32[8,64,256]{2,1,0:T(8,128)S(1)}, u32[]{:S(2)}, u32[]{:S(2)}) async-start(f32[8,64,256]{2,1,0:T(8,128)} %share_update.1), calls=%async_computation.1 | async-start | bytes 1048576 | tf_op jit(solution)/shard_map/all_to_all | solution.py:316
  40.3 0.0 collective-permute-done.2.vi_ref
  40.3 0.0 collective-permute-done.3.vo_ref
  40.4 0.0 copy-done.2
  40.4 0.0 copy-done.1
  40.4 3.1 %edges_added.1 = f32[4,3,8,64,256]{4,3,2,1,0:T(8,128)} custom-call(s32[1]{0:T(128)} %bitcast.1.odd_ref, f32[4]{0:T(128)S(1)} %copy-done.2, s32[8,64,256]{2,1,0:T(8,128)S(1)} %copy-done.1, f32[4,3,1,64,256]{4,3,2,1,0:T(8,128)S(1)} %collective-permute-done.2.vi_ref, ...), custom_call_target="tpu_custom_call", output_to_operand_aliasing={{}: (5, {})} | custom-call | flops 196608 | bytes 6291456 | tf_op jit(solution)/shard_map/edges_added/pallas_call | solution.py:277
  43.4 11.6 %all-to-all-done.1 = f32[8,64,256]{2,1,0:T(8,128)S(1)} async-done(((f32[8,64,256]{2,1,0:T(8,128)}), f32[8,64,256]{2,1,0:T(8,128)S(1)}, u32[]{:S(2)}, u32[]{:S(2)}) %all-to-all-start.1) | async-done | bytes 524320 | tf_op jit(solution)/shard_map/all_to_all | solution.py:316
  55.0 0.8 %copy.12 = f32[8,64,256]{2,1,0:T(8,128)} copy(f32[8,64,256]{2,1,0:T(8,128)S(1)} %all-to-all-done.1) | data formatting | bytes 1048576
Async XLA Ops:
  0.6 34.8 %copy-start = (f32[8,64,256]{2,1,0:T(8,128)S(1)}, f32[8,64,256]{2,1,0:T(8,128)}, u32[]{:S(2)}) copy-start(f32[8,64,256]{2,1,0:T(8,128)} %refs_1_.1) | copy-start | bytes 1572868
  0.6 39.7 %copy-start.2 = (f32[4]{0:T(128)S(1)}, f32[4]{0:T(128)}, u32[]{:S(2)}) copy-start(f32[4]{0:T(128)} %stiff.3) | copy-start | bytes 52
  0.7 39.7 %copy-start.1 = (s32[8,64,256]{2,1,0:T(8,128)S(1)}, s32[8,64,256]{2,1,0:T(8,128)}, u32[]{:S(2)}) copy-start(s32[8,64,256]{2,1,0:T(8,128)} %lab_hbm.3) | copy-start | bytes 1572868
  1.6 6.9 %collective-permute-start.1 = (f32[1,64,256]{2,1,0:T(8,128)S(1)}, f32[1,64,256]{2,1,0:T(8,128)S(1)}, u32[]{:S(2)}, u32[]{:S(2)}) collective-permute-start(f32[1,64,256]{2,1,0:T(8,128)S(1)} %get-tuple-element.10), channel_id=1, source_target_pairs={{1,2},{3,4},{5,6},{7,8},{9,10},{11,12},{13,14},{15,16},{17,18},{19... | collective-permute-start | bytes 196616 | tf_op jit(solution)/shard_map/ppermute | solution.py:307
  6.6 1.9 %collective-permute-start = (f32[1,64,256]{2,1,0:T(8,128)S(1)}, f32[1,64,256]{2,1,0:T(8,128)S(1)}, u32[]{:S(2)}, u32[]{:S(2)}) collective-permute-start(f32[1,64,256]{2,1,0:T(8,128)S(1)} %get-tuple-element.11), channel_id=1, source_target_pairs={{0,1},{1,0},{2,3},{3,2},{4,5},{5,4},{6,7},{7,6},{8,9},{9,8},{10,11... | collective-permute-start | bytes 196616 | tf_op jit(solution)/shard_map/ppermute | solution.py:306
  8.5 0.6 %copy-start.3 = (f32[1,64,256]{2,1,0:T(8,128)}, f32[1,64,256]{2,1,0:T(8,128)S(1)}, u32[]{:S(2)}) copy-start(f32[1,64,256]{2,1,0:T(8,128)S(1)} %collective-permute-done.1.to_hbm) | copy-start | bytes 196612
  8.5 0.6 %copy-start.4 = (f32[1,64,256]{2,1,0:T(8,128)}, f32[1,64,256]{2,1,0:T(8,128)S(1)}, u32[]{:S(2)}) copy-start(f32[1,64,256]{2,1,0:T(8,128)S(1)} %collective-permute-done.ti_hbm) | copy-start | bytes 196612
  21.2 14.3 %all-to-all-start = ((f32[8,64,256]{2,1,0:T(8,128)}), f32[8,64,256]{2,1,0:T(8,128)S(1)}, u32[]{:S(2)}, u32[]{:S(2)}) async-start(f32[8,64,256]{2,1,0:T(8,128)} %get-tuple-element.6), calls=%async_computation | async-start | bytes 1048576 | tf_op jit(solution)/shard_map/all_to_all | solution.py:314
  26.3 14.0 %collective-permute-start.2 = (f32[4,3,1,64,256]{4,3,2,1,0:T(8,128)}, f32[4,3,1,64,256]{4,3,2,1,0:T(8,128)S(1)}, u32[]{:S(2)}, u32[]{:S(2)}) collective-permute-start(f32[4,3,1,64,256]{4,3,2,1,0:T(8,128)} %get-tuple-element.7), channel_id=1, source_target_pairs={{0,1},{1,0},{2,3},{3,2},{4,5},{5,4},{6,7},{7,6},{8,9},{9,8},{10,11... | collective-permute-start | bytes 2359304 | tf_op jit(solution)/shard_map/ppermute | solution.py:312
  26.3 14.0 %collective-permute-start.3 = (f32[4,3,1,64,256]{4,3,2,1,0:T(8,128)}, f32[4,3,1,64,256]{4,3,2,1,0:T(8,128)S(1)}, u32[]{:S(2)}, u32[]{:S(2)}) collective-permute-start(f32[4,3,1,64,256]{4,3,2,1,0:T(8,128)} %get-tuple-element.8), channel_id=1, source_target_pairs={{1,2},{3,4},{5,6},{7,8},{9,10},{11,12},{13,14},{15,16},{17,18},{19... | collective-permute-start | bytes 2359304 | tf_op jit(solution)/shard_map/ppermute | solution.py:313
  36.4 18.6 %all-to-all-start.1 = ((f32[8,64,256]{2,1,0:T(8,128)}), f32[8,64,256]{2,1,0:T(8,128)S(1)}, u32[]{:S(2)}, u32[]{:S(2)}) async-start(f32[8,64,256]{2,1,0:T(8,128)} %share_update.1), calls=%async_computation.1 | async-start | bytes 1048576 | tf_op jit(solution)/shard_map/all_to_all | solution.py:316

commit v7 on v6

--- a/solution.py
+++ b/solution.py
@@ -52,17 +52,6 @@
                 also(z, rows)
 
 
-def template_copies(odd, t_hbm, ti_hbm, to_hbm, t_ref, sem):
-    depth = t_hbm.shape[0]
-    inner = jnp.where(odd == 1, 0, depth + 1)
-    outer = depth + 1 - inner
-    return [
-        pltpu.make_async_copy(t_hbm, t_ref.at[pl.ds(1, depth)], sem.at[0]),
-        pltpu.make_async_copy(ti_hbm, t_ref.at[pl.ds(inner, 1)], sem.at[1]),
-        pltpu.make_async_copy(to_hbm, t_ref.at[pl.ds(outer, 1)], sem.at[2]),
-    ]
-
-
 def share_kernel(place, scale, t_hbm, parts_ref, out_ref, own_ref, sem):
     groups, count, width = parts_ref.shape
     copy = pltpu.make_async_copy(t_hbm.at[place[0]], own_ref, sem)
@@ -70,24 +59,52 @@
     copy.wait()
     for j in range(count // ROWS):
         rows = pl.ds(j * ROWS, ROWS)
-        total = parts_ref[0, rows, :]
+        value = parts_ref[0, rows, :]
         for g in range(1, groups):
-            total = total + parts_ref[g, rows, :]
-        value = own_ref[rows, :] - scale * total
+            value = value + parts_ref[g, rows, :]
+        if j * ROWS < own_ref.shape[0]:
+            value = own_ref[rows, :] - scale * value
         for g in range(groups):
             out_ref[g, rows, :] = value
 
 
+def finish_kernel(odd_ref, scale, all_ref, ti_hbm, to_hbm, out_ref, halo_ref, sem):
+    depth, count, width = out_ref.shape
+    pieces = depth // 2
+    odd = odd_ref[0]
+    copies = [
+        pltpu.make_async_copy(far.at[far.shape[0] - 1], halo_ref.at[side], sem.at[side])
+        for side, far in enumerate((ti_hbm, to_hbm))
+    ]
+    for copy in copies:
+        copy.start()
+
+    @pl.loop(0, depth)
+    def _(z):
+        out_ref[z] = all_ref[z, pl.ds(0, count), :]
+
+    facing = jnp.where(odd == 1, 0, depth - 1)
+    for side, z in enumerate((facing, depth - 1 - facing)):
+        copies[side].wait()
+        factor = jnp.where(z == 0, 0.5 * scale, -0.5 * scale)
+        for q in range(pieces):
+            rows = pl.ds(q * (count // pieces), count // pieces)
+            speed = all_ref[jnp.where(z == 0, q, pieces + q), pl.ds(count, count // pieces), :]
+            out_ref[z, rows, :] = out_ref[z, rows, :] + factor * halo_ref[side, rows, :] * speed
+
+
 def move_kernel(
-    odd_ref, cohort, gain, stiff, t_hbm, ti_hbm, to_hbm, lab_hbm, im_hbm, v_hbm,
+    odd_ref, cohort, gain, stiff, t_hbm, lab_hbm, im_hbm, v_hbm,
     sum_ref, inner_hbm, outer_hbm, out_hbm,
     t_ref, lab_ref, im_ref, v_ref, new_ref, s_ref, k_ref,
-    t_sem, lab_sem, im_sem, v_sem, in_sem, far_sem, out_sem,
+    t_sem, lab_sem, im_sem, v_sem, in_sem, far_sem, out_sem, face_sem,
 ):
     subjects, depth, count, width = im_ref.shape
     odd = odd_ref[0]
-    template = template_copies(odd, t_hbm, ti_hbm, to_hbm, t_ref, t_sem)
-    template.append(pltpu.make_async_copy(lab_hbm, lab_ref, lab_sem))
+    template = [
+        pltpu.make_async_copy(t_hbm, t_ref.at[pl.ds(1, depth)], t_sem),
+        pltpu.make_async_copy(lab_hbm, lab_ref, lab_sem),
+    ]
     facing = jnp.where(odd == 1, 0, depth - 1)
     half = depth // 2
 
@@ -101,9 +118,14 @@
 
     def edges(s):
         return [
-            pltpu.make_async_copy(v_ref.at[s, :, pl.ds(1 + facing, 1)], inner_hbm.at[s], in_sem.at[s]),
-            pltpu.make_async_copy(v_ref.at[s, :, pl.ds(depth - facing, 1)], outer_hbm.at[s], far_sem.at[s]),
+            pltpu.make_async_copy(v_ref.at[s, :, 1 + facing], inner_hbm.at[pl.ds(3 * s, 3)], in_sem.at[s]),
+            pltpu.make_async_copy(v_ref.at[s, :, depth - facing], outer_hbm.at[pl.ds(3 * s, 3)], far_sem.at[s]),
         ]
+
+    faces = [
+        pltpu.make_async_copy(t_ref.at[1 + facing], inner_hbm.at[3 * subjects], face_sem.at[0]),
+        pltpu.make_async_copy(t_ref.at[depth - facing], outer_hbm.at[3 * subjects], face_sem.at[1]),
+    ]
 
     def departure(s, part):
         planes = pl.ds(part * half, half)
@@ -117,6 +139,8 @@
             copy.start()
     sum_ref[...] = jnp.zeros_like(sum_ref)
     outside = jnp.zeros((count, width), jnp.float32)
+    t_ref[0] = outside
+    t_ref[depth + 1] = outside
 
     @pl.loop(0, subjects)
     def _(s):
@@ -126,6 +150,8 @@
 
     for copy in template:
         copy.wait()
+    for copy in faces:
+        copy.start()
 
     def rate_of(z, rows):
         k_ref[z, rows, :] = rate_at(lab_ref[z, rows, :], stiff)
@@ -147,6 +173,7 @@
         level = gain[cohort[s]]
 
         def plane(z):
+            force = jnp.where((z == 0) | (z == depth - 1), 0.0, velocity_step)
             for j in range(count // ROWS):
                 start = j * ROWS
                 rows = pl.ds(start, ROWS)
@@ -157,7 +184,7 @@
                 for c in range(3):
                     value = value + slopes[c] * field[c]
                 sum_ref[z, rows, :] = sum_ref[z, rows, :] + value
-                value = velocity_step * value
+                value = force * value
                 for c in range(3):
                     here = field[c]
                     y_low, y_high = beside_y(
@@ -173,6 +200,17 @@
             pl.loop(part * half, (part + 1) * half)(plane)
             departure(s, part).start()
 
+    piece = sum_ref.shape[1] - count
+    for z, first in ((1, 0), (depth, depth // 2)):
+        for q in range(depth // 2):
+            rows = pl.ds(q * piece, piece)
+            speed = v_ref[0, 0, z, rows, :]
+            for s in range(1, subjects):
+                speed = speed + v_ref[s, 0, z, rows, :]
+            sum_ref[first + q, pl.ds(count, piece), :] = speed
+    for copy in faces:
+        copy.wait()
+
     @pl.loop(0, subjects)
     def _(s):
         for copy in edges(s):
@@ -189,39 +227,78 @@
 
 
 def edge_kernel(
-    odd_ref, stiff, lab_hbm, vi_ref, vo_ref, old_hbm, out_hbm, lab_ref, near_ref, far_ref,
-    lab_sem, near_sem, far_sem,
+    odd_ref, cohort, gain, stiff, t_hbm, lab_hbm, im_hbm, own_in_hbm, own_far_hbm, vi_ref, vo_ref, old_hbm, out_hbm,
+    t_ref, lab_ref, im_ref, own_ref, new_ref, s_ref, t_sem, lab_sem, im_sem, own_sem, get_sem, put_sem,
 ):
-    subjects = vi_ref.shape[0]
-    depth = lab_hbm.shape[0]
+    subjects = im_ref.shape[1]
+    depth, count, width = t_hbm.shape
     odd = odd_ref[0]
     facing = jnp.where(odd == 1, 0, depth - 1)
-    sides = ((facing, vi_ref, near_ref, near_sem, 0), (depth - 1 - facing, vo_ref, far_ref, far_sem, 1))
-
-    def fetch(s, z, buffer, sem):
-        return pltpu.make_async_copy(old_hbm.at[s, :, pl.ds(z, 1)], buffer.at[s], sem.at[0, s])
-
-    def store(s, z, buffer, sem):
-        return pltpu.make_async_copy(buffer.at[s], out_hbm.at[s, :, pl.ds(z, 1)], sem.at[1, s])
-
-    labels = [pltpu.make_async_copy(lab_hbm.at[z], lab_ref.at[side], lab_sem.at[side]) for z, *_, side in sides]
-    for copy in labels:
-        copy.start()
+    sides = ((0, facing, vi_ref, own_in_hbm), (1, depth - 1 - facing, vo_ref, own_far_hbm))
+
+    def early(side, z, own):
+        beside = jnp.where(z == 0, 1, depth - 2)
+        return [
+            pltpu.make_async_copy(t_hbm.at[z], t_ref.at[side, 0], t_sem.at[side, 0]),
+            pltpu.make_async_copy(t_hbm.at[beside], t_ref.at[side, 1], t_sem.at[side, 1]),
+            pltpu.make_async_copy(lab_hbm.at[z], lab_ref.at[side], lab_sem.at[side]),
+        ]
+
+    def late(side, z, own, s):
+        return [
+            pltpu.make_async_copy(im_hbm.at[s, z], im_ref.at[side, s], im_sem.at[side, s]),
+            pltpu.make_async_copy(own.at[pl.ds(3 * s, 3)], own_ref.at[side, s], own_sem.at[side, s]),
+            pltpu.make_async_copy(old_hbm.at[s, :, z], new_ref.at[side, s], get_sem.at[side, s]),
+        ]
+
+    def store(side, z, s):
+        return pltpu.make_async_copy(new_ref.at[side, s], out_hbm.at[s, :, z], put_sem.at[side, s])
+
+    for side, z, _, own in sides:
+        for copy in early(side, z, own):
+            copy.start()
     for s in range(subjects):
-        for z, _, buffer, sem, _ in sides:
-            fetch(s, z, buffer, sem).start()
-    for copy in labels:
-        copy.wait()
+        for side, z, _, own in sides:
+            for copy in late(side, z, own, s):
+                copy.start()
+    for side, z, halo, own in sides:
+        for copy in early(side, z, own):
+            copy.wait()
+        sign = jnp.where(z == 0, 0.5, -0.5)
+        for j in range(count // ROWS):
+            start = j * ROWS
+            rows = pl.ds(start, ROWS)
+            here = t_ref[side, 0, rows, :]
+            y_low, y_high = beside_y(
+                lambda at: t_ref[side, 0, pl.ds(at, 1), :], here, j == 0, start + ROWS == count, count, start
+            )
+            x_low, x_high = beside_x(here)
+            s_ref[side, 0, rows, :] = sign * (t_ref[side, 1, rows, :] - halo[3 * subjects, rows, :])
+            s_ref[side, 1, rows, :] = 0.5 * (y_high - y_low)
+            s_ref[side, 2, rows, :] = 0.5 * (x_high - x_low)
+            s_ref[side, 3, rows, :] = rate_at(lab_ref[side, rows, :], stiff)
     for s in range(subjects):
-        for z, halo, buffer, sem, side in sides:
-            fetch(s, z, buffer, sem).wait()
-            rate = rate_at(lab_ref[side], stiff)
-            for c in range(3):
-                buffer[s, c, 0] = buffer[s, c, 0] + rate * halo[s, c, 0]
-            store(s, z, buffer, sem).start()
+        level = gain[cohort[s]]
+        for side, z, halo, own in sides:
+            for copy in late(side, z, own, s):
+                copy.wait()
+            for j in range(count // ROWS):
+                rows = pl.ds(j * ROWS, ROWS)
+                value = t_ref[side, 0, rows, :] - level * im_ref[side, s, rows, :].astype(jnp.float32)
+                for c in range(3):
+                    value = value + s_ref[side, c, rows, :] * own_ref[side, s, c, rows, :]
+                value = velocity_step * value
+                rate = s_ref[side, 3, rows, :]
+                for c in range(3):
+                    new_ref[side, s, c, rows, :] = (
+                        new_ref[side, s, c, rows, :]
+                        + rate * halo[3 * s + c, rows, :]
+                        - value * s_ref[side, c, rows, :]
+                    )
+            store(side, z, s).start()
     for s in range(subjects):
-        for z, _, buffer, sem, _ in sides:
-            store(s, z, buffer, sem).wait()
+        for side, z, _, _ in sides:
+            store(side, z, s).wait()
 
 
 SMALL = pl.BlockSpec(memory_space=pltpu.SMEM)
@@ -244,15 +321,15 @@
     )(place, template, parts)
 
 
-def moved(odd, cohort, gain, stiffness, template, t_inner, t_outer, labels, images, velocity):
+def moved(odd, cohort, gain, stiffness, template, labels, images, velocity, share_rows):
     subjects = images.shape[0]
     depth, count, width = template.shape
-    edge = jax.ShapeDtypeStruct((subjects, 3, 1, count, width), jnp.float32)
+    edge = jax.ShapeDtypeStruct((3 * subjects + 1, count, width), jnp.float32)
     whole = jax.ShapeDtypeStruct(velocity.shape, jnp.float32)
     return pl.pallas_call(
         move_kernel,
-        out_shape=[jax.ShapeDtypeStruct(template.shape, jnp.float32), edge, edge, whole],
-        in_specs=[SMALL] * 4 + [FAR] * 6,
+        out_shape=[jax.ShapeDtypeStruct((depth, share_rows, width), jnp.float32), edge, edge, whole],
+        in_specs=[SMALL] * 4 + [FAR] * 4,
         out_specs=[NEAR, FAR, FAR, FAR],
         scratch_shapes=[
             pltpu.VMEM((depth + 2, count, width), jnp.float32),
@@ -262,59 +339,75 @@
             pltpu.VMEM(velocity.shape, jnp.float32),
             pltpu.VMEM((3,) + template.shape, jnp.float32),
             pltpu.VMEM(template.shape, jnp.float32),
-            COPY((3,)), COPY(()), COPY((subjects,)), COPY((subjects, 3)),
-            COPY((subjects,)), COPY((subjects,)), COPY((subjects, 2)),
+            COPY(()), COPY(()), COPY((subjects,)), COPY((subjects, 3)),
+            COPY((subjects,)), COPY((subjects,)), COPY((subjects, 2)), COPY((2,)),
         ],
         compiler_params=pltpu.CompilerParams(vmem_limit_bytes=60 * MIB),
         cost_estimate=pl.CostEstimate(flops=8 * velocity.size, bytes_accessed=16 * MIB, transcendentals=0),
         name="moved",
-    )(odd, cohort, gain, stiffness, template, t_inner, t_outer, labels, images, velocity)
-
-
-def edges_added(odd, stiffness, labels, v_inner, v_outer, velocity):
-    subjects = velocity.shape[0]
-    count, width = labels.shape[1:]
+    )(odd, cohort, gain, stiffness, template, labels, images, velocity)
+
+
+def edges_added(odd, cohort, gain, stiffness, template, labels, images, inner, outer, v_inner, v_outer, velocity):
+    subjects = images.shape[0]
+    depth, count, width = template.shape
     return pl.pallas_call(
         edge_kernel,
         out_shape=jax.ShapeDtypeStruct(velocity.shape, jnp.float32),
-        in_specs=[SMALL] * 2 + [FAR, NEAR, NEAR, FAR],
+        in_specs=[SMALL] * 4 + [FAR] * 5 + [NEAR, NEAR, FAR],
         out_specs=FAR,
         scratch_shapes=[
+            pltpu.VMEM((2, 2, count, width), jnp.float32),
             pltpu.VMEM((2, count, width), labels.dtype),
-            pltpu.VMEM(v_inner.shape, jnp.float32),
-            pltpu.VMEM(v_outer.shape, jnp.float32),
-            COPY((2,)), COPY((2, subjects)), COPY((2, subjects)),
+            pltpu.VMEM((2, subjects, count, width), images.dtype),
+            pltpu.VMEM((2, subjects, 3, count, width), jnp.float32),
+            pltpu.VMEM((2, subjects, 3, count, width), jnp.float32),
+            pltpu.VMEM((2, 4, count, width), jnp.float32),
+            COPY((2, 2)), COPY((2,)), COPY((2, subjects)), COPY((2, subjects)), COPY((2, subjects)), COPY((2, subjects)),
         ],
-        input_output_aliases={5: 0},
+        input_output_aliases={11: 0},
         compiler_params=pltpu.CompilerParams(vmem_limit_bytes=50 * MIB),
-        cost_estimate=pl.CostEstimate(flops=v_inner.size, bytes_accessed=6 * MIB, transcendentals=0),
+        cost_estimate=pl.CostEstimate(flops=velocity.size, bytes_accessed=8 * MIB, transcendentals=0),
         name="edges_added",
-    )(odd, stiffness, labels, v_inner, v_outer, velocity)
+    )(odd, cohort, gain, stiffness, template, labels, images, inner, outer, v_inner, v_outer, velocity)
+
+
+def finished(odd, scale, shares, t_inner, t_outer, shape):
+    return pl.pallas_call(
+        lambda *refs: finish_kernel(refs[0], scale, *refs[1:]),
+        out_shape=jax.ShapeDtypeStruct(shape, jnp.float32),
+        in_specs=[SMALL, NEAR, FREE, FREE],
+        out_specs=NEAR,
+        scratch_shapes=[pltpu.VMEM((2,) + shape[1:], jnp.float32), COPY((2,))],
+        compiler_params=pltpu.CompilerParams(vmem_limit_bytes=8 * MIB),
+        cost_estimate=pl.CostEstimate(flops=shares.size, bytes_accessed=2 * MIB, transcendentals=0),
+        name="finished",
+    )(odd, shares, t_inner, t_outer)
 
 
 def local(template, images, velocity, labels, stiffness, cohort, site_gain):
-    depth = template.shape[0]
+    depth, count, _ = template.shape
     slabs = lax.axis_size("slab")
     groups = lax.axis_size("grp")
-    assert depth == groups and slabs % 2 == 0
-    odd = lax.axis_index("slab") % 2
+    assert depth == groups and slabs % 2 == 0 and 2 * count == ROWS * groups
+    odd = (lax.axis_index("slab") % 2).reshape(1)
     place = lax.axis_index("grp").reshape(1)
     inside = [(i, i ^ 1) for i in range(slabs)]
     across = [(i, i + 1) for i in range(1, slabs - 1, 2)]
     across = across + [(target, source) for source, target in across]
-    facing = jnp.where(odd == 1, 0, depth - 1)
-    t_inner = lax.ppermute(lax.dynamic_slice_in_dim(template, facing, 1, 0), "slab", inside)
-    t_outer = lax.ppermute(lax.dynamic_slice_in_dim(template, depth - 1 - facing, 1, 0), "slab", across)
-    odd = odd.reshape(1)
+    scale = template_step / (images.shape[0] * groups)
     part, inner, outer, new_velocity = moved(
-        odd, cohort, site_gain, stiffness, template, t_inner, t_outer, labels, images, velocity
+        odd, cohort, site_gain, stiffness, template, labels, images, velocity, count + ROWS
     )
     v_inner = lax.ppermute(inner, "slab", inside)
     v_outer = lax.ppermute(outer, "slab", across)
     parts = lax.all_to_all(part, "grp", 0, 0, tiled=True)
-    shares = share_update(place, template_step / (images.shape[0] * groups), template, parts)
-    new_template = lax.all_to_all(shares, "grp", 0, 0, tiled=True)
-    new_velocity = edges_added(odd, stiffness, labels, v_inner, v_outer, new_velocity)
+    shares = share_update(place, scale, template, parts)
+    shares = lax.all_to_all(shares, "grp", 0, 0, tiled=True)
+    new_velocity = edges_added(
+        odd, cohort, site_gain, stiffness, template, labels, images, inner, outer, v_inner, v_outer, new_velocity
+    )
+    new_template = finished(odd, scale, shares, v_inner, v_outer, template.shape)
     return (new_template, new_velocity)
 
 

time: 56.2 us -> 54.6 us (0.972)
  the two profiles are of different devices: /device:TPU:1 before, /device:TPU:230 now
where the time goes in v7:
time: 54.6 us; the launch traced here: 54.1 us
  Pallas kernels  19.7 us (36%)
  starting transfers between devices  14.8 us (27%)
  waiting for transfers between devices  14.4 us (26%)
  local copies, waits for them, and re-layouts  4.38 us (8%)
  between operations  0.76 us (1%)
    all_to_all x1, waiting for transfers between devices, local(): parts = lax.all_to_all(part, 'grp', 0, 0, tiled=True)  14.4 us
    pallas_call x1, Pallas kernels, moved(): pl.pallas_call(move_kernel, out_shape=[jax.ShapeDtypeStruct((depth, share...  12 us
    all_to_all x1, starting transfers between devices, local(): parts = lax.all_to_all(part, 'grp', 0, 0, tiled=True)  5.94 us
    all_to_all x1, starting transfers between devices, local(): shares = lax.all_to_all(shares, 'grp', 0, 0, tiled=True)  5.83 us
    pallas_call x1, Pallas kernels, edges_added(): pl.pallas_call(edge_kernel, out_shape=jax.ShapeDtypeStruct(velocity.shape...  5.77 us
    unnamed x18, local copies, waits for them, and re-layouts  4.38 us
    ppermute x1, starting transfers between devices, local(): v_outer = lax.ppermute(outer, 'slab', across)  3.02 us
  transfers between devices with their start and end apart: 4, of which 1 were waited for; matrix products, arithmetic and copies ran while one was open for 0% of the time, Pallas kernels for 12%

profile of v7, /device:TPU:230, one launch (start us, length us, event | category | flops | bytes accessed | tf_op | source)
XLA Modules:
  0.0 54.1 jit_solution(5457653572845540490)
XLA Ops:
  0.6 0.0 copy-start
  0.7 0.0 copy-start.3
  0.7 0.0 copy-start.6
  0.7 0.0 copy-start.7
  0.7 0.0 copy-start.8
  0.7 12.0 %moved.1 = (f32[8,80,256]{2,1,0:T(8,128)}, f32[13,64,256]{2,1,0:T(8,128)}, f32[13,64,256]{2,1,0:T(8,128)}, f32[4,3,8,64,256]{4,3,2,1,0:T(8,128)}) custom-call(s32[1]{0:T(128)} %bitcast.odd_ref.refs_0_, s32[4]{0:T(128)} %cohort.3, f32[8]{0:T(128)} %gain.3, f32[4]{0:T(128)} %stiff.3, f32[8,64,256]{2,1,0:T(8,128)} %t_hbm.3, s32[8,64,256]{2,1,0:T(8,128)} %lab_hbm.3, ...), custom_call_target="tpu_custom_call" | custom-call | flops 12582912 | bytes 16777216 | tf_op jit(solution)/shard_map/moved/pallas_call | solution.py:329
  12.7 5.9 %all-to-all-start = ((f32[8,80,256]{2,1,0:T(8,128)}), f32[8,80,256]{2,1,0:T(8,128)S(1)}, u32[]{:S(2)}, u32[]{:S(2)}) async-start(f32[8,80,256]{2,1,0:T(8,128)} %get-tuple-element.6), calls=%async_computation | async-start | bytes 1310720 | tf_op jit(solution)/shard_map/all_to_all | solution.py:404
  18.6 0.0 collective-permute-start
  18.6 3.0 %collective-permute-start.1 = (f32[13,64,256]{2,1,0:T(8,128)}, f32[13,64,256]{2,1,0:T(8,128)S(1)}, u32[]{:S(2)}, u32[]{:S(2)}) collective-permute-start(f32[13,64,256]{2,1,0:T(8,128)} %get-tuple-element.8.own_far_hbm), channel_id=1, source_target_pairs={{1,2},{3,4},{5,6},{7,8},{9,10},{11,12},{13,14},{15,16},{17,18},{19... | collective-permute-start | bytes 2555912 | tf_op jit(solution)/shard_map/ppermute | solution.py:403
  21.6 14.4 %all-to-all-done.refs_2_ = f32[8,80,256]{2,1,0:T(8,128)S(1)} async-done(((f32[8,80,256]{2,1,0:T(8,128)}), f32[8,80,256]{2,1,0:T(8,128)S(1)}, u32[]{:S(2)}, u32[]{:S(2)}) %all-to-all-start) | async-done | bytes 655392 | tf_op jit(solution)/shard_map/all_to_all | solution.py:404
  36.1 0.0 copy-done
  36.1 1.0 %share_update.1 = f32[8,80,256]{2,1,0:T(8,128)} custom-call(s32[1]{0:T(128)} %bitcast.1.refs_0_, f32[8,64,256]{2,1,0:T(8,128)S(1)} %copy-done, f32[8,80,256]{2,1,0:T(8,128)S(1)} %all-to-all-done.refs_2_), custom_call_target="tpu_custom_call" | custom-call | flops 163840 | bytes 2097152 | tf_op jit(solution)/shard_map/share_update/pallas_call | solution.py:312
  37.0 5.8 %all-to-all-start.1 = ((f32[8,80,256]{2,1,0:T(8,128)}), f32[8,80,256]{2,1,0:T(8,128)S(1)}, u32[]{:S(2)}, u32[]{:S(2)}) async-start(f32[8,80,256]{2,1,0:T(8,128)} %share_update.1), calls=%async_computation.1 | async-start | bytes 1310720 | tf_op jit(solution)/shard_map/all_to_all | solution.py:406
  42.9 0.0 collective-permute-done.refs_2_.vi_ref
  42.9 0.0 collective-permute-done.1.refs_3_.vo_ref
  42.9 0.0 copy-start.1
  42.9 0.9 %copy-done.1 = f32[13,64,256]{2,1,0:T(8,128)} copy-done((f32[13,64,256]{2,1,0:T(8,128)}, f32[13,64,256]{2,1,0:T(8,128)S(1)}, u32[]{:S(2)}) %copy-start.1) | copy-done | bytes 851992
  43.8 0.0 copy-done.3
  43.8 0.0 copy-done.6
  43.8 0.0 copy-done.7
  43.8 0.0 copy-done.8
  43.8 0.0 copy-start.4
  43.8 1.1 %copy-done.4 = f32[13,64,256]{2,1,0:T(8,128)S(1)} copy-done((f32[13,64,256]{2,1,0:T(8,128)S(1)}, f32[13,64,256]{2,1,0:T(8,128)}, u32[]{:S(2)}) %copy-start.4) | copy-done | bytes 851992
  45.0 0.0 copy-start.5
  45.0 1.2 %copy-done.5 = f32[13,64,256]{2,1,0:T(8,128)S(1)} copy-done((f32[13,64,256]{2,1,0:T(8,128)S(1)}, f32[13,64,256]{2,1,0:T(8,128)}, u32[]{:S(2)}) %copy-start.5) | copy-done | bytes 851992
  46.1 5.8 %edges_added.1 = f32[4,3,8,64,256]{4,3,2,1,0:T(8,128)} custom-call(s32[1]{0:T(128)} %bitcast.odd_ref.refs_0_, s32[4]{0:T(128)S(1)} %copy-done.6, f32[8]{0:T(128)S(1)} %copy-done.7, f32[4]{0:T(128)S(1)} %copy-done.8, f32[8,64,256]{2,1,0:T(8,128)S(1)} %copy-done, s32[8,64,256]{2,1,0:T(8,128)S(1)} %copy-done.3, ...), custom_call_target="tpu_custom_call", output_to_operand_aliasing={{}: (11, {})} | custom-call | flops 1572864 | bytes 8388608 | tf_op jit(solution)/shard_map/edges_added/pallas_call | solution.py:354
  51.9 0.0 all-to-all-done.1.refs_1_
  51.9 0.0 copy-start.2
  51.9 1.1 %copy-done.2 = f32[13,64,256]{2,1,0:T(8,128)S(1)} copy-done((f32[13,64,256]{2,1,0:T(8,128)S(1)}, f32[13,64,256]{2,1,0:T(8,128)}, u32[]{:S(2)}) %copy-start.2) | copy-done | bytes 851992
  53.1 1.0 %finished.1 = f32[8,64,256]{2,1,0:T(8,128)} custom-call(s32[1]{0:T(128)} %bitcast.odd_ref.refs_0_, f32[8,80,256]{2,1,0:T(8,128)S(1)} %all-to-all-done.1.refs_1_, f32[13,64,256]{2,1,0:T(8,128)S(1)} %collective-permute-done.refs_2_.vi_ref, f32[13,64,256]{2,1,0:T(8,128)S(1)} %copy-done.2), custom_call_target="tpu_custom_call" | custom-call | flops 163840 | bytes 2097152 | tf_op jit(solution)/shard_map/finished/pallas_call | solution.py:376
Async XLA Ops:
  0.6 35.4 %copy-start = (f32[8,64,256]{2,1,0:T(8,128)S(1)}, f32[8,64,256]{2,1,0:T(8,128)}, u32[]{:S(2)}) copy-start(f32[8,64,256]{2,1,0:T(8,128)} %t_hbm.3) | copy-start | bytes 1572868
  0.7 43.1 %copy-start.3 = (s32[8,64,256]{2,1,0:T(8,128)S(1)}, s32[8,64,256]{2,1,0:T(8,128)}, u32[]{:S(2)}) copy-start(s32[8,64,256]{2,1,0:T(8,128)} %lab_hbm.3) | copy-start | bytes 1572868
  0.7 43.1 %copy-start.6 = (s32[4]{0:T(128)S(1)}, s32[4]{0:T(128)}, u32[]{:S(2)}) copy-start(s32[4]{0:T(128)} %cohort.3) | copy-start | bytes 52
  0.7 43.1 %copy-start.7 = (f32[8]{0:T(128)S(1)}, f32[8]{0:T(128)}, u32[]{:S(2)}) copy-start(f32[8]{0:T(128)} %gain.3) | copy-start | bytes 100
  0.7 43.1 %copy-start.8 = (f32[4]{0:T(128)S(1)}, f32[4]{0:T(128)}, u32[]{:S(2)}) copy-start(f32[4]{0:T(128)} %stiff.3) | copy-start | bytes 52
  12.7 23.4 %all-to-all-start = ((f32[8,80,256]{2,1,0:T(8,128)}), f32[8,80,256]{2,1,0:T(8,128)S(1)}, u32[]{:S(2)}, u32[]{:S(2)}) async-start(f32[8,80,256]{2,1,0:T(8,128)} %get-tuple-element.6), calls=%async_computation | async-start | bytes 1310720 | tf_op jit(solution)/shard_map/all_to_all | solution.py:404
  18.6 24.3 %collective-permute-start = (f32[13,64,256]{2,1,0:T(8,128)}, f32[13,64,256]{2,1,0:T(8,128)S(1)}, u32[]{:S(2)}, u32[]{:S(2)}) collective-permute-start(f32[13,64,256]{2,1,0:T(8,128)} %get-tuple-element.7.own_in_hbm), channel_id=1, source_target_pairs={{0,1},{1,0},{2,3},{3,2},{4,5},{5,4},{6,7},{7,6},{8,9},{9,8},{10,11... | collective-permute-start | bytes 2555912 | tf_op jit(solution)/shard_map/ppermute | solution.py:402
  18.6 24.3 %collective-permute-start.1 = (f32[13,64,256]{2,1,0:T(8,128)}, f32[13,64,256]{2,1,0:T(8,128)S(1)}, u32[]{:S(2)}, u32[]{:S(2)}) collective-permute-start(f32[13,64,256]{2,1,0:T(8,128)} %get-tuple-element.8.own_far_hbm), channel_id=1, source_target_pairs={{1,2},{3,4},{5,6},{7,8},{9,10},{11,12},{13,14},{15,16},{17,18},{19... | collective-permute-start | bytes 2555912 | tf_op jit(solution)/shard_map/ppermute | solution.py:403
  37.0 14.9 %all-to-all-start.1 = ((f32[8,80,256]{2,1,0:T(8,128)}), f32[8,80,256]{2,1,0:T(8,128)S(1)}, u32[]{:S(2)}, u32[]{:S(2)}) async-start(f32[8,80,256]{2,1,0:T(8,128)} %share_update.1), calls=%async_computation.1 | async-start | bytes 1310720 | tf_op jit(solution)/shard_map/all_to_all | solution.py:406
  42.9 0.9 %copy-start.1 = (f32[13,64,256]{2,1,0:T(8,128)}, f32[13,64,256]{2,1,0:T(8,128)S(1)}, u32[]{:S(2)}) copy-start(f32[13,64,256]{2,1,0:T(8,128)S(1)} %collective-permute-done.1.refs_3_.vo_ref) | copy-start | bytes 2555908
  43.8 1.2 %copy-start.4 = (f32[13,64,256]{2,1,0:T(8,128)S(1)}, f32[13,64,256]{2,1,0:T(8,128)}, u32[]{:S(2)}) copy-start(f32[13,64,256]{2,1,0:T(8,128)} %get-tuple-element.7.own_in_hbm) | copy-start | bytes 2555908
  45.0 1.2 %copy-start.5 = (f32[13,64,256]{2,1,0:T(8,128)S(1)}, f32[13,64,256]{2,1,0:T(8,128)}, u32[]{:S(2)}) copy-start(f32[13,64,256]{2,1,0:T(8,128)} %get-tuple-element.8.own_far_hbm) | copy-start | bytes 2555908
  51.9 1.2 %copy-start.2 = (f32[13,64,256]{2,1,0:T(8,128)S(1)}, f32[13,64,256]{2,1,0:T(8,128)}, u32[]{:S(2)}) copy-start(f32[13,64,256]{2,1,0:T(8,128)} %copy-done.1) | copy-start | bytes 2555908

commit v8 on v7

--- a/solution.py
+++ b/solution.py
@@ -68,16 +68,10 @@
             out_ref[g, rows, :] = value
 
 
-def finish_kernel(odd_ref, scale, all_ref, ti_hbm, to_hbm, out_ref, halo_ref, sem):
+def finish_kernel(odd_ref, scale, all_ref, halo_ref, out_ref):
     depth, count, width = out_ref.shape
     pieces = depth // 2
     odd = odd_ref[0]
-    copies = [
-        pltpu.make_async_copy(far.at[far.shape[0] - 1], halo_ref.at[side], sem.at[side])
-        for side, far in enumerate((ti_hbm, to_hbm))
-    ]
-    for copy in copies:
-        copy.start()
 
     @pl.loop(0, depth)
     def _(z):
@@ -85,7 +79,6 @@
 
     facing = jnp.where(odd == 1, 0, depth - 1)
     for side, z in enumerate((facing, depth - 1 - facing)):
-        copies[side].wait()
         factor = jnp.where(z == 0, 0.5 * scale, -0.5 * scale)
         for q in range(pieces):
             rows = pl.ds(q * (count // pieces), count // pieces)
@@ -227,44 +220,48 @@
 
 
 def edge_kernel(
-    odd_ref, cohort, gain, stiff, t_hbm, lab_hbm, im_hbm, own_in_hbm, own_far_hbm, vi_ref, vo_ref, old_hbm, out_hbm,
-    t_ref, lab_ref, im_ref, own_ref, new_ref, s_ref, t_sem, lab_sem, im_sem, own_sem, get_sem, put_sem,
+    odd_ref, cohort, gain, stiff, t_hbm, lab_hbm, im_hbm, own_in_hbm, own_far_hbm, vi_hbm, vo_hbm, old_hbm, out_hbm, beyond_ref,
+    t_ref, lab_ref, im_ref, own_ref, halo_ref, new_ref, s_ref,
+    t_sem, lab_sem, im_sem, own_sem, halo_sem, get_sem, put_sem,
 ):
     subjects = im_ref.shape[1]
     depth, count, width = t_hbm.shape
     odd = odd_ref[0]
     facing = jnp.where(odd == 1, 0, depth - 1)
-    sides = ((0, facing, vi_ref, own_in_hbm), (1, depth - 1 - facing, vo_ref, own_far_hbm))
-
-    def early(side, z, own):
+    sides = ((0, facing, vi_hbm, own_in_hbm), (1, depth - 1 - facing, vo_hbm, own_far_hbm))
+
+    def early(side, z, halo):
         beside = jnp.where(z == 0, 1, depth - 2)
         return [
             pltpu.make_async_copy(t_hbm.at[z], t_ref.at[side, 0], t_sem.at[side, 0]),
             pltpu.make_async_copy(t_hbm.at[beside], t_ref.at[side, 1], t_sem.at[side, 1]),
+            pltpu.make_async_copy(halo.at[3 * subjects], t_ref.at[side, 2], t_sem.at[side, 2]),
             pltpu.make_async_copy(lab_hbm.at[z], lab_ref.at[side], lab_sem.at[side]),
         ]
 
-    def late(side, z, own, s):
+    def late(side, z, halo, own, s):
         return [
             pltpu.make_async_copy(im_hbm.at[s, z], im_ref.at[side, s], im_sem.at[side, s]),
             pltpu.make_async_copy(own.at[pl.ds(3 * s, 3)], own_ref.at[side, s], own_sem.at[side, s]),
+            pltpu.make_async_copy(halo.at[pl.ds(3 * s, 3)], halo_ref.at[side, s], halo_sem.at[side, s]),
             pltpu.make_async_copy(old_hbm.at[s, :, z], new_ref.at[side, s], get_sem.at[side, s]),
         ]
 
     def store(side, z, s):
         return pltpu.make_async_copy(new_ref.at[side, s], out_hbm.at[s, :, z], put_sem.at[side, s])
 
-    for side, z, _, own in sides:
-        for copy in early(side, z, own):
+    for side, z, halo, _ in sides:
+        for copy in early(side, z, halo):
             copy.start()
     for s in range(subjects):
-        for side, z, _, own in sides:
-            for copy in late(side, z, own, s):
+        for side, z, halo, own in sides:
+            for copy in late(side, z, halo, own, s):
                 copy.start()
-    for side, z, halo, own in sides:
-        for copy in early(side, z, own):
+    for side, z, halo, _ in sides:
+        for copy in early(side, z, halo):
             copy.wait()
         sign = jnp.where(z == 0, 0.5, -0.5)
+        beyond_ref[side] = t_ref[side, 2]
         for j in range(count // ROWS):
             start = j * ROWS
             rows = pl.ds(start, ROWS)
@@ -273,14 +270,14 @@
                 lambda at: t_ref[side, 0, pl.ds(at, 1), :], here, j == 0, start + ROWS == count, count, start
             )
             x_low, x_high = beside_x(here)
-            s_ref[side, 0, rows, :] = sign * (t_ref[side, 1, rows, :] - halo[3 * subjects, rows, :])
+            s_ref[side, 0, rows, :] = sign * (t_ref[side, 1, rows, :] - t_ref[side, 2, rows, :])
             s_ref[side, 1, rows, :] = 0.5 * (y_high - y_low)
             s_ref[side, 2, rows, :] = 0.5 * (x_high - x_low)
             s_ref[side, 3, rows, :] = rate_at(lab_ref[side, rows, :], stiff)
     for s in range(subjects):
         level = gain[cohort[s]]
         for side, z, halo, own in sides:
-            for copy in late(side, z, own, s):
+            for copy in late(side, z, halo, own, s):
                 copy.wait()
             for j in range(count // ROWS):
                 rows = pl.ds(j * ROWS, ROWS)
@@ -292,7 +289,7 @@
                 for c in range(3):
                     new_ref[side, s, c, rows, :] = (
                         new_ref[side, s, c, rows, :]
-                        + rate * halo[3 * s + c, rows, :]
+                        + rate * halo_ref[side, s, c, rows, :]
                         - value * s_ref[side, c, rows, :]
                     )
             store(side, z, s).start()
@@ -353,36 +350,39 @@
     depth, count, width = template.shape
     return pl.pallas_call(
         edge_kernel,
-        out_shape=jax.ShapeDtypeStruct(velocity.shape, jnp.float32),
-        in_specs=[SMALL] * 4 + [FAR] * 5 + [NEAR, NEAR, FAR],
-        out_specs=FAR,
+        out_shape=[
+            jax.ShapeDtypeStruct(velocity.shape, jnp.float32),
+            jax.ShapeDtypeStruct((2, count, width), jnp.float32),
+        ],
+        in_specs=[SMALL] * 4 + [FAR] * 8,
+        out_specs=[FAR, NEAR],
         scratch_shapes=[
-            pltpu.VMEM((2, 2, count, width), jnp.float32),
+            pltpu.VMEM((2, 3, count, width), jnp.float32),
             pltpu.VMEM((2, count, width), labels.dtype),
             pltpu.VMEM((2, subjects, count, width), images.dtype),
             pltpu.VMEM((2, subjects, 3, count, width), jnp.float32),
             pltpu.VMEM((2, subjects, 3, count, width), jnp.float32),
+            pltpu.VMEM((2, subjects, 3, count, width), jnp.float32),
             pltpu.VMEM((2, 4, count, width), jnp.float32),
-            COPY((2, 2)), COPY((2,)), COPY((2, subjects)), COPY((2, subjects)), COPY((2, subjects)), COPY((2, subjects)),
+            COPY((2, 3)), COPY((2,)), COPY((2, subjects)), COPY((2, subjects)), COPY((2, subjects)), COPY((2, subjects)), COPY((2, subjects)),
         ],
         input_output_aliases={11: 0},
-        compiler_params=pltpu.CompilerParams(vmem_limit_bytes=50 * MIB),
+        compiler_params=pltpu.CompilerParams(vmem_limit_bytes=56 * MIB),
         cost_estimate=pl.CostEstimate(flops=velocity.size, bytes_accessed=8 * MIB, transcendentals=0),
         name="edges_added",
     )(odd, cohort, gain, stiffness, template, labels, images, inner, outer, v_inner, v_outer, velocity)
 
 
-def finished(odd, scale, shares, t_inner, t_outer, shape):
+def finished(odd, scale, shares, halo, shape):
     return pl.pallas_call(
         lambda *refs: finish_kernel(refs[0], scale, *refs[1:]),
         out_shape=jax.ShapeDtypeStruct(shape, jnp.float32),
-        in_specs=[SMALL, NEAR, FREE, FREE],
+        in_specs=[SMALL, NEAR, NEAR],
         out_specs=NEAR,
-        scratch_shapes=[pltpu.VMEM((2,) + shape[1:], jnp.float32), COPY((2,))],
         compiler_params=pltpu.CompilerParams(vmem_limit_bytes=8 * MIB),
         cost_estimate=pl.CostEstimate(flops=shares.size, bytes_accessed=2 * MIB, transcendentals=0),
         name="finished",
-    )(odd, shares, t_inner, t_outer)
+    )(odd, shares, halo)
 
 
 def local(template, images, velocity, labels, stiffness, cohort, site_gain):
@@ -404,10 +404,10 @@
     parts = lax.all_to_all(part, "grp", 0, 0, tiled=True)
     shares = share_update(place, scale, template, parts)
     shares = lax.all_to_all(shares, "grp", 0, 0, tiled=True)
-    new_velocity = edges_added(
+    new_velocity, halo = edges_added(
         odd, cohort, site_gain, stiffness, template, labels, images, inner, outer, v_inner, v_outer, new_velocity
     )
-    new_template = finished(odd, scale, shares, v_inner, v_outer, template.shape)
+    new_template = finished(odd, scale, shares, halo, template.shape)
     return (new_template, new_velocity)
 
 

time: 54.6 us -> 52.8 us (0.967)
  the two profiles are of different devices: /device:TPU:230 before, /device:TPU:228 now
where the time goes in v8:
time: 52.8 us; the launch traced here: 52.5 us
  Pallas kernels  19.2 us (36%)
  waiting for transfers between devices  16.2 us (31%)
  starting transfers between devices  14.3 us (27%)
  local copies, waits for them, and re-layouts  2.07 us (4%)
  between operations  0.72 us (1%)
    all_to_all x1, waiting for transfers between devices, local(): parts = lax.all_to_all(part, 'grp', 0, 0, tiled=True)  14.1 us
    pallas_call x1, Pallas kernels, moved(): pl.pallas_call(move_kernel, out_shape=[jax.ShapeDtypeStruct((depth, share...  11.9 us
    all_to_all x1, starting transfers between devices, local(): shares = lax.all_to_all(shares, 'grp', 0, 0, tiled=True)  6.2 us
    pallas_call x1, Pallas kernels, edges_added(): pl.pallas_call(edge_kernel, out_shape=[jax.ShapeDtypeStruct(velocity.shap...  5.47 us
    all_to_all x1, starting transfers between devices, local(): parts = lax.all_to_all(part, 'grp', 0, 0, tiled=True)  5.12 us
    ppermute x1, starting transfers between devices, local(): v_outer = lax.ppermute(outer, 'slab', across)  3.01 us
    all_to_all x1, waiting for transfers between devices, local(): shares = lax.all_to_all(shares, 'grp', 0, 0, tiled=True)  2.13 us
    unnamed x8, local copies, waits for them, and re-layouts  2.07 us
  transfers between devices with their start and end apart: 4, of which 2 were waited for; matrix products, arithmetic and copies ran while one was open for 0% of the time, Pallas kernels for 12%

profile of v8, /device:TPU:228, one launch (start us, length us, event | category | flops | bytes accessed | tf_op | source)
XLA Modules:
  0.0 52.5 jit_solution(12040426941882650166)
XLA Ops:
  0.6 0.0 copy-start
  0.7 11.9 %moved.1 = (f32[8,80,256]{2,1,0:T(8,128)}, f32[13,64,256]{2,1,0:T(8,128)}, f32[13,64,256]{2,1,0:T(8,128)}, f32[4,3,8,64,256]{4,3,2,1,0:T(8,128)}) custom-call(s32[1]{0:T(128)} %bitcast.odd_ref.refs_0_, s32[4]{0:T(128)} %cohort.3, f32[8]{0:T(128)} %gain.3, f32[4]{0:T(128)} %stiff.3, f32[8,64,256]{2,1,0:T(8,128)} %t_hbm.3, s32[8,64,256]{2,1,0:T(8,128)} %lab_hbm.3, ...), custom_call_target="tpu_custom_call" | custom-call | flops 12582912 | bytes 16777216 | tf_op jit(solution)/shard_map/moved/pallas_call | solution.py:326
  12.5 5.1 %all-to-all-start = ((f32[8,80,256]{2,1,0:T(8,128)}), f32[8,80,256]{2,1,0:T(8,128)S(1)}, u32[]{:S(2)}, u32[]{:S(2)}) async-start(f32[8,80,256]{2,1,0:T(8,128)} %get-tuple-element.8), calls=%async_computation | async-start | bytes 1310720 | tf_op jit(solution)/shard_map/all_to_all | solution.py:404
  17.6 0.0 collective-permute-start
  17.6 3.0 %collective-permute-start.1 = (f32[13,64,256]{2,1,0:T(8,128)}, f32[13,64,256]{2,1,0:T(8,128)S(1)}, u32[]{:S(2)}, u32[]{:S(2)}) collective-permute-start(f32[13,64,256]{2,1,0:T(8,128)} %get-tuple-element.10.own_far_hbm), channel_id=1, source_target_pairs={{1,2},{3,4},{5,6},{7,8},{9,10},{11,12},{13,14},{15,16},{17,18},{19... | collective-permute-start | bytes 2555912 | tf_op jit(solution)/shard_map/ppermute | solution.py:403
  20.7 14.1 %all-to-all-done.refs_2_ = f32[8,80,256]{2,1,0:T(8,128)S(1)} async-done(((f32[8,80,256]{2,1,0:T(8,128)}), f32[8,80,256]{2,1,0:T(8,128)S(1)}, u32[]{:S(2)}, u32[]{:S(2)}) %all-to-all-start) | async-done | bytes 655392 | tf_op jit(solution)/shard_map/all_to_all | solution.py:404
  34.7 0.0 copy-done
  34.7 1.0 %share_update.1 = f32[8,80,256]{2,1,0:T(8,128)} custom-call(s32[1]{0:T(128)} %bitcast.1.refs_0_, f32[8,64,256]{2,1,0:T(8,128)S(1)} %copy-done, f32[8,80,256]{2,1,0:T(8,128)S(1)} %all-to-all-done.refs_2_), custom_call_target="tpu_custom_call" | custom-call | flops 163840 | bytes 2097152 | tf_op jit(solution)/shard_map/share_update/pallas_call | solution.py:309
  35.7 6.2 %all-to-all-start.1 = ((f32[8,80,256]{2,1,0:T(8,128)}), f32[8,80,256]{2,1,0:T(8,128)S(1)}, u32[]{:S(2)}, u32[]{:S(2)}) async-start(f32[8,80,256]{2,1,0:T(8,128)} %share_update.1), calls=%async_computation.1 | async-start | bytes 1310720 | tf_op jit(solution)/shard_map/all_to_all | solution.py:406
  41.9 0.0 collective-permute-done.vi_hbm
  41.9 0.0 copy-start.2
  41.9 0.0 collective-permute-done.1.vo_hbm
  41.9 0.0 copy-start.3
  42.0 0.9 %copy-done.2 = f32[13,64,256]{2,1,0:T(8,128)} copy-done((f32[13,64,256]{2,1,0:T(8,128)}, f32[13,64,256]{2,1,0:T(8,128)S(1)}, u32[]{:S(2)}) %copy-start.2) | copy-done | bytes 851992
  42.8 0.3 copy-done.3
  43.1 5.5 %edges_added.1 = (f32[4,3,8,64,256]{4,3,2,1,0:T(8,128)}, f32[2,64,256]{2,1,0:T(8,128)}) custom-call(s32[1]{0:T(128)} %bitcast.odd_ref.refs_0_, s32[4]{0:T(128)} %cohort.3, f32[8]{0:T(128)} %gain.3, f32[4]{0:T(128)} %stiff.3, f32[8,64,256]{2,1,0:T(8,128)} %t_hbm.3, s32[8,64,256]{2,1,0:T(8,128)} %lab_hbm.3, ...), custom_call_target="tpu_custom_call", output_to_operand_aliasing={{0}: (11, {})} | custom-call | flops 1572864 | bytes 8388608 | tf_op jit(solution)/shard_map/edges_added/pallas_call | solution.py:351
  48.6 2.1 %all-to-all-done.1.refs_1_ = f32[8,80,256]{2,1,0:T(8,128)S(1)} async-done(((f32[8,80,256]{2,1,0:T(8,128)}), f32[8,80,256]{2,1,0:T(8,128)S(1)}, u32[]{:S(2)}, u32[]{:S(2)}) %all-to-all-start.1) | async-done | bytes 655392 | tf_op jit(solution)/shard_map/all_to_all | solution.py:406
  50.7 0.0 copy-start.1
  50.7 0.9 %copy-done.1 = f32[2,64,256]{2,1,0:T(8,128)S(1)} copy-done((f32[2,64,256]{2,1,0:T(8,128)S(1)}, f32[2,64,256]{2,1,0:T(8,128)}, u32[]{:S(2)}) %copy-start.1) | copy-done | bytes 131096
  51.6 0.9 %finished.1 = f32[8,64,256]{2,1,0:T(8,128)} custom-call(s32[1]{0:T(128)} %bitcast.odd_ref.refs_0_, f32[8,80,256]{2,1,0:T(8,128)S(1)} %all-to-all-done.1.refs_1_, f32[2,64,256]{2,1,0:T(8,128)S(1)} %copy-done.1), custom_call_target="tpu_custom_call" | custom-call | flops 163840 | bytes 2097152 | tf_op jit(solution)/shard_map/finished/pallas_call | solution.py:377
Async XLA Ops:
  0.6 34.1 %copy-start = (f32[8,64,256]{2,1,0:T(8,128)S(1)}, f32[8,64,256]{2,1,0:T(8,128)}, u32[]{:S(2)}) copy-start(f32[8,64,256]{2,1,0:T(8,128)} %t_hbm.3) | copy-start | bytes 1572868
  12.5 22.2 %all-to-all-start = ((f32[8,80,256]{2,1,0:T(8,128)}), f32[8,80,256]{2,1,0:T(8,128)S(1)}, u32[]{:S(2)}, u32[]{:S(2)}) async-start(f32[8,80,256]{2,1,0:T(8,128)} %get-tuple-element.8), calls=%async_computation | async-start | bytes 1310720 | tf_op jit(solution)/shard_map/all_to_all | solution.py:404
  17.6 24.3 %collective-permute-start = (f32[13,64,256]{2,1,0:T(8,128)}, f32[13,64,256]{2,1,0:T(8,128)S(1)}, u32[]{:S(2)}, u32[]{:S(2)}) collective-permute-start(f32[13,64,256]{2,1,0:T(8,128)} %get-tuple-element.9.own_in_hbm), channel_id=1, source_target_pairs={{0,1},{1,0},{2,3},{3,2},{4,5},{5,4},{6,7},{7,6},{8,9},{9,8},{10,11... | collective-permute-start | bytes 2555912 | tf_op jit(solution)/shard_map/ppermute | solution.py:402
  17.6 24.3 %collective-permute-start.1 = (f32[13,64,256]{2,1,0:T(8,128)}, f32[13,64,256]{2,1,0:T(8,128)S(1)}, u32[]{:S(2)}, u32[]{:S(2)}) collective-permute-start(f32[13,64,256]{2,1,0:T(8,128)} %get-tuple-element.10.own_far_hbm), channel_id=1, source_target_pairs={{1,2},{3,4},{5,6},{7,8},{9,10},{11,12},{13,14},{15,16},{17,18},{19... | collective-permute-start | bytes 2555912 | tf_op jit(solution)/shard_map/ppermute | solution.py:403
  35.7 15.0 %all-to-all-start.1 = ((f32[8,80,256]{2,1,0:T(8,128)}), f32[8,80,256]{2,1,0:T(8,128)S(1)}, u32[]{:S(2)}, u32[]{:S(2)}) async-start(f32[8,80,256]{2,1,0:T(8,128)} %share_update.1), calls=%async_computation.1 | async-start | bytes 1310720 | tf_op jit(solution)/shard_map/all_to_all | solution.py:406
  41.9 0.9 %copy-start.2 = (f32[13,64,256]{2,1,0:T(8,128)}, f32[13,64,256]{2,1,0:T(8,128)S(1)}, u32[]{:S(2)}) copy-start(f32[13,64,256]{2,1,0:T(8,128)S(1)} %collective-permute-done.vi_hbm) | copy-start | bytes 2555908
  41.9 1.2 %copy-start.3 = (f32[13,64,256]{2,1,0:T(8,128)}, f32[13,64,256]{2,1,0:T(8,128)S(1)}, u32[]{:S(2)}) copy-start(f32[13,64,256]{2,1,0:T(8,128)S(1)} %collective-permute-done.1.vo_hbm) | copy-start | bytes 2555908
  50.7 0.9 %copy-start.1 = (f32[2,64,256]{2,1,0:T(8,128)S(1)}, f32[2,64,256]{2,1,0:T(8,128)}, u32[]{:S(2)}) copy-start(f32[2,64,256]{2,1,0:T(8,128)} %get-tuple-element.12.refs_2_) | copy-start | bytes 393220

commit v9 on v8

--- a/solution.py
+++ b/solution.py
@@ -220,7 +220,7 @@
 
 
 def edge_kernel(
-    odd_ref, cohort, gain, stiff, t_hbm, lab_hbm, im_hbm, own_in_hbm, own_far_hbm, vi_hbm, vo_hbm, old_hbm, out_hbm, beyond_ref,
+    odd_ref, cohort, gain, stiff, t_hbm, lab_hbm, im_hbm, own_in_hbm, own_far_hbm, vi_hbm, vo_hbm, old_hbm, out_hbm,
     t_ref, lab_ref, im_ref, own_ref, halo_ref, new_ref, s_ref,
     t_sem, lab_sem, im_sem, own_sem, halo_sem, get_sem, put_sem,
 ):
@@ -261,7 +261,6 @@
         for copy in early(side, z, halo):
             copy.wait()
         sign = jnp.where(z == 0, 0.5, -0.5)
-        beyond_ref[side] = t_ref[side, 2]
         for j in range(count // ROWS):
             start = j * ROWS
             rows = pl.ds(start, ROWS)
@@ -350,12 +349,9 @@
     depth, count, width = template.shape
     return pl.pallas_call(
         edge_kernel,
-        out_shape=[
-            jax.ShapeDtypeStruct(velocity.shape, jnp.float32),
-            jax.ShapeDtypeStruct((2, count, width), jnp.float32),
-        ],
+        out_shape=jax.ShapeDtypeStruct(velocity.shape, jnp.float32),
         in_specs=[SMALL] * 4 + [FAR] * 8,
-        out_specs=[FAR, NEAR],
+        out_specs=FAR,
         scratch_shapes=[
             pltpu.VMEM((2, 3, count, width), jnp.float32),
             pltpu.VMEM((2, count, width), labels.dtype),
@@ -404,10 +400,10 @@
     parts = lax.all_to_all(part, "grp", 0, 0, tiled=True)
     shares = share_update(place, scale, template, parts)
     shares = lax.all_to_all(shares, "grp", 0, 0, tiled=True)
-    new_velocity, halo = edges_added(
+    new_velocity = edges_added(
         odd, cohort, site_gain, stiffness, template, labels, images, inner, outer, v_inner, v_outer, new_velocity
     )
-    new_template = finished(odd, scale, shares, halo, template.shape)
+    new_template = finished(odd, scale, shares, jnp.stack([v_inner[-1], v_outer[-1]]), template.shape)
     return (new_template, new_velocity)
 
 

time: 52.8 us -> 52.3 us (level)
  waiting for transfers between devices: 16.2 us -> 20.7 us
  starting transfers between devices: 14.3 us -> 10.8 us
  local copies, waits for them, and re-layouts: 2.07 us -> 1.17 us
  Pallas kernels: 19.2 us -> 18.5 us
    all_to_all x1, waiting for transfers between devices: 14.1 us -> 17.6 us  [local(): parts = lax.all_to_all(part, 'grp', 0, 0, tiled=True)]
    all_to_all x1, starting transfers between devices: 6.2 us -> 3.55 us  [local(): shares = lax.all_to_all(shares, 'grp', 0, 0, tiled=True)]
    ppermute x1, starting transfers between devices: 3.01 us -> 2.06 us  [local(): v_outer = lax.ppermute(outer, 'slab', across)]
    all_to_all x1, waiting for transfers between devices: 2.13 us -> 3.07 us  [local(): shares = lax.all_to_all(shares, 'grp', 0, 0, tiled=True)]
    unnamed x8 -> x6, local copies, waits for them, and re-layouts: 2.07 us -> 1.15 us
    pallas_call x1, Pallas kernels: 5.47 us -> 4.81 us  [edges_added(): pl.pallas_call(edge_kernel, out_shape=jax.ShapeDtypeStruct(velocity.shape...]
  transfers between devices with their start and end apart: 4 -> 4, of which waited for: 2 -> 2; matrix products, arithmetic and copies ran while one was open for 0% -> 0% of each run, Pallas kernels for 12% -> 11%
where the time goes in v9:
time: 52.3 us; the launch traced here: 52 us
  waiting for transfers between devices  20.7 us (40%)
  Pallas kernels  18.5 us (35%)
  starting transfers between devices  10.8 us (21%)
  local copies, waits for them, and re-layouts  1.17 us (2%)
  between operations  0.76 us (1%)
    all_to_all x1, waiting for transfers between devices, local(): parts = lax.all_to_all(part, 'grp', 0, 0, tiled=True)  17.6 us
    pallas_call x1, Pallas kernels, moved(): pl.pallas_call(move_kernel, out_shape=[jax.ShapeDtypeStruct((depth, share...  11.9 us
    all_to_all x1, starting transfers between devices, local(): parts = lax.all_to_all(part, 'grp', 0, 0, tiled=True)  5.12 us
    pallas_call x1, Pallas kernels, edges_added(): pl.pallas_call(edge_kernel, out_shape=jax.ShapeDtypeStruct(velocity.shape...  4.81 us
    all_to_all x1, starting transfers between devices, local(): shares = lax.all_to_all(shares, 'grp', 0, 0, tiled=True)  3.55 us
    all_to_all x1, waiting for transfers between devices, local(): shares = lax.all_to_all(shares, 'grp', 0, 0, tiled=True)  3.07 us
    ppermute x1, starting transfers between devices, local(): v_outer = lax.ppermute(outer, 'slab', across)  2.06 us
    unnamed x6, local copies, waits for them, and re-layouts  1.15 us
  transfers between devices with their start and end apart: 4, of which 2 were waited for; matrix products, arithmetic and copies ran while one was open for 0% of the time, Pallas kernels for 11%

profile of v9, /device:TPU:228, one launch (start us, length us, event | category | flops | bytes accessed | tf_op | source)
XLA Modules:
  0.0 52.0 jit_solution(6431401968684092975)
XLA Ops:
  0.6 0.0 copy-start
  0.7 11.9 %moved.1 = (f32[8,80,256]{2,1,0:T(8,128)}, f32[13,64,256]{2,1,0:T(8,128)}, f32[13,64,256]{2,1,0:T(8,128)}, f32[4,3,8,64,256]{4,3,2,1,0:T(8,128)}) custom-call(s32[1]{0:T(128)} %bitcast.odd_ref.refs_0_, s32[4]{0:T(128)} %cohort.3, f32[8]{0:T(128)} %gain.3, f32[4]{0:T(128)} %stiff.3, f32[8,64,256]{2,1,0:T(8,128)} %t_hbm.3, s32[8,64,256]{2,1,0:T(8,128)} %lab_hbm.3, ...), custom_call_target="tpu_custom_call" | custom-call | flops 12582912 | bytes 16777216 | tf_op jit(solution)/shard_map/moved/pallas_call | solution.py:325
  12.5 5.1 %all-to-all-start = ((f32[8,80,256]{2,1,0:T(8,128)}), f32[8,80,256]{2,1,0:T(8,128)S(1)}, u32[]{:S(2)}, u32[]{:S(2)}) async-start(f32[8,80,256]{2,1,0:T(8,128)} %get-tuple-element.6), calls=%async_computation | async-start | bytes 1310720 | tf_op jit(solution)/shard_map/all_to_all | solution.py:400
  17.7 2.1 %collective-permute-start.1 = (f32[13,64,256]{2,1,0:T(8,128)}, f32[13,64,256]{2,1,0:T(8,128)S(1)}, u32[]{:S(2)}, u32[]{:S(2)}) collective-permute-start(f32[13,64,256]{2,1,0:T(8,128)} %get-tuple-element.8.own_far_hbm), channel_id=1, source_target_pairs={{1,2},{3,4},{5,6},{7,8},{9,10},{11,12},{13,14},{15,16},{17,18},{19... | collective-permute-start | bytes 2555912 | tf_op jit(solution)/shard_map/ppermute | solution.py:399
  19.7 0.1 collective-permute-start
  19.8 17.6 %all-to-all-done.refs_2_ = f32[8,80,256]{2,1,0:T(8,128)S(1)} async-done(((f32[8,80,256]{2,1,0:T(8,128)}), f32[8,80,256]{2,1,0:T(8,128)S(1)}, u32[]{:S(2)}, u32[]{:S(2)}) %all-to-all-start) | async-done | bytes 655392 | tf_op jit(solution)/shard_map/all_to_all | solution.py:400
  37.4 0.0 copy-done
  37.4 1.0 %share_update.1 = f32[8,80,256]{2,1,0:T(8,128)} custom-call(s32[1]{0:T(128)} %bitcast.1.refs_0_, f32[8,64,256]{2,1,0:T(8,128)S(1)} %copy-done, f32[8,80,256]{2,1,0:T(8,128)S(1)} %all-to-all-done.refs_2_), custom_call_target="tpu_custom_call" | custom-call | flops 163840 | bytes 2097152 | tf_op jit(solution)/shard_map/share_update/pallas_call | solution.py:308
  38.4 3.6 %all-to-all-start.1 = ((f32[8,80,256]{2,1,0:T(8,128)}), f32[8,80,256]{2,1,0:T(8,128)S(1)}, u32[]{:S(2)}, u32[]{:S(2)}) async-start(f32[8,80,256]{2,1,0:T(8,128)} %share_update.1), calls=%async_computation.1 | async-start | bytes 1310720 | tf_op jit(solution)/shard_map/all_to_all | solution.py:402
  42.0 0.0 collective-permute-done.1.vo_hbm
  42.0 0.0 copy-start.1
  42.0 0.0 collective-permute-done.vi_hbm
  42.0 0.0 copy-start.2
  42.0 0.9 %copy-done.1 = f32[13,64,256]{2,1,0:T(8,128)} copy-done((f32[13,64,256]{2,1,0:T(8,128)}, f32[13,64,256]{2,1,0:T(8,128)S(1)}, u32[]{:S(2)}) %copy-start.1) | copy-done | bytes 851992
  42.9 0.3 copy-done.2
  43.2 4.8 %edges_added.1 = f32[4,3,8,64,256]{4,3,2,1,0:T(8,128)} custom-call(s32[1]{0:T(128)} %bitcast.odd_ref.refs_0_, s32[4]{0:T(128)} %cohort.3, f32[8]{0:T(128)} %gain.3, f32[4]{0:T(128)} %stiff.3, f32[8,64,256]{2,1,0:T(8,128)} %t_hbm.3, s32[8,64,256]{2,1,0:T(8,128)} %lab_hbm.3, bf16[4,8,64,256]{3,2,1,0:T(8,128)(2,1)} %im_hbm.3, ...), custom_call_target="tpu_custom_call", output_to_operand_aliasing={{}: (11, {})} | custom-call | flops 1572864 | bytes 8388608 | tf_op jit(solution)/shard_map/edges_added/pallas_call | solution.py:350
  48.0 3.1 %all-to-all-done.1.refs_1_ = f32[8,80,256]{2,1,0:T(8,128)S(1)} async-done(((f32[8,80,256]{2,1,0:T(8,128)}), f32[8,80,256]{2,1,0:T(8,128)S(1)}, u32[]{:S(2)}, u32[]{:S(2)}) %all-to-all-start.1) | async-done | bytes 655392 | tf_op jit(solution)/shard_map/all_to_all | solution.py:402
  51.1 0.9 %finished.1 = f32[8,64,256]{2,1,0:T(8,128)} custom-call(s32[1]{0:T(128)} %bitcast.odd_ref.refs_0_, f32[8,80,256]{2,1,0:T(8,128)S(1)} %all-to-all-done.1.refs_1_, f32[2,64,256]{2,1,0:T(8,128)S(1)} %pad_maximum_fusion.refs_2_), custom_call_target="tpu_custom_call" | custom-call | flops 163840 | bytes 2097152 | tf_op jit(solution)/shard_map/finished/pallas_call | solution.py:373
  (3 shorter events, 0.0 us)
Async XLA Ops:
  0.6 36.8 %copy-start = (f32[8,64,256]{2,1,0:T(8,128)S(1)}, f32[8,64,256]{2,1,0:T(8,128)}, u32[]{:S(2)}) copy-start(f32[8,64,256]{2,1,0:T(8,128)} %t_hbm.3) | copy-start | bytes 1572868
  12.5 24.9 %all-to-all-start = ((f32[8,80,256]{2,1,0:T(8,128)}), f32[8,80,256]{2,1,0:T(8,128)S(1)}, u32[]{:S(2)}, u32[]{:S(2)}) async-start(f32[8,80,256]{2,1,0:T(8,128)} %get-tuple-element.6), calls=%async_computation | async-start | bytes 1310720 | tf_op jit(solution)/shard_map/all_to_all | solution.py:400
  17.7 24.3 %collective-permute-start.1 = (f32[13,64,256]{2,1,0:T(8,128)}, f32[13,64,256]{2,1,0:T(8,128)S(1)}, u32[]{:S(2)}, u32[]{:S(2)}) collective-permute-start(f32[13,64,256]{2,1,0:T(8,128)} %get-tuple-element.8.own_far_hbm), channel_id=1, source_target_pairs={{1,2},{3,4},{5,6},{7,8},{9,10},{11,12},{13,14},{15,16},{17,18},{19... | collective-permute-start | bytes 2555912 | tf_op jit(solution)/shard_map/ppermute | solution.py:399
  19.7 22.3 %collective-permute-start = (f32[13,64,256]{2,1,0:T(8,128)}, f32[13,64,256]{2,1,0:T(8,128)S(1)}, u32[]{:S(2)}, u32[]{:S(2)}) collective-permute-start(f32[13,64,256]{2,1,0:T(8,128)} %get-tuple-element.7.own_in_hbm), channel_id=1, source_target_pairs={{0,1},{1,0},{2,3},{3,2},{4,5},{5,4},{6,7},{7,6},{8,9},{9,8},{10,11... | collective-permute-start | bytes 2555912 | tf_op jit(solution)/shard_map/ppermute | solution.py:398
  38.4 12.7 %all-to-all-start.1 = ((f32[8,80,256]{2,1,0:T(8,128)}), f32[8,80,256]{2,1,0:T(8,128)S(1)}, u32[]{:S(2)}, u32[]{:S(2)}) async-start(f32[8,80,256]{2,1,0:T(8,128)} %share_update.1), calls=%async_computation.1 | async-start | bytes 1310720 | tf_op jit(solution)/shard_map/all_to_all | solution.py:402
  42.0 0.9 %copy-start.1 = (f32[13,64,256]{2,1,0:T(8,128)}, f32[13,64,256]{2,1,0:T(8,128)S(1)}, u32[]{:S(2)}) copy-start(f32[13,64,256]{2,1,0:T(8,128)S(1)} %collective-permute-done.1.vo_hbm) | copy-start | bytes 2555908
  42.0 1.2 %copy-start.2 = (f32[13,64,256]{2,1,0:T(8,128)}, f32[13,64,256]{2,1,0:T(8,128)S(1)}, u32[]{:S(2)}) copy-start(f32[13,64,256]{2,1,0:T(8,128)S(1)} %collective-permute-done.vi_hbm) | copy-start | bytes 2555908
